TPU v7x, 256 devices: a whole 4x4x8 slice. The times are simulated.
256 devices in a mesh: gx: 32 (over y, z), gy: 8 (over x, core).
Axes of the slice: x: 4, y: 4, z: 8, core: 2. Of those that a mesh axis runs over, the one named last changes fastest.
Arguments:
- operators: float32 [32, 8, 1536, 1536], P('gx', 'gy'), may hold values from -0.15625 to 0.15625
- sources: float32 [32, 8, 5, 64, 128], P('gx', 'gy'), may hold values from -6 to 6
- source_rows: int32 [32, 8, 128], P('gx', 'gy'), may hold values from 0 to 1535
- batch_plan: int32 [5], replicated, may hold values from 0 to 4, each once
Outputs:
- traces: float32 [32, 8, 4, 64, 1536], P('gx', 'gy')
- basis: float32 [32, 8, 64, 1536], P('gx', 'gy')
- factor: float32 [64, 64], replicated
Inputs may be any that keep to these rules, and one draw needn't show every extreme that they name: `batch_plan`: a permutation of the 5 source blocks.
All inputs are finite; a program needn't handle non-finite values.
Results may differ from a plain program's by a relative error of at most 0.0003.
Values sent between devices are 32-bit elements; how exact they have to be, the bound alone decides.
No kernel may reach another device: no remote copies, remote signals or barrier semaphores. Data moves between devices by JAX's collectives and lax.ppermute only.
A program may use at most 64 MiB of HBM per device.

v0:
```python
import jax
import jax.numpy as jnp
from jax import lax
from jax.sharding import PartitionSpec as P


def passed_along(block, axis, distance):
    devices = range(lax.axis_size(axis))
    route = [(i - distance, i) for i in devices if i - distance in devices]
    return lax.ppermute(block, axis, route)


def over_pieces(value, axis):
    return lax.all_gather(value, axis).sum(0)


def body(operators, sources, source_rows, batch_plan):
    col_index = lax.axis_index("gx")
    row_index = lax.axis_index("gy")
    depth = lax.axis_size("gx") + lax.axis_size("gy") - 1
    trace_map = operators[0, 0]
    order = trace_map.shape[0]
    half = order // 2
    ordered = jnp.take(sources[0, 0], batch_plan, axis=0)
    batches, columns, placed_count = ordered.shape
    pieces = 2
    width = columns // pieces
    count = batches * pieces
    blocks = ordered.reshape(count, width, placed_count)
    placing = (source_rows[0, 0][:, None] == jnp.arange(order, dtype=jnp.int32)[None, :]).astype(
        jnp.float32
    )

    def advance(step, carry):
        west_in, south_in, results = carry
        target = step - col_index - row_index
        active = (target >= 0) & (target < count)
        picked = jnp.clip(target, 0, count - 1)

        def compute():
            joined = jnp.concatenate([west_in, south_in], axis=1)
            source = lax.dynamic_index_in_dim(blocks, picked, 0, keepdims=False)
            outgoing = jnp.dot(
                joined,
                trace_map,
                precision=lax.Precision.HIGHEST,
                preferred_element_type=jnp.float32,
            )
            return outgoing + jnp.dot(
                source, placing, precision=lax.Precision.HIGHEST, preferred_element_type=jnp.float32
            )

        def resting():
            return jnp.zeros((width, order), jnp.float32)

        outgoing = lax.cond(active, compute, resting)
        kept = lax.dynamic_index_in_dim(results, picked, 0, keepdims=False)
        results = lax.dynamic_update_index_in_dim(
            results, jnp.where(active, outgoing, kept), picked, 0
        )
        west_next = passed_along(outgoing[:, :half], "gx", 1)
        south_next = passed_along(outgoing[:, half:], "gy", 1)
        return (west_next, south_next, results)

    total = depth + count - 1
    start = (
        jnp.zeros((width, half), jnp.float32),
        jnp.zeros((width, half), jnp.float32),
        jnp.zeros((count, width, order), jnp.float32),
    )
    split_step = depth + pieces - 1
    carry = lax.fori_loop(0, split_step, advance, start)
    first = carry[2][:pieces].reshape(columns, order)
    partial_gram = lax.dot_general(
        first,
        first,
        (((1,), (1,)), ((), ())),
        precision=lax.Precision.HIGHEST,
        preferred_element_type=jnp.float32,
    )
    gram = over_pieces(partial_gram, ("gx", "gy")) / (
        lax.axis_size("gx") * lax.axis_size("gy") * order
    )
    lower = jnp.linalg.cholesky(gram)
    basis = jax.scipy.linalg.solve_triangular(lower, first, lower=True)
    basis, factor = (basis, lower.T)
    carry = lax.fori_loop(split_step, total, advance, carry)
    results = carry[2].reshape(batches, columns, order)
    return (results[1:][None, None], basis[None, None], factor)


def solution(mesh):
    return jax.shard_map(
        body,
        mesh=mesh,
        in_specs=(
            P("gx", "gy", None, None),
            P("gx", "gy", None, None, None),
            P("gx", "gy", None),
            P(),
        ),
        out_specs=(P("gx", "gy", None, None, None), P("gx", "gy", None, None), P()),
        check_vma=False,
    )
```

profile of v0, /device:TPU:1, one launch (start us, length us, event | category | flops | bytes accessed | tf_op | source)
XLA Modules:
  0.0 784.9 jit_solution(11771474775425710388)
XLA Ops:
  10.3 555.0 %while.36 = (s32[]{:T(128)}, f32[32,768]{1,0:T(8,128)S(1)}, f32[32,768]{1,0:T(8,128)S(1)}, f32[10,32,1536]{2,1,0:T(8,128)S(1)}, s32[]{:T(128)}, /*index=5*/s32[]...) while((s32[]{:T(128)}, f32[32,768]{1,0:T(8,128)S(1)}, ...), condition=%wide.region_3.4_spmd.clone, body=%wide.region_0.3_spmd.clone.sunk | while | flops 982007808 | bytes 13976446 | solution.py:72
  26.4 9.1 %conditional.6 = (f32[32,1536]{1,0:T(8,128)S(1)}) conditional(s32[]{:T(128)} %convert_element_type.35, () %tuple.89, (f32[32,768]{1,0:T(8,128)S(1)}, f32[32,768]{1,0:T(8,128)S(1)}, f32[1536,1536]{1,0:T(8,128)}, s32[]{:T(128)}, f32[10,32,128]{2,1,0:T(8,128)}, /*index=5*/f32[128,1536]{1,0:T(8,128)S(1)}) %tuple.90), branch_computations={%region_1.1_spmd, %region_2.2_spmd} | conditional | flops 981565440 | bytes 11026478 | solution.py:56
  26.4 7.9 %fusion.4 = f32[32,1536]{1,0:T(8,128)S(1)} fusion(f32[1536,1536]{1,0:T(8,128)} %get-tuple-element.326, f32[32,768]{1,0:T(8,128)S(1)} %get-tuple-element.325, f32[32,768]{1,0:T(8,128)S(1)} %get-tuple-element.324), kind=kOutput, calls=%fused_computation.4 | convolution fusion | flops 906018816 | bytes 9830400 | tf_op jit(solution)/shard_map/while/body/eval_jaxpr/cond/branch_1_fun/dot_general | solution.py:43
  42.2 9.1 %conditional.6 = (f32[32,1536]{1,0:T(8,128)S(1)}) conditional(s32[]{:T(128)} %convert_element_type.35, () %tuple.89, (f32[32,768]{1,0:T(8,128)S(1)}, f32[32,768]{1,0:T(8,128)S(1)}, f32[1536,1536]{1,0:T(8,128)}, s32[]{:T(128)}, f32[10,32,128]{2,1,0:T(8,128)}, /*index=5*/f32[128,1536]{1,0:T(8,128)S(1)}) %tuple.90), branch_computations={%region_1.1_spmd, %region_2.2_spmd} | conditional | flops 981565440 | bytes 11026478 | solution.py:56
  42.2 7.9 %fusion.4 = f32[32,1536]{1,0:T(8,128)S(1)} fusion(f32[1536,1536]{1,0:T(8,128)} %get-tuple-element.326, f32[32,768]{1,0:T(8,128)S(1)} %get-tuple-element.325, f32[32,768]{1,0:T(8,128)S(1)} %get-tuple-element.324), kind=kOutput, calls=%fused_computation.4 | convolution fusion | flops 906018816 | bytes 9830400 | tf_op jit(solution)/shard_map/while/body/eval_jaxpr/cond/branch_1_fun/dot_general | solution.py:43
  58.0 9.1 %conditional.6 = (f32[32,1536]{1,0:T(8,128)S(1)}) conditional(s32[]{:T(128)} %convert_element_type.35, () %tuple.89, (f32[32,768]{1,0:T(8,128)S(1)}, f32[32,768]{1,0:T(8,128)S(1)}, f32[1536,1536]{1,0:T(8,128)}, s32[]{:T(128)}, f32[10,32,128]{2,1,0:T(8,128)}, /*index=5*/f32[128,1536]{1,0:T(8,128)S(1)}) %tuple.90), branch_computations={%region_1.1_spmd, %region_2.2_spmd} | conditional | flops 981565440 | bytes 11026478 | solution.py:56
  74.2 9.1 %conditional.6 = (f32[32,1536]{1,0:T(8,128)S(1)}) conditional(s32[]{:T(128)} %convert_element_type.35, () %tuple.89, (f32[32,768]{1,0:T(8,128)S(1)}, f32[32,768]{1,0:T(8,128)S(1)}, f32[1536,1536]{1,0:T(8,128)}, s32[]{:T(128)}, f32[10,32,128]{2,1,0:T(8,128)}, /*index=5*/f32[128,1536]{1,0:T(8,128)S(1)}) %tuple.90), branch_computations={%region_1.1_spmd, %region_2.2_spmd} | conditional | flops 981565440 | bytes 11026478 | solution.py:56
  74.2 7.9 %fusion.4 = f32[32,1536]{1,0:T(8,128)S(1)} fusion(f32[1536,1536]{1,0:T(8,128)} %get-tuple-element.326, f32[32,768]{1,0:T(8,128)S(1)} %get-tuple-element.325, f32[32,768]{1,0:T(8,128)S(1)} %get-tuple-element.324), kind=kOutput, calls=%fused_computation.4 | convolution fusion | flops 906018816 | bytes 9830400 | tf_op jit(solution)/shard_map/while/body/eval_jaxpr/cond/branch_1_fun/dot_general | solution.py:43
  91.3 9.1 %conditional.6 = (f32[32,1536]{1,0:T(8,128)S(1)}) conditional(s32[]{:T(128)} %convert_element_type.35, () %tuple.89, (f32[32,768]{1,0:T(8,128)S(1)}, f32[32,768]{1,0:T(8,128)S(1)}, f32[1536,1536]{1,0:T(8,128)}, s32[]{:T(128)}, f32[10,32,128]{2,1,0:T(8,128)}, /*index=5*/f32[128,1536]{1,0:T(8,128)S(1)}) %tuple.90), branch_computations={%region_1.1_spmd, %region_2.2_spmd} | conditional | flops 981565440 | bytes 11026478 | solution.py:56
  91.3 7.9 %fusion.4 = f32[32,1536]{1,0:T(8,128)S(1)} fusion(f32[1536,1536]{1,0:T(8,128)} %get-tuple-element.326, f32[32,768]{1,0:T(8,128)S(1)} %get-tuple-element.325, f32[32,768]{1,0:T(8,128)S(1)} %get-tuple-element.324), kind=kOutput, calls=%fused_computation.4 | convolution fusion | flops 906018816 | bytes 9830400 | tf_op jit(solution)/shard_map/while/body/eval_jaxpr/cond/branch_1_fun/dot_general | solution.py:43
  108.5 9.1 %conditional.6 = (f32[32,1536]{1,0:T(8,128)S(1)}) conditional(s32[]{:T(128)} %convert_element_type.35, () %tuple.89, (f32[32,768]{1,0:T(8,128)S(1)}, f32[32,768]{1,0:T(8,128)S(1)}, f32[1536,1536]{1,0:T(8,128)}, s32[]{:T(128)}, f32[10,32,128]{2,1,0:T(8,128)}, /*index=5*/f32[128,1536]{1,0:T(8,128)S(1)}) %tuple.90), branch_computations={%region_1.1_spmd, %region_2.2_spmd} | conditional | flops 981565440 | bytes 11026478 | solution.py:56
  108.5 7.9 %fusion.4 = f32[32,1536]{1,0:T(8,128)S(1)} fusion(f32[1536,1536]{1,0:T(8,128)} %get-tuple-element.326, f32[32,768]{1,0:T(8,128)S(1)} %get-tuple-element.325, f32[32,768]{1,0:T(8,128)S(1)} %get-tuple-element.324), kind=kOutput, calls=%fused_computation.4 | convolution fusion | flops 906018816 | bytes 9830400 | tf_op jit(solution)/shard_map/while/body/eval_jaxpr/cond/branch_1_fun/dot_general | solution.py:43
  125.7 9.1 %conditional.6 = (f32[32,1536]{1,0:T(8,128)S(1)}) conditional(s32[]{:T(128)} %convert_element_type.35, () %tuple.89, (f32[32,768]{1,0:T(8,128)S(1)}, f32[32,768]{1,0:T(8,128)S(1)}, f32[1536,1536]{1,0:T(8,128)}, s32[]{:T(128)}, f32[10,32,128]{2,1,0:T(8,128)}, /*index=5*/f32[128,1536]{1,0:T(8,128)S(1)}) %tuple.90), branch_computations={%region_1.1_spmd, %region_2.2_spmd} | conditional | flops 981565440 | bytes 11026478 | solution.py:56
  125.7 7.9 %fusion.4 = f32[32,1536]{1,0:T(8,128)S(1)} fusion(f32[1536,1536]{1,0:T(8,128)} %get-tuple-element.326, f32[32,768]{1,0:T(8,128)S(1)} %get-tuple-element.325, f32[32,768]{1,0:T(8,128)S(1)} %get-tuple-element.324), kind=kOutput, calls=%fused_computation.4 | convolution fusion | flops 906018816 | bytes 9830400 | tf_op jit(solution)/shard_map/while/body/eval_jaxpr/cond/branch_1_fun/dot_general | solution.py:43
  142.8 9.1 %conditional.6 = (f32[32,1536]{1,0:T(8,128)S(1)}) conditional(s32[]{:T(128)} %convert_element_type.35, () %tuple.89, (f32[32,768]{1,0:T(8,128)S(1)}, f32[32,768]{1,0:T(8,128)S(1)}, f32[1536,1536]{1,0:T(8,128)}, s32[]{:T(128)}, f32[10,32,128]{2,1,0:T(8,128)}, /*index=5*/f32[128,1536]{1,0:T(8,128)S(1)}) %tuple.90), branch_computations={%region_1.1_spmd, %region_2.2_spmd} | conditional | flops 981565440 | bytes 11026478 | solution.py:56
  142.8 7.9 %fusion.4 = f32[32,1536]{1,0:T(8,128)S(1)} fusion(f32[1536,1536]{1,0:T(8,128)} %get-tuple-element.326, f32[32,768]{1,0:T(8,128)S(1)} %get-tuple-element.325, f32[32,768]{1,0:T(8,128)S(1)} %get-tuple-element.324), kind=kOutput, calls=%fused_computation.4 | convolution fusion | flops 906018816 | bytes 9830400 | tf_op jit(solution)/shard_map/while/body/eval_jaxpr/cond/branch_1_fun/dot_general | solution.py:43
  160.0 9.1 %conditional.6 = (f32[32,1536]{1,0:T(8,128)S(1)}) conditional(s32[]{:T(128)} %convert_element_type.35, () %tuple.89, (f32[32,768]{1,0:T(8,128)S(1)}, f32[32,768]{1,0:T(8,128)S(1)}, f32[1536,1536]{1,0:T(8,128)}, s32[]{:T(128)}, f32[10,32,128]{2,1,0:T(8,128)}, /*index=5*/f32[128,1536]{1,0:T(8,128)S(1)}) %tuple.90), branch_computations={%region_1.1_spmd, %region_2.2_spmd} | conditional | flops 981565440 | bytes 11026478 | solution.py:56
  160.0 7.9 %fusion.4 = f32[32,1536]{1,0:T(8,128)S(1)} fusion(f32[1536,1536]{1,0:T(8,128)} %get-tuple-element.326, f32[32,768]{1,0:T(8,128)S(1)} %get-tuple-element.325, f32[32,768]{1,0:T(8,128)S(1)} %get-tuple-element.324), kind=kOutput, calls=%fused_computation.4 | convolution fusion | flops 906018816 | bytes 9830400 | tf_op jit(solution)/shard_map/while/body/eval_jaxpr/cond/branch_1_fun/dot_general | solution.py:43
  177.1 9.1 %conditional.6 = (f32[32,1536]{1,0:T(8,128)S(1)}) conditional(s32[]{:T(128)} %convert_element_type.35, () %tuple.89, (f32[32,768]{1,0:T(8,128)S(1)}, f32[32,768]{1,0:T(8,128)S(1)}, f32[1536,1536]{1,0:T(8,128)}, s32[]{:T(128)}, f32[10,32,128]{2,1,0:T(8,128)}, /*index=5*/f32[128,1536]{1,0:T(8,128)S(1)}) %tuple.90), branch_computations={%region_1.1_spmd, %region_2.2_spmd} | conditional | flops 981565440 | bytes 11026478 | solution.py:56
  177.2 7.9 %fusion.4 = f32[32,1536]{1,0:T(8,128)S(1)} fusion(f32[1536,1536]{1,0:T(8,128)} %get-tuple-element.326, f32[32,768]{1,0:T(8,128)S(1)} %get-tuple-element.325, f32[32,768]{1,0:T(8,128)S(1)} %get-tuple-element.324), kind=kOutput, calls=%fused_computation.4 | convolution fusion | flops 906018816 | bytes 9830400 | tf_op jit(solution)/shard_map/while/body/eval_jaxpr/cond/branch_1_fun/dot_general | solution.py:43
  194.4 10.7 %collective-permute-start = (f32[32,768]{1,0:T(8,128)S(1)}, f32[32,768]{1,0:T(8,128)S(1)}, u32[]{:S(2)}, u32[]{:S(2)}) collective-permute-start(f32[32,768]{1,0:T(8,128)S(1)} %get-tuple-element.565), channel_id=1, source_target_pairs={{0,8},{8,16},{16,24},{24,32},{32,40},{40,48},{48,56},{56,64},{64,7... | collective-permute-start | bytes 294920 | tf_op jit(solution)/shard_map/while/body/eval_jaxpr/ppermute | solution.py:10
  213.2 13.7 %collective-permute-start.1 = (f32[32,768]{1,0:T(8,128)S(1)}, f32[32,768]{1,0:T(8,128)S(1)}, u32[]{:S(2)}, u32[]{:S(2)}) collective-permute-start(f32[32,768]{1,0:T(8,128)S(1)} %get-tuple-element.566), channel_id=1, source_target_pairs={{0,1},{1,2},{2,3},{3,4},{4,5},{5,6},{6,7},{8,9},{9,10},{10,11},{11... | collective-permute-start | bytes 294920 | tf_op jit(solution)/shard_map/while/body/eval_jaxpr/ppermute | solution.py:10
  236.8 9.4 %collective-permute-start = (f32[32,768]{1,0:T(8,128)S(1)}, f32[32,768]{1,0:T(8,128)S(1)}, u32[]{:S(2)}, u32[]{:S(2)}) collective-permute-start(f32[32,768]{1,0:T(8,128)S(1)} %get-tuple-element.565), channel_id=1, source_target_pairs={{0,8},{8,16},{16,24},{24,32},{32,40},{40,48},{48,56},{56,64},{64,7... | collective-permute-start | bytes 294920 | tf_op jit(solution)/shard_map/while/body/eval_jaxpr/ppermute | solution.py:10
  312.6 8.4 %collective-permute-start = (f32[32,768]{1,0:T(8,128)S(1)}, f32[32,768]{1,0:T(8,128)S(1)}, u32[]{:S(2)}, u32[]{:S(2)}) collective-permute-start(f32[32,768]{1,0:T(8,128)S(1)} %get-tuple-element.565), channel_id=1, source_target_pairs={{0,8},{8,16},{16,24},{24,32},{32,40},{40,48},{48,56},{56,64},{64,7... | collective-permute-start | bytes 294920 | tf_op jit(solution)/shard_map/while/body/eval_jaxpr/ppermute | solution.py:10
  338.8 8.5 %collective-permute-start = (f32[32,768]{1,0:T(8,128)S(1)}, f32[32,768]{1,0:T(8,128)S(1)}, u32[]{:S(2)}, u32[]{:S(2)}) collective-permute-start(f32[32,768]{1,0:T(8,128)S(1)} %get-tuple-element.565), channel_id=1, source_target_pairs={{0,8},{8,16},{16,24},{24,32},{32,40},{40,48},{48,56},{56,64},{64,7... | collective-permute-start | bytes 294920 | tf_op jit(solution)/shard_map/while/body/eval_jaxpr/ppermute | solution.py:10
  365.1 8.5 %collective-permute-start = (f32[32,768]{1,0:T(8,128)S(1)}, f32[32,768]{1,0:T(8,128)S(1)}, u32[]{:S(2)}, u32[]{:S(2)}) collective-permute-start(f32[32,768]{1,0:T(8,128)S(1)} %get-tuple-element.565), channel_id=1, source_target_pairs={{0,8},{8,16},{16,24},{24,32},{32,40},{40,48},{48,56},{56,64},{64,7... | collective-permute-start | bytes 294920 | tf_op jit(solution)/shard_map/while/body/eval_jaxpr/ppermute | solution.py:10
  391.1 8.5 %collective-permute-start = (f32[32,768]{1,0:T(8,128)S(1)}, f32[32,768]{1,0:T(8,128)S(1)}, u32[]{:S(2)}, u32[]{:S(2)}) collective-permute-start(f32[32,768]{1,0:T(8,128)S(1)} %get-tuple-element.565), channel_id=1, source_target_pairs={{0,8},{8,16},{16,24},{24,32},{32,40},{40,48},{48,56},{56,64},{64,7... | collective-permute-start | bytes 294920 | tf_op jit(solution)/shard_map/while/body/eval_jaxpr/ppermute | solution.py:10
  417.1 8.4 %collective-permute-start = (f32[32,768]{1,0:T(8,128)S(1)}, f32[32,768]{1,0:T(8,128)S(1)}, u32[]{:S(2)}, u32[]{:S(2)}) collective-permute-start(f32[32,768]{1,0:T(8,128)S(1)} %get-tuple-element.565), channel_id=1, source_target_pairs={{0,8},{8,16},{16,24},{24,32},{32,40},{40,48},{48,56},{56,64},{64,7... | collective-permute-start | bytes 294920 | tf_op jit(solution)/shard_map/while/body/eval_jaxpr/ppermute | solution.py:10
  442.9 8.4 %collective-permute-start = (f32[32,768]{1,0:T(8,128)S(1)}, f32[32,768]{1,0:T(8,128)S(1)}, u32[]{:S(2)}, u32[]{:S(2)}) collective-permute-start(f32[32,768]{1,0:T(8,128)S(1)} %get-tuple-element.565), channel_id=1, source_target_pairs={{0,8},{8,16},{16,24},{24,32},{32,40},{40,48},{48,56},{56,64},{64,7... | collective-permute-start | bytes 294920 | tf_op jit(solution)/shard_map/while/body/eval_jaxpr/ppermute | solution.py:10
  567.2 97.7 %while.37 = (s32[]{:T(128)}, f32[32,768]{1,0:T(8,128)S(1)}, f32[32,768]{1,0:T(8,128)S(1)}, f32[10,32,1536]{2,1,0:T(8,128)S(1)}, s32[]{:T(128)}, /*index=5*/s32[]...) while((s32[]{:T(128)}, f32[32,768]{1,0:T(8,128)S(1)}, ...), condition=%wide.region_7.8_spmd.clone, body=%wide.region_4.7_spmd.clone.sunk | while | flops 982007808 | bytes 13976466 | solution.py:87
  639.2 8.4 %collective-permute-start.2 = (f32[32,768]{1,0:T(8,128)S(1)}, f32[32,768]{1,0:T(8,128)S(1)}, u32[]{:S(2)}, u32[]{:S(2)}) collective-permute-start(f32[32,768]{1,0:T(8,128)S(1)} %get-tuple-element.576), channel_id=1, source_target_pairs={{0,8},{8,16},{16,24},{24,32},{32,40},{40,48},{48,56},{56,64},{64,7... | collective-permute-start | bytes 294920 | tf_op jit(solution)/shard_map/while/body/eval_jaxpr/ppermute | solution.py:10
  666.1 93.6 %all-gather.3.cloned.1.call-done = f32[16384,64]{1,0:T(8,128)} async-done(((f32[64,64]{1,0:T(8,128)}), f32[16384,64]{1,0:T(8,128)}) %all-gather.3.cloned.1.call-update) | async-done | bytes 4194320 | tf_op jit(solution)/shard_map/all_gather | solution.py:14
  (496 shorter events, 510.7 us)
Async XLA Ops:
  7.2 752.6 %all-gather.3.cloned.1.call-start = ((), (), s32[]{:S(2)}) async-start(), calls=%async_computation | async-start | bytes 8421376 | tf_op jit(solution)/shard_map/all_gather | solution.py:14
  14.9 11.3 %collective-permute-start.1 = (f32[32,768]{1,0:T(8,128)S(1)}, f32[32,768]{1,0:T(8,128)S(1)}, u32[]{:S(2)}, u32[]{:S(2)}) collective-permute-start(f32[32,768]{1,0:T(8,128)S(1)} %get-tuple-element.566), channel_id=1, source_target_pairs={{0,1},{1,2},{2,3},{3,4},{4,5},{5,6},{6,7},{8,9},{9,10},{10,11},{11... | collective-permute-start | bytes 294920 | tf_op jit(solution)/shard_map/while/body/eval_jaxpr/ppermute | solution.py:10
  194.4 15.4 %collective-permute-start = (f32[32,768]{1,0:T(8,128)S(1)}, f32[32,768]{1,0:T(8,128)S(1)}, u32[]{:S(2)}, u32[]{:S(2)}) collective-permute-start(f32[32,768]{1,0:T(8,128)S(1)} %get-tuple-element.565), channel_id=1, source_target_pairs={{0,8},{8,16},{16,24},{24,32},{32,40},{40,48},{48,56},{56,64},{64,7... | collective-permute-start | bytes 294920 | tf_op jit(solution)/shard_map/while/body/eval_jaxpr/ppermute | solution.py:10
  211.5 15.4 %collective-permute-start = (f32[32,768]{1,0:T(8,128)S(1)}, f32[32,768]{1,0:T(8,128)S(1)}, u32[]{:S(2)}, u32[]{:S(2)}) collective-permute-start(f32[32,768]{1,0:T(8,128)S(1)} %get-tuple-element.565), channel_id=1, source_target_pairs={{0,8},{8,16},{16,24},{24,32},{32,40},{40,48},{48,56},{56,64},{64,7... | collective-permute-start | bytes 294920 | tf_op jit(solution)/shard_map/while/body/eval_jaxpr/ppermute | solution.py:10
  213.2 15.3 %collective-permute-start.1 = (f32[32,768]{1,0:T(8,128)S(1)}, f32[32,768]{1,0:T(8,128)S(1)}, u32[]{:S(2)}, u32[]{:S(2)}) collective-permute-start(f32[32,768]{1,0:T(8,128)S(1)} %get-tuple-element.566), channel_id=1, source_target_pairs={{0,1},{1,2},{2,3},{3,4},{4,5},{5,6},{6,7},{8,9},{9,10},{10,11},{11... | collective-permute-start | bytes 294920 | tf_op jit(solution)/shard_map/while/body/eval_jaxpr/ppermute | solution.py:10
  236.8 14.1 %collective-permute-start = (f32[32,768]{1,0:T(8,128)S(1)}, f32[32,768]{1,0:T(8,128)S(1)}, u32[]{:S(2)}, u32[]{:S(2)}) collective-permute-start(f32[32,768]{1,0:T(8,128)S(1)} %get-tuple-element.565), channel_id=1, source_target_pairs={{0,8},{8,16},{16,24},{24,32},{32,40},{40,48},{48,56},{56,64},{64,7... | collective-permute-start | bytes 294920 | tf_op jit(solution)/shard_map/while/body/eval_jaxpr/ppermute | solution.py:10
  263.6 11.1 %collective-permute-start = (f32[32,768]{1,0:T(8,128)S(1)}, f32[32,768]{1,0:T(8,128)S(1)}, u32[]{:S(2)}, u32[]{:S(2)}) collective-permute-start(f32[32,768]{1,0:T(8,128)S(1)} %get-tuple-element.565), channel_id=1, source_target_pairs={{0,8},{8,16},{16,24},{24,32},{32,40},{40,48},{48,56},{56,64},{64,7... | collective-permute-start | bytes 294920 | tf_op jit(solution)/shard_map/while/body/eval_jaxpr/ppermute | solution.py:10
  287.5 13.0 %collective-permute-start = (f32[32,768]{1,0:T(8,128)S(1)}, f32[32,768]{1,0:T(8,128)S(1)}, u32[]{:S(2)}, u32[]{:S(2)}) collective-permute-start(f32[32,768]{1,0:T(8,128)S(1)} %get-tuple-element.565), channel_id=1, source_target_pairs={{0,8},{8,16},{16,24},{24,32},{32,40},{40,48},{48,56},{56,64},{64,7... | collective-permute-start | bytes 294920 | tf_op jit(solution)/shard_map/while/body/eval_jaxpr/ppermute | solution.py:10
  312.6 13.0 %collective-permute-start = (f32[32,768]{1,0:T(8,128)S(1)}, f32[32,768]{1,0:T(8,128)S(1)}, u32[]{:S(2)}, u32[]{:S(2)}) collective-permute-start(f32[32,768]{1,0:T(8,128)S(1)} %get-tuple-element.565), channel_id=1, source_target_pairs={{0,8},{8,16},{16,24},{24,32},{32,40},{40,48},{48,56},{56,64},{64,7... | collective-permute-start | bytes 294920 | tf_op jit(solution)/shard_map/while/body/eval_jaxpr/ppermute | solution.py:10
  327.4 9.7 %collective-permute-start = (f32[32,768]{1,0:T(8,128)S(1)}, f32[32,768]{1,0:T(8,128)S(1)}, u32[]{:S(2)}, u32[]{:S(2)}) collective-permute-start(f32[32,768]{1,0:T(8,128)S(1)} %get-tuple-element.565), channel_id=1, source_target_pairs={{0,8},{8,16},{16,24},{24,32},{32,40},{40,48},{48,56},{56,64},{64,7... | collective-permute-start | bytes 294920 | tf_op jit(solution)/shard_map/while/body/eval_jaxpr/ppermute | solution.py:10
  338.8 13.2 %collective-permute-start = (f32[32,768]{1,0:T(8,128)S(1)}, f32[32,768]{1,0:T(8,128)S(1)}, u32[]{:S(2)}, u32[]{:S(2)}) collective-permute-start(f32[32,768]{1,0:T(8,128)S(1)} %get-tuple-element.565), channel_id=1, source_target_pairs={{0,8},{8,16},{16,24},{24,32},{32,40},{40,48},{48,56},{56,64},{64,7... | collective-permute-start | bytes 294920 | tf_op jit(solution)/shard_map/while/body/eval_jaxpr/ppermute | solution.py:10
  353.8 9.6 %collective-permute-start = (f32[32,768]{1,0:T(8,128)S(1)}, f32[32,768]{1,0:T(8,128)S(1)}, u32[]{:S(2)}, u32[]{:S(2)}) collective-permute-start(f32[32,768]{1,0:T(8,128)S(1)} %get-tuple-element.565), channel_id=1, source_target_pairs={{0,8},{8,16},{16,24},{24,32},{32,40},{40,48},{48,56},{56,64},{64,7... | collective-permute-start | bytes 294920 | tf_op jit(solution)/shard_map/while/body/eval_jaxpr/ppermute | solution.py:10
  365.1 13.2 %collective-permute-start = (f32[32,768]{1,0:T(8,128)S(1)}, f32[32,768]{1,0:T(8,128)S(1)}, u32[]{:S(2)}, u32[]{:S(2)}) collective-permute-start(f32[32,768]{1,0:T(8,128)S(1)} %get-tuple-element.565), channel_id=1, source_target_pairs={{0,8},{8,16},{16,24},{24,32},{32,40},{40,48},{48,56},{56,64},{64,7... | collective-permute-start | bytes 294920 | tf_op jit(solution)/shard_map/while/body/eval_jaxpr/ppermute | solution.py:10
  391.1 13.2 %collective-permute-start = (f32[32,768]{1,0:T(8,128)S(1)}, f32[32,768]{1,0:T(8,128)S(1)}, u32[]{:S(2)}, u32[]{:S(2)}) collective-permute-start(f32[32,768]{1,0:T(8,128)S(1)} %get-tuple-element.565), channel_id=1, source_target_pairs={{0,8},{8,16},{16,24},{24,32},{32,40},{40,48},{48,56},{56,64},{64,7... | collective-permute-start | bytes 294920 | tf_op jit(solution)/shard_map/while/body/eval_jaxpr/ppermute | solution.py:10
  417.1 13.0 %collective-permute-start = (f32[32,768]{1,0:T(8,128)S(1)}, f32[32,768]{1,0:T(8,128)S(1)}, u32[]{:S(2)}, u32[]{:S(2)}) collective-permute-start(f32[32,768]{1,0:T(8,128)S(1)} %get-tuple-element.565), channel_id=1, source_target_pairs={{0,8},{8,16},{16,24},{24,32},{32,40},{40,48},{48,56},{56,64},{64,7... | collective-permute-start | bytes 294920 | tf_op jit(solution)/shard_map/while/body/eval_jaxpr/ppermute | solution.py:10
  442.9 13.0 %collective-permute-start = (f32[32,768]{1,0:T(8,128)S(1)}, f32[32,768]{1,0:T(8,128)S(1)}, u32[]{:S(2)}, u32[]{:S(2)}) collective-permute-start(f32[32,768]{1,0:T(8,128)S(1)} %get-tuple-element.565), channel_id=1, source_target_pairs={{0,8},{8,16},{16,24},{24,32},{32,40},{40,48},{48,56},{56,64},{64,7... | collective-permute-start | bytes 294920 | tf_op jit(solution)/shard_map/while/body/eval_jaxpr/ppermute | solution.py:10
  457.7 9.3 %collective-permute-start = (f32[32,768]{1,0:T(8,128)S(1)}, f32[32,768]{1,0:T(8,128)S(1)}, u32[]{:S(2)}, u32[]{:S(2)}) collective-permute-start(f32[32,768]{1,0:T(8,128)S(1)} %get-tuple-element.565), channel_id=1, source_target_pairs={{0,8},{8,16},{16,24},{24,32},{32,40},{40,48},{48,56},{56,64},{64,7... | collective-permute-start | bytes 294920 | tf_op jit(solution)/shard_map/while/body/eval_jaxpr/ppermute | solution.py:10
  468.8 11.1 %collective-permute-start = (f32[32,768]{1,0:T(8,128)S(1)}, f32[32,768]{1,0:T(8,128)S(1)}, u32[]{:S(2)}, u32[]{:S(2)}) collective-permute-start(f32[32,768]{1,0:T(8,128)S(1)} %get-tuple-element.565), channel_id=1, source_target_pairs={{0,8},{8,16},{16,24},{24,32},{32,40},{40,48},{48,56},{56,64},{64,7... | collective-permute-start | bytes 294920 | tf_op jit(solution)/shard_map/while/body/eval_jaxpr/ppermute | solution.py:10
  481.6 9.3 %collective-permute-start = (f32[32,768]{1,0:T(8,128)S(1)}, f32[32,768]{1,0:T(8,128)S(1)}, u32[]{:S(2)}, u32[]{:S(2)}) collective-permute-start(f32[32,768]{1,0:T(8,128)S(1)} %get-tuple-element.565), channel_id=1, source_target_pairs={{0,8},{8,16},{16,24},{24,32},{32,40},{40,48},{48,56},{56,64},{64,7... | collective-permute-start | bytes 294920 | tf_op jit(solution)/shard_map/while/body/eval_jaxpr/ppermute | solution.py:10
  492.7 11.1 %collective-permute-start = (f32[32,768]{1,0:T(8,128)S(1)}, f32[32,768]{1,0:T(8,128)S(1)}, u32[]{:S(2)}, u32[]{:S(2)}) collective-permute-start(f32[32,768]{1,0:T(8,128)S(1)} %get-tuple-element.565), channel_id=1, source_target_pairs={{0,8},{8,16},{16,24},{24,32},{32,40},{40,48},{48,56},{56,64},{64,7... | collective-permute-start | bytes 294920 | tf_op jit(solution)/shard_map/while/body/eval_jaxpr/ppermute | solution.py:10
  505.5 9.3 %collective-permute-start = (f32[32,768]{1,0:T(8,128)S(1)}, f32[32,768]{1,0:T(8,128)S(1)}, u32[]{:S(2)}, u32[]{:S(2)}) collective-permute-start(f32[32,768]{1,0:T(8,128)S(1)} %get-tuple-element.565), channel_id=1, source_target_pairs={{0,8},{8,16},{16,24},{24,32},{32,40},{40,48},{48,56},{56,64},{64,7... | collective-permute-start | bytes 294920 | tf_op jit(solution)/shard_map/while/body/eval_jaxpr/ppermute | solution.py:10
  516.5 11.1 %collective-permute-start = (f32[32,768]{1,0:T(8,128)S(1)}, f32[32,768]{1,0:T(8,128)S(1)}, u32[]{:S(2)}, u32[]{:S(2)}) collective-permute-start(f32[32,768]{1,0:T(8,128)S(1)} %get-tuple-element.565), channel_id=1, source_target_pairs={{0,8},{8,16},{16,24},{24,32},{32,40},{40,48},{48,56},{56,64},{64,7... | collective-permute-start | bytes 294920 | tf_op jit(solution)/shard_map/while/body/eval_jaxpr/ppermute | solution.py:10
  529.3 9.3 %collective-permute-start = (f32[32,768]{1,0:T(8,128)S(1)}, f32[32,768]{1,0:T(8,128)S(1)}, u32[]{:S(2)}, u32[]{:S(2)}) collective-permute-start(f32[32,768]{1,0:T(8,128)S(1)} %get-tuple-element.565), channel_id=1, source_target_pairs={{0,8},{8,16},{16,24},{24,32},{32,40},{40,48},{48,56},{56,64},{64,7... | collective-permute-start | bytes 294920 | tf_op jit(solution)/shard_map/while/body/eval_jaxpr/ppermute | solution.py:10
  540.4 12.3 %collective-permute-start = (f32[32,768]{1,0:T(8,128)S(1)}, f32[32,768]{1,0:T(8,128)S(1)}, u32[]{:S(2)}, u32[]{:S(2)}) collective-permute-start(f32[32,768]{1,0:T(8,128)S(1)} %get-tuple-element.565), channel_id=1, source_target_pairs={{0,8},{8,16},{16,24},{24,32},{32,40},{40,48},{48,56},{56,64},{64,7... | collective-permute-start | bytes 294920 | tf_op jit(solution)/shard_map/while/body/eval_jaxpr/ppermute | solution.py:10
  554.4 9.3 %collective-permute-start = (f32[32,768]{1,0:T(8,128)S(1)}, f32[32,768]{1,0:T(8,128)S(1)}, u32[]{:S(2)}, u32[]{:S(2)}) collective-permute-start(f32[32,768]{1,0:T(8,128)S(1)} %get-tuple-element.565), channel_id=1, source_target_pairs={{0,8},{8,16},{16,24},{24,32},{32,40},{40,48},{48,56},{56,64},{64,7... | collective-permute-start | bytes 294920 | tf_op jit(solution)/shard_map/while/body/eval_jaxpr/ppermute | solution.py:10
  567.4 11.1 %collective-permute-start.2 = (f32[32,768]{1,0:T(8,128)S(1)}, f32[32,768]{1,0:T(8,128)S(1)}, u32[]{:S(2)}, u32[]{:S(2)}) collective-permute-start(f32[32,768]{1,0:T(8,128)S(1)} %get-tuple-element.576), channel_id=1, source_target_pairs={{0,8},{8,16},{16,24},{24,32},{32,40},{40,48},{48,56},{56,64},{64,7... | collective-permute-start | bytes 294920 | tf_op jit(solution)/shard_map/while/body/eval_jaxpr/ppermute | solution.py:10
  580.2 9.3 %collective-permute-start.2 = (f32[32,768]{1,0:T(8,128)S(1)}, f32[32,768]{1,0:T(8,128)S(1)}, u32[]{:S(2)}, u32[]{:S(2)}) collective-permute-start(f32[32,768]{1,0:T(8,128)S(1)} %get-tuple-element.576), channel_id=1, source_target_pairs={{0,8},{8,16},{16,24},{24,32},{32,40},{40,48},{48,56},{56,64},{64,7... | collective-permute-start | bytes 294920 | tf_op jit(solution)/shard_map/while/body/eval_jaxpr/ppermute | solution.py:10
  591.3 11.1 %collective-permute-start.2 = (f32[32,768]{1,0:T(8,128)S(1)}, f32[32,768]{1,0:T(8,128)S(1)}, u32[]{:S(2)}, u32[]{:S(2)}) collective-permute-start(f32[32,768]{1,0:T(8,128)S(1)} %get-tuple-element.576), channel_id=1, source_target_pairs={{0,8},{8,16},{16,24},{24,32},{32,40},{40,48},{48,56},{56,64},{64,7... | collective-permute-start | bytes 294920 | tf_op jit(solution)/shard_map/while/body/eval_jaxpr/ppermute | solution.py:10
  604.1 9.3 %collective-permute-start.2 = (f32[32,768]{1,0:T(8,128)S(1)}, f32[32,768]{1,0:T(8,128)S(1)}, u32[]{:S(2)}, u32[]{:S(2)}) collective-permute-start(f32[32,768]{1,0:T(8,128)S(1)} %get-tuple-element.576), channel_id=1, source_target_pairs={{0,8},{8,16},{16,24},{24,32},{32,40},{40,48},{48,56},{56,64},{64,7... | collective-permute-start | bytes 294920 | tf_op jit(solution)/shard_map/while/body/eval_jaxpr/ppermute | solution.py:10
  615.2 11.2 %collective-permute-start.2 = (f32[32,768]{1,0:T(8,128)S(1)}, f32[32,768]{1,0:T(8,128)S(1)}, u32[]{:S(2)}, u32[]{:S(2)}) collective-permute-start(f32[32,768]{1,0:T(8,128)S(1)} %get-tuple-element.576), channel_id=1, source_target_pairs={{0,8},{8,16},{16,24},{24,32},{32,40},{40,48},{48,56},{56,64},{64,7... | collective-permute-start | bytes 294920 | tf_op jit(solution)/shard_map/while/body/eval_jaxpr/ppermute | solution.py:10
  639.2 13.0 %collective-permute-start.2 = (f32[32,768]{1,0:T(8,128)S(1)}, f32[32,768]{1,0:T(8,128)S(1)}, u32[]{:S(2)}, u32[]{:S(2)}) collective-permute-start(f32[32,768]{1,0:T(8,128)S(1)} %get-tuple-element.576), channel_id=1, source_target_pairs={{0,8},{8,16},{16,24},{24,32},{32,40},{40,48},{48,56},{56,64},{64,7... | collective-permute-start | bytes 294920 | tf_op jit(solution)/shard_map/while/body/eval_jaxpr/ppermute | solution.py:10
  654.0 9.3 %collective-permute-start.2 = (f32[32,768]{1,0:T(8,128)S(1)}, f32[32,768]{1,0:T(8,128)S(1)}, u32[]{:S(2)}, u32[]{:S(2)}) collective-permute-start(f32[32,768]{1,0:T(8,128)S(1)} %get-tuple-element.576), channel_id=1, source_target_pairs={{0,8},{8,16},{16,24},{24,32},{32,40},{40,48},{48,56},{56,64},{64,7... | collective-permute-start | bytes 294920 | tf_op jit(solution)/shard_map/while/body/eval_jaxpr/ppermute | solution.py:10
  (69 other events, 444.2 us)
Sparse Core Ops, SparseCore 0:
  567.3 192.3 all-gather.2
where the time goes:
time: 788 us; the launch traced here: 785 us
  starting transfers between devices  465 us (59%)
  waiting for transfers between devices  176 us (22%)
  matrix products  93.4 us (12%)
  other arithmetic  25.5 us (3%)
  between operations  14.1 us (2%)
    ppermute x96, starting transfers between devices, passed_along(): return lax.ppermute(block, axis, route)  465 us
    all_gather x1, waiting for transfers between devices, over_pieces(): return lax.all_gather(value, axis).sum(0)  93.6 us
    ppermute x96, waiting for transfers between devices, passed_along(): return lax.ppermute(block, axis, route)  82.3 us
    dot_general x10, matrix products, compute(): jnp.dot(joined, trace_map, precision=lax.Precision.HIGHEST, preferred_ele...  78.6 us
  transfers between devices with their start and end apart: 97, of which 49 were waited for; matrix products, arithmetic and copies ran while one was open for 1% of the time, Pallas kernels for 0%

commit v1 on v0

v1 whole, which is shorter than its diff:
```python
import functools

import jax
import jax.numpy as jnp
from jax import lax
from jax.experimental import pallas as pl
from jax.experimental.pallas import tpu as pltpu
from jax.sharding import PartitionSpec as P

PIECES = 2
UNROLL = 8
VMEM = pl.BlockSpec(memory_space=pltpu.VMEM)
SMEM = pl.BlockSpec(memory_space=pltpu.SMEM)
HBM = pl.BlockSpec(memory_space=pltpu.HBM)
F32 = jnp.float32
BF16 = jnp.bfloat16


def halves(value):
    high = value.astype(BF16)
    low = (value - high.astype(F32)).astype(BF16)
    return high, low


def product(value, high_ref, low_ref):
    rows = value.shape[0]
    high, low = halves(value)
    both = jnp.concatenate([high, low], axis=0)
    main = jnp.dot(both, high_ref[...], preferred_element_type=F32)
    rest = jnp.dot(high, low_ref[...], preferred_element_type=F32)
    return main[:rows] + (main[rows:] + rest)


def held(value):
    return pltpu.with_memory_space_constraint(value, pltpu.VMEM)


def params(mib):
    return pltpu.CompilerParams(vmem_limit_bytes=mib << 20)


def split_kernel(chunk, w_hbm, high_ref, low_ref, buf, sem):
    count = w_hbm.shape[0] // chunk

    def fetch(i):
        return pltpu.make_async_copy(
            w_hbm.at[pl.ds(i * chunk, chunk)], buf.at[i % 2], sem.at[i % 2]
        )

    fetch(0).start()
    for i in range(count):
        if i + 1 < count:
            fetch(i + 1).start()
        fetch(i).wait()
        high, low = halves(buf[i % 2])
        high_ref[i * chunk : (i + 1) * chunk, :] = high
        low_ref[i * chunk : (i + 1) * chunk, :] = low


def split_operator(w):
    order = w.shape[0]
    chunk = order // 6
    shape = pltpu.VMEM((order, order), BF16)
    return pl.pallas_call(
        functools.partial(split_kernel, chunk),
        out_shape=(shape, shape),
        in_specs=[HBM],
        out_specs=(VMEM, VMEM),
        scratch_shapes=[
            pltpu.VMEM((2, chunk, order), F32),
            pltpu.SemaphoreType.DMA((2,)),
        ],
        compiler_params=params(16),
        name="split_operator",
    )(w)


def when_active(offset, count, age_ref):
    age = age_ref[0] + offset
    piece = lax.div(age, 2)
    return (age >= 0) & (age < 2 * count) & (age == 2 * piece), piece


def south_kernel(offset, count, age_ref, placed_ref, south_ref, high_ref, low_ref, out_ref):
    active, piece = when_active(offset, count, age_ref)
    half = south_ref.shape[1]

    @pl.when(active)
    def _():
        out_ref[...] = placed_ref[piece] + product(
            south_ref[...], high_ref.at[half:, :], low_ref.at[half:, :]
        )


def west_kernel(offset, count, first, age_ref, partial_ref, west_ref, high_ref, low_ref, *refs):
    out_ref = refs[-1]
    active, _ = when_active(offset, count, age_ref)
    half = west_ref.shape[1]
    cols = slice(first, first + half)

    @pl.when(active)
    def _():
        out_ref[...] = partial_ref[:, cols] + product(
            west_ref[...], high_ref.at[:half, cols], low_ref.at[:half, cols]
        )


def south_part(offset, count, age, placed, south, high, low):
    _, width, order = placed.shape
    return pl.pallas_call(
        functools.partial(south_kernel, offset, count),
        out_shape=jax.ShapeDtypeStruct((width, order), F32),
        in_specs=[SMEM] + [VMEM] * 4,
        out_specs=VMEM,
        compiler_params=params(4),
        cost_estimate=pl.CostEstimate(flops=6 * width * order * order // 2, bytes_accessed=1 << 20, transcendentals=0),
        name="south",
    )(age, held(placed), south, held(high), held(low))


def west_part(offset, count, first, age, partial, west, high, low, after=()):
    width, half = west.shape
    return pl.pallas_call(
        functools.partial(west_kernel, offset, count, first),
        out_shape=jax.ShapeDtypeStruct((width, half), F32),
        in_specs=[SMEM] + [VMEM] * (4 + len(after)),
        out_specs=VMEM,
        compiler_params=params(4),
        cost_estimate=pl.CostEstimate(flops=6 * width * half * half, bytes_accessed=1 << 20, transcendentals=0),
        name="north" if first else "east",
    )(age, partial, west, held(high), held(low), *after)


def place_kernel(plan_ref, rows_ref, sources_ref, out_ref):
    batches, columns, placed_count = sources_ref.shape
    order = out_ref.shape[-1]
    at = lax.broadcasted_iota(jnp.int32, (order, placed_count), 0)
    placing = jnp.where(at == rows_ref[...], 1.0, 0.0).astype(BF16)
    for b in range(batches):
        source = sources_ref[plan_ref[b]]
        high, middle = halves(source)
        low = (source - high.astype(F32) - middle.astype(F32)).astype(BF16)
        parts = jnp.concatenate([high, middle, low], axis=0)
        spread = lax.dot_general(
            parts, placing, (((1,), (1,)), ((), ())), preferred_element_type=F32
        )
        out_ref[b] = spread[:columns] + (
            spread[columns : 2 * columns] + spread[2 * columns :]
        )


def place(plan, rows, sources, order):
    batches, columns, _ = sources.shape
    return pl.pallas_call(
        place_kernel,
        out_shape=pltpu.VMEM((batches, columns, order), F32),
        in_specs=[SMEM, VMEM, VMEM],
        out_specs=VMEM,
        compiler_params=params(8),
        name="place",
    )(plan, rows, sources)


def sweep_pairs(shape, parity, dx, dy):
    nx, ny = shape
    return [
        (x * ny + y, (x + dx) * ny + y + dy)
        for x in range(parity, nx - dx, 2)
        for y in range(ny - dy)
    ]


def body(shape, operators, sources, source_rows, batch_plan):
    nx, ny = shape
    axes = ("gx", "gy")
    depth = lax.axis_index("gx") + 2 * lax.axis_index("gy")
    order = operators.shape[-1]
    half = order // 2
    _, _, batches, columns, placed_count = sources.shape
    width = columns // PIECES
    count = batches * PIECES
    placed = place(batch_plan, source_rows[0], sources[0, 0], order)
    placed = placed.reshape(count, width, order)
    high, low = split_operator(operators[0, 0])

    halves_needed = nx - 1 + 2 * (ny - 1) + 2 * (count - 1) + 1
    trips = -(-halves_needed // (2 * UNROLL))

    def advance(trip, carry):
        west, south, results = carry
        west, south = list(west), list(south)
        age = trip * (2 * UNROLL) - depth
        age_ref = age[None].astype(jnp.int32)
        for offset in range(2 * UNROLL):
            parity = offset % 2
            partial = south_part(offset, count, age_ref, placed, south[parity], high, low)
            to_east = west_part(offset, count, 0, age_ref, partial, west[parity], high, low)
            west[1 - parity] = lax.ppermute(
                to_east, axes, sweep_pairs(shape, parity, 1, 0)
            )
            to_north = west_part(
                offset, count, half, age_ref, partial, west[parity], high, low, (to_east,)
            )
            south[parity] = lax.ppermute(
                to_north, axes, sweep_pairs(shape, parity, 0, 1)
            )
            now = age + offset
            active = (now >= 0) & (now < 2 * count) & (now % 2 == 0)
            slot = jnp.where(active, now // 2 + 1, 0)
            results = lax.dynamic_update_slice(results, to_east[None], (slot, 0, 0))
            results = lax.dynamic_update_slice(results, to_north[None], (slot, 0, half))
        return (tuple(west), tuple(south), results)

    zero = jnp.zeros((width, half), F32)
    carry = ((zero, zero), (zero, zero), jnp.zeros((count + 1, width, order), F32))
    _, _, results = lax.fori_loop(0, trips, advance, carry)
    first = results[1 : 1 + PIECES].reshape(columns, order)
    rest = results[1 + PIECES :]
    partial_gram = lax.dot_general(
        first,
        first,
        (((1,), (1,)), ((), ())),
        precision=lax.Precision.HIGHEST,
        preferred_element_type=F32,
    )
    gram = lax.psum(partial_gram, axes) / (nx * ny * order)
    lower = jnp.linalg.cholesky(gram)
    basis = jax.scipy.linalg.solve_triangular(lower, first, lower=True)
    traces = rest.reshape(batches - 1, columns, order)
    return (traces[None, None], basis[None, None], lower.T)


def solution(mesh):
    return jax.shard_map(
        functools.partial(body, (mesh.shape["gx"], mesh.shape["gy"])),
        mesh=mesh,
        in_specs=(
            P("gx", "gy", None, None),
            P("gx", "gy", None, None, None),
            P("gx", "gy", None),
            P(),
        ),
        out_specs=(P("gx", "gy", None, None, None), P("gx", "gy", None, None), P()),
        check_vma=False,
    )
```

time: 788 us -> 603 us (0.77)
  waiting for transfers between devices: 176 us -> 0.48 us
  local copies, waits for them, and re-layouts: 6.24 us -> 144 us
  starting transfers between devices: 465 us -> 335 us
  matrix products: 93.4 us -> 1.75 us
  blocking collectives: 0 us -> 79.7 us
  Pallas kernels: 0 us -> 23.1 us
  other arithmetic: 25.5 us -> 12.1 us
  between operations: 14.1 us -> 0.73 us
    ppermute x96 -> x128, starting transfers between devices: 465 us -> 335 us  [the longest x64 231 us: advance(): lax.ppermute(to_east, axes, sweep_pairs(shape, parity, 1, 0))]
    all_gather x1 -> x0, waiting for transfers between devices: 93.6 us -> none  [over_pieces(): return lax.all_gather(value, axis).sum(0)]
    dot_general x20 -> x0, matrix products: 91.1 us -> none  [the longest x10 78.6 us: compute(): jnp.dot(joined, trace_map, precision=lax.Precision.HIGHEST, preferred_ele...]
    dynamic_update_slice x0 -> x128, local copies, waits for them, and re-layouts: none -> 83.9 us  [the longest x64 42.2 us: advance(): results = lax.dynamic_update_slice(results, to_north[None], (slot, 0, half))]
    ppermute x96 -> x128, waiting for transfers between devices: 82.3 us -> 0.48 us  [the longest x64 0.31 us: advance(): lax.ppermute(to_east, axes, sweep_pairs(shape, parity, 1, 0))]
    psum x0 -> x1, blocking collectives: none -> 79.7 us  [body(): gram = lax.psum(partial_gram, axes) / (nx * ny * order)]
    while x0 -> x64, local copies, waits for them, and re-layouts: none -> 46.1 us
    pallas_call x0 -> x194, Pallas kernels: none -> 23.1 us  [the longest x128 10.8 us: west_part(): pl.pallas_call(functools.partial(west_kernel, offset, count, first), out_...]
  transfers between devices with their start and end apart: 97 -> 128, of which waited for: 49 -> 0; matrix products, arithmetic and copies ran while one was open for 1% -> 14% of each run, Pallas kernels for 0% -> 3%
where the time goes in v1:
time: 603 us; the launch traced here: 600 us
  starting transfers between devices  335 us (56%)
  local copies, waits for them, and re-layouts  144 us (24%)
  blocking collectives  79.7 us (13%)
  Pallas kernels  23.1 us (4%)
  other arithmetic  12.1 us (2%)
    ppermute x64, starting transfers between devices, advance(): lax.ppermute(to_east, axes, sweep_pairs(shape, parity, 1, 0))  231 us
    ppermute x64, starting transfers between devices, advance(): lax.ppermute(to_north, axes, sweep_pairs(shape, parity, 0, 1))  103 us
    psum x1, blocking collectives, body(): gram = lax.psum(partial_gram, axes) / (nx * ny * order)  79.7 us
    while x64, local copies, waits for them, and re-layouts  46.1 us
    dynamic_update_slice x64, local copies, waits for them, and re-layouts, advance(): results = lax.dynamic_update_slice(results, to_north[None], (slot, 0, half))  42.2 us
    dynamic_update_slice x64, local copies, waits for them, and re-layouts, advance(): results = lax.dynamic_update_slice(results, to_east[None], (slot, 0, 0))  41.7 us
  transfers between devices with their start and end apart: 128, of which 0 were waited for; matrix products, arithmetic and copies ran while one was open for 14% of the time, Pallas kernels for 3%

profile of v1, /device:TPU:1, one launch (start us, length us, event | category | flops | bytes accessed | tf_op | source)
XLA Modules:
  0.0 599.5 jit_solution(12934022581751367266)
XLA Ops:
  13.7 487.8 %while.22 = (s32[]{:T(128)}, f32[32,768]{1,0:T(8,128)S(1)}, f32[32,768]{1,0:T(8,128)S(1)}, f32[32,768]{1,0:T(8,128)S(1)}, f32[11,32,1536]{2,1,0:T(8,128)}, /*ind...) while((s32[]{:T(128)}, f32[32,768]{1,0:T(8,128)S(1)}, ...), condition=%wide.region_1.2_spmd, body=%wide.region_0.1_spmd.sunk | while | flops 7247757312 | bytes 173022288 | solution.py:216
  39.6 6.6 %collective-permute-start.4 = (f32[32,768]{1,0:T(8,128)S(1)}, f32[32,768]{1,0:T(8,128)S(1)}, u32[]{:S(2)}, u32[]{:S(2)}) collective-permute-start(f32[32,768]{1,0:T(8,128)S(1)} %east.18.refs_0_), channel_id=1, source_target_pairs={{0,8},{1,9},{2,10},{3,11},{4,12},{5,13},{6,14},{7,15},{16,24},{17,... | collective-permute-start | bytes 294920 | tf_op jit(solution)/shard_map/while/body/eval_jaxpr/ppermute | solution.py:198
  55.1 7.1 %collective-permute-start.8 = (f32[32,768]{1,0:T(8,128)S(1)}, f32[32,768]{1,0:T(8,128)S(1)}, u32[]{:S(2)}, u32[]{:S(2)}) collective-permute-start(f32[32,768]{1,0:T(8,128)S(1)} %east.20.refs_0_), channel_id=1, source_target_pairs={{0,8},{1,9},{2,10},{3,11},{4,12},{5,13},{6,14},{7,15},{16,24},{17,... | collective-permute-start | bytes 294920 | tf_op jit(solution)/shard_map/while/body/eval_jaxpr/ppermute | solution.py:198
  97.2 5.0 collective-permute-start.20
  110.3 6.4 %collective-permute-start.24 = (f32[32,768]{1,0:T(8,128)S(1)}, f32[32,768]{1,0:T(8,128)S(1)}, u32[]{:S(2)}, u32[]{:S(2)}) collective-permute-start(f32[32,768]{1,0:T(8,128)S(1)} %east.28.refs_0_), channel_id=1, source_target_pairs={{0,8},{1,9},{2,10},{3,11},{4,12},{5,13},{6,14},{7,15},{16,24},{17,... | collective-permute-start | bytes 294920 | tf_op jit(solution)/shard_map/while/body/eval_jaxpr/ppermute | solution.py:198
  124.9 5.9 collective-permute-start.28
  143.6 6.2 %collective-permute-start = (f32[32,768]{1,0:T(8,128)S(1)}, f32[32,768]{1,0:T(8,128)S(1)}, u32[]{:S(2)}, u32[]{:S(2)}) collective-permute-start(f32[32,768]{1,0:T(8,128)S(1)} %east.16.refs_0_), channel_id=1, source_target_pairs={{0,8},{1,9},{2,10},{3,11},{4,12},{5,13},{6,14},{7,15},{16,24},{17,... | collective-permute-start | bytes 294920 | tf_op jit(solution)/shard_map/while/body/eval_jaxpr/ppermute | solution.py:198
  167.6 5.6 collective-permute-start.4
  181.3 6.0 %collective-permute-start.8 = (f32[32,768]{1,0:T(8,128)S(1)}, f32[32,768]{1,0:T(8,128)S(1)}, u32[]{:S(2)}, u32[]{:S(2)}) collective-permute-start(f32[32,768]{1,0:T(8,128)S(1)} %east.20.refs_0_), channel_id=1, source_target_pairs={{0,8},{1,9},{2,10},{3,11},{4,12},{5,13},{6,14},{7,15},{16,24},{17,... | collective-permute-start | bytes 294920 | tf_op jit(solution)/shard_map/while/body/eval_jaxpr/ppermute | solution.py:198
  194.1 7.4 %collective-permute-start.12 = (f32[32,768]{1,0:T(8,128)S(1)}, f32[32,768]{1,0:T(8,128)S(1)}, u32[]{:S(2)}, u32[]{:S(2)}) collective-permute-start(f32[32,768]{1,0:T(8,128)S(1)} %east.22.refs_0_), channel_id=1, source_target_pairs={{0,8},{1,9},{2,10},{3,11},{4,12},{5,13},{6,14},{7,15},{16,24},{17,... | collective-permute-start | bytes 294920 | tf_op jit(solution)/shard_map/while/body/eval_jaxpr/ppermute | solution.py:198
  208.2 6.5 %collective-permute-start.16 = (f32[32,768]{1,0:T(8,128)S(1)}, f32[32,768]{1,0:T(8,128)S(1)}, u32[]{:S(2)}, u32[]{:S(2)}) collective-permute-start(f32[32,768]{1,0:T(8,128)S(1)} %east.24.refs_0_), channel_id=1, source_target_pairs={{0,8},{1,9},{2,10},{3,11},{4,12},{5,13},{6,14},{7,15},{16,24},{17,... | collective-permute-start | bytes 294920 | tf_op jit(solution)/shard_map/while/body/eval_jaxpr/ppermute | solution.py:198
  221.0 6.5 %collective-permute-start.20 = (f32[32,768]{1,0:T(8,128)S(1)}, f32[32,768]{1,0:T(8,128)S(1)}, u32[]{:S(2)}, u32[]{:S(2)}) collective-permute-start(f32[32,768]{1,0:T(8,128)S(1)} %east.26.refs_0_), channel_id=1, source_target_pairs={{0,8},{1,9},{2,10},{3,11},{4,12},{5,13},{6,14},{7,15},{16,24},{17,... | collective-permute-start | bytes 294920 | tf_op jit(solution)/shard_map/while/body/eval_jaxpr/ppermute | solution.py:198
  233.8 7.4 %collective-permute-start.24 = (f32[32,768]{1,0:T(8,128)S(1)}, f32[32,768]{1,0:T(8,128)S(1)}, u32[]{:S(2)}, u32[]{:S(2)}) collective-permute-start(f32[32,768]{1,0:T(8,128)S(1)} %east.28.refs_0_), channel_id=1, source_target_pairs={{0,8},{1,9},{2,10},{3,11},{4,12},{5,13},{6,14},{7,15},{16,24},{17,... | collective-permute-start | bytes 294920 | tf_op jit(solution)/shard_map/while/body/eval_jaxpr/ppermute | solution.py:198
  247.4 7.4 %collective-permute-start.28 = (f32[32,768]{1,0:T(8,128)S(1)}, f32[32,768]{1,0:T(8,128)S(1)}, u32[]{:S(2)}, u32[]{:S(2)}) collective-permute-start(f32[32,768]{1,0:T(8,128)S(1)} %east.30.refs_0_), channel_id=1, source_target_pairs={{0,8},{1,9},{2,10},{3,11},{4,12},{5,13},{6,14},{7,15},{16,24},{17,... | collective-permute-start | bytes 294920 | tf_op jit(solution)/shard_map/while/body/eval_jaxpr/ppermute | solution.py:198
  265.8 7.7 %collective-permute-start = (f32[32,768]{1,0:T(8,128)S(1)}, f32[32,768]{1,0:T(8,128)S(1)}, u32[]{:S(2)}, u32[]{:S(2)}) collective-permute-start(f32[32,768]{1,0:T(8,128)S(1)} %east.16.refs_0_), channel_id=1, source_target_pairs={{0,8},{1,9},{2,10},{3,11},{4,12},{5,13},{6,14},{7,15},{16,24},{17,... | collective-permute-start | bytes 294920 | tf_op jit(solution)/shard_map/while/body/eval_jaxpr/ppermute | solution.py:198
  289.4 7.4 %collective-permute-start.4 = (f32[32,768]{1,0:T(8,128)S(1)}, f32[32,768]{1,0:T(8,128)S(1)}, u32[]{:S(2)}, u32[]{:S(2)}) collective-permute-start(f32[32,768]{1,0:T(8,128)S(1)} %east.18.refs_0_), channel_id=1, source_target_pairs={{0,8},{1,9},{2,10},{3,11},{4,12},{5,13},{6,14},{7,15},{16,24},{17,... | collective-permute-start | bytes 294920 | tf_op jit(solution)/shard_map/while/body/eval_jaxpr/ppermute | solution.py:198
  303.1 7.4 %collective-permute-start.8 = (f32[32,768]{1,0:T(8,128)S(1)}, f32[32,768]{1,0:T(8,128)S(1)}, u32[]{:S(2)}, u32[]{:S(2)}) collective-permute-start(f32[32,768]{1,0:T(8,128)S(1)} %east.20.refs_0_), channel_id=1, source_target_pairs={{0,8},{1,9},{2,10},{3,11},{4,12},{5,13},{6,14},{7,15},{16,24},{17,... | collective-permute-start | bytes 294920 | tf_op jit(solution)/shard_map/while/body/eval_jaxpr/ppermute | solution.py:198
  316.8 7.4 %collective-permute-start.12 = (f32[32,768]{1,0:T(8,128)S(1)}, f32[32,768]{1,0:T(8,128)S(1)}, u32[]{:S(2)}, u32[]{:S(2)}) collective-permute-start(f32[32,768]{1,0:T(8,128)S(1)} %east.22.refs_0_), channel_id=1, source_target_pairs={{0,8},{1,9},{2,10},{3,11},{4,12},{5,13},{6,14},{7,15},{16,24},{17,... | collective-permute-start | bytes 294920 | tf_op jit(solution)/shard_map/while/body/eval_jaxpr/ppermute | solution.py:198
  330.5 6.0 %collective-permute-start.16 = (f32[32,768]{1,0:T(8,128)S(1)}, f32[32,768]{1,0:T(8,128)S(1)}, u32[]{:S(2)}, u32[]{:S(2)}) collective-permute-start(f32[32,768]{1,0:T(8,128)S(1)} %east.24.refs_0_), channel_id=1, source_target_pairs={{0,8},{1,9},{2,10},{3,11},{4,12},{5,13},{6,14},{7,15},{16,24},{17,... | collective-permute-start | bytes 294920 | tf_op jit(solution)/shard_map/while/body/eval_jaxpr/ppermute | solution.py:198
  342.8 6.2 %collective-permute-start.20 = (f32[32,768]{1,0:T(8,128)S(1)}, f32[32,768]{1,0:T(8,128)S(1)}, u32[]{:S(2)}, u32[]{:S(2)}) collective-permute-start(f32[32,768]{1,0:T(8,128)S(1)} %east.26.refs_0_), channel_id=1, source_target_pairs={{0,8},{1,9},{2,10},{3,11},{4,12},{5,13},{6,14},{7,15},{16,24},{17,... | collective-permute-start | bytes 294920 | tf_op jit(solution)/shard_map/while/body/eval_jaxpr/ppermute | solution.py:198
  355.3 7.3 %collective-permute-start.24 = (f32[32,768]{1,0:T(8,128)S(1)}, f32[32,768]{1,0:T(8,128)S(1)}, u32[]{:S(2)}, u32[]{:S(2)}) collective-permute-start(f32[32,768]{1,0:T(8,128)S(1)} %east.28.refs_0_), channel_id=1, source_target_pairs={{0,8},{1,9},{2,10},{3,11},{4,12},{5,13},{6,14},{7,15},{16,24},{17,... | collective-permute-start | bytes 294920 | tf_op jit(solution)/shard_map/while/body/eval_jaxpr/ppermute | solution.py:198
  368.8 6.9 %collective-permute-start.28 = (f32[32,768]{1,0:T(8,128)S(1)}, f32[32,768]{1,0:T(8,128)S(1)}, u32[]{:S(2)}, u32[]{:S(2)}) collective-permute-start(f32[32,768]{1,0:T(8,128)S(1)} %east.30.refs_0_), channel_id=1, source_target_pairs={{0,8},{1,9},{2,10},{3,11},{4,12},{5,13},{6,14},{7,15},{16,24},{17,... | collective-permute-start | bytes 294920 | tf_op jit(solution)/shard_map/while/body/eval_jaxpr/ppermute | solution.py:198
  386.7 7.2 %collective-permute-start = (f32[32,768]{1,0:T(8,128)S(1)}, f32[32,768]{1,0:T(8,128)S(1)}, u32[]{:S(2)}, u32[]{:S(2)}) collective-permute-start(f32[32,768]{1,0:T(8,128)S(1)} %east.16.refs_0_), channel_id=1, source_target_pairs={{0,8},{1,9},{2,10},{3,11},{4,12},{5,13},{6,14},{7,15},{16,24},{17,... | collective-permute-start | bytes 294920 | tf_op jit(solution)/shard_map/while/body/eval_jaxpr/ppermute | solution.py:198
  409.8 7.3 %collective-permute-start.4 = (f32[32,768]{1,0:T(8,128)S(1)}, f32[32,768]{1,0:T(8,128)S(1)}, u32[]{:S(2)}, u32[]{:S(2)}) collective-permute-start(f32[32,768]{1,0:T(8,128)S(1)} %east.18.refs_0_), channel_id=1, source_target_pairs={{0,8},{1,9},{2,10},{3,11},{4,12},{5,13},{6,14},{7,15},{16,24},{17,... | collective-permute-start | bytes 294920 | tf_op jit(solution)/shard_map/while/body/eval_jaxpr/ppermute | solution.py:198
  423.4 6.9 %collective-permute-start.8 = (f32[32,768]{1,0:T(8,128)S(1)}, f32[32,768]{1,0:T(8,128)S(1)}, u32[]{:S(2)}, u32[]{:S(2)}) collective-permute-start(f32[32,768]{1,0:T(8,128)S(1)} %east.20.refs_0_), channel_id=1, source_target_pairs={{0,8},{1,9},{2,10},{3,11},{4,12},{5,13},{6,14},{7,15},{16,24},{17,... | collective-permute-start | bytes 294920 | tf_op jit(solution)/shard_map/while/body/eval_jaxpr/ppermute | solution.py:198
  436.6 6.9 %collective-permute-start.12 = (f32[32,768]{1,0:T(8,128)S(1)}, f32[32,768]{1,0:T(8,128)S(1)}, u32[]{:S(2)}, u32[]{:S(2)}) collective-permute-start(f32[32,768]{1,0:T(8,128)S(1)} %east.22.refs_0_), channel_id=1, source_target_pairs={{0,8},{1,9},{2,10},{3,11},{4,12},{5,13},{6,14},{7,15},{16,24},{17,... | collective-permute-start | bytes 294920 | tf_op jit(solution)/shard_map/while/body/eval_jaxpr/ppermute | solution.py:198
  449.8 6.0 %collective-permute-start.16 = (f32[32,768]{1,0:T(8,128)S(1)}, f32[32,768]{1,0:T(8,128)S(1)}, u32[]{:S(2)}, u32[]{:S(2)}) collective-permute-start(f32[32,768]{1,0:T(8,128)S(1)} %east.24.refs_0_), channel_id=1, source_target_pairs={{0,8},{1,9},{2,10},{3,11},{4,12},{5,13},{6,14},{7,15},{16,24},{17,... | collective-permute-start | bytes 294920 | tf_op jit(solution)/shard_map/while/body/eval_jaxpr/ppermute | solution.py:198
  462.0 6.6 %collective-permute-start.20 = (f32[32,768]{1,0:T(8,128)S(1)}, f32[32,768]{1,0:T(8,128)S(1)}, u32[]{:S(2)}, u32[]{:S(2)}) collective-permute-start(f32[32,768]{1,0:T(8,128)S(1)} %east.26.refs_0_), channel_id=1, source_target_pairs={{0,8},{1,9},{2,10},{3,11},{4,12},{5,13},{6,14},{7,15},{16,24},{17,... | collective-permute-start | bytes 294920 | tf_op jit(solution)/shard_map/while/body/eval_jaxpr/ppermute | solution.py:198
  474.9 6.9 %collective-permute-start.24 = (f32[32,768]{1,0:T(8,128)S(1)}, f32[32,768]{1,0:T(8,128)S(1)}, u32[]{:S(2)}, u32[]{:S(2)}) collective-permute-start(f32[32,768]{1,0:T(8,128)S(1)} %east.28.refs_0_), channel_id=1, source_target_pairs={{0,8},{1,9},{2,10},{3,11},{4,12},{5,13},{6,14},{7,15},{16,24},{17,... | collective-permute-start | bytes 294920 | tf_op jit(solution)/shard_map/while/body/eval_jaxpr/ppermute | solution.py:198
  488.1 6.9 %collective-permute-start.28 = (f32[32,768]{1,0:T(8,128)S(1)}, f32[32,768]{1,0:T(8,128)S(1)}, u32[]{:S(2)}, u32[]{:S(2)}) collective-permute-start(f32[32,768]{1,0:T(8,128)S(1)} %east.30.refs_0_), channel_id=1, source_target_pairs={{0,8},{1,9},{2,10},{3,11},{4,12},{5,13},{6,14},{7,15},{16,24},{17,... | collective-permute-start | bytes 294920 | tf_op jit(solution)/shard_map/while/body/eval_jaxpr/ppermute | solution.py:198
  503.0 79.7 %psum.7 = f32[64,64]{0,1:T(8,128)S(1)} all-reduce(f32[64,64]{0,1:T(8,128)S(1)} %fusion.3), channel_id=1, replica_groups=mesh['gx'=32,'gy'=8] {'gx','gy'}, use_global_device_ids=true, to_apply=%region_2.3 | all-reduce | flops 4096 | bytes 32768 | tf_op jit(solution)/shard_map/psum | solution.py:226
  582.8 5.8 cholesky.16
  (649 shorter events, 314.9 us)
Async XLA Ops:
  18.6 14.5 %collective-permute-start = (f32[32,768]{1,0:T(8,128)S(1)}, f32[32,768]{1,0:T(8,128)S(1)}, u32[]{:S(2)}, u32[]{:S(2)}) collective-permute-start(f32[32,768]{1,0:T(8,128)S(1)} %east.16.refs_0_), channel_id=1, source_target_pairs={{0,8},{1,9},{2,10},{3,11},{4,12},{5,13},{6,14},{7,15},{16,24},{17,... | collective-permute-start | bytes 294920 | tf_op jit(solution)/shard_map/while/body/eval_jaxpr/ppermute | solution.py:198
  23.0 15.2 %collective-permute-start.2 = (f32[32,768]{1,0:T(8,128)S(1)}, f32[32,768]{1,0:T(8,128)S(1)}, u32[]{:S(2)}, u32[]{:S(2)}) collective-permute-start(f32[32,768]{1,0:T(8,128)S(1)} %north.145), channel_id=1, source_target_pairs={{0,1},{1,2},{2,3},{3,4},{4,5},{5,6},{6,7},{16,17},{17,18},{18,19},... | collective-permute-start | bytes 294920 | tf_op jit(solution)/shard_map/while/body/eval_jaxpr/ppermute | solution.py:204
  36.0 15.0 %collective-permute-start.1 = (f32[32,768]{1,0:T(8,128)S(1)}, f32[32,768]{1,0:T(8,128)S(1)}, u32[]{:S(2)}, u32[]{:S(2)}) collective-permute-start(f32[32,768]{1,0:T(8,128)S(1)} %north.144), channel_id=1, source_target_pairs={{8,9},{9,10},{10,11},{11,12},{12,13},{13,14},{14,15},{24,25},{25,2... | collective-permute-start | bytes 294920 | tf_op jit(solution)/shard_map/while/body/eval_jaxpr/ppermute | solution.py:204
  51.7 15.3 %collective-permute-start.5 = (f32[32,768]{1,0:T(8,128)S(1)}, f32[32,768]{1,0:T(8,128)S(1)}, u32[]{:S(2)}, u32[]{:S(2)}) collective-permute-start(f32[32,768]{1,0:T(8,128)S(1)} %north.146), channel_id=1, source_target_pairs={{8,9},{9,10},{10,11},{11,12},{12,13},{13,14},{14,15},{24,25},{25,2... | collective-permute-start | bytes 294920 | tf_op jit(solution)/shard_map/while/body/eval_jaxpr/ppermute | solution.py:204
  67.8 12.2 %collective-permute-start.9 = (f32[32,768]{1,0:T(8,128)S(1)}, f32[32,768]{1,0:T(8,128)S(1)}, u32[]{:S(2)}, u32[]{:S(2)}) collective-permute-start(f32[32,768]{1,0:T(8,128)S(1)} %north.148), channel_id=1, source_target_pairs={{8,9},{9,10},{10,11},{11,12},{12,13},{13,14},{14,15},{24,25},{25,2... | collective-permute-start | bytes 294920 | tf_op jit(solution)/shard_map/while/body/eval_jaxpr/ppermute | solution.py:204
  80.6 12.4 %collective-permute-start.13 = (f32[32,768]{1,0:T(8,128)S(1)}, f32[32,768]{1,0:T(8,128)S(1)}, u32[]{:S(2)}, u32[]{:S(2)}) collective-permute-start(f32[32,768]{1,0:T(8,128)S(1)} %north.150), channel_id=1, source_target_pairs={{8,9},{9,10},{10,11},{11,12},{12,13},{13,14},{14,15},{24,25},{25,2... | collective-permute-start | bytes 294920 | tf_op jit(solution)/shard_map/while/body/eval_jaxpr/ppermute | solution.py:204
  93.8 12.4 %collective-permute-start.17 = (f32[32,768]{1,0:T(8,128)S(1)}, f32[32,768]{1,0:T(8,128)S(1)}, u32[]{:S(2)}, u32[]{:S(2)}) collective-permute-start(f32[32,768]{1,0:T(8,128)S(1)} %north.152), channel_id=1, source_target_pairs={{8,9},{9,10},{10,11},{11,12},{12,13},{13,14},{14,15},{24,25},{25,2... | collective-permute-start | bytes 294920 | tf_op jit(solution)/shard_map/while/body/eval_jaxpr/ppermute | solution.py:204
  106.9 13.9 %collective-permute-start.21 = (f32[32,768]{1,0:T(8,128)S(1)}, f32[32,768]{1,0:T(8,128)S(1)}, u32[]{:S(2)}, u32[]{:S(2)}) collective-permute-start(f32[32,768]{1,0:T(8,128)S(1)} %north.154), channel_id=1, source_target_pairs={{8,9},{9,10},{10,11},{11,12},{12,13},{13,14},{14,15},{24,25},{25,2... | collective-permute-start | bytes 294920 | tf_op jit(solution)/shard_map/while/body/eval_jaxpr/ppermute | solution.py:204
  121.5 13.3 %collective-permute-start.25 = (f32[32,768]{1,0:T(8,128)S(1)}, f32[32,768]{1,0:T(8,128)S(1)}, u32[]{:S(2)}, u32[]{:S(2)}) collective-permute-start(f32[32,768]{1,0:T(8,128)S(1)} %north.156), channel_id=1, source_target_pairs={{8,9},{9,10},{10,11},{11,12},{12,13},{13,14},{14,15},{24,25},{25,2... | collective-permute-start | bytes 294920 | tf_op jit(solution)/shard_map/while/body/eval_jaxpr/ppermute | solution.py:204
  143.6 17.4 %collective-permute-start = (f32[32,768]{1,0:T(8,128)S(1)}, f32[32,768]{1,0:T(8,128)S(1)}, u32[]{:S(2)}, u32[]{:S(2)}) collective-permute-start(f32[32,768]{1,0:T(8,128)S(1)} %east.16.refs_0_), channel_id=1, source_target_pairs={{0,8},{1,9},{2,10},{3,11},{4,12},{5,13},{6,14},{7,15},{16,24},{17,... | collective-permute-start | bytes 294920 | tf_op jit(solution)/shard_map/while/body/eval_jaxpr/ppermute | solution.py:198
  150.3 15.8 %collective-permute-start.2 = (f32[32,768]{1,0:T(8,128)S(1)}, f32[32,768]{1,0:T(8,128)S(1)}, u32[]{:S(2)}, u32[]{:S(2)}) collective-permute-start(f32[32,768]{1,0:T(8,128)S(1)} %north.145), channel_id=1, source_target_pairs={{0,1},{1,2},{2,3},{3,4},{4,5},{5,6},{6,7},{16,17},{17,18},{18,19},... | collective-permute-start | bytes 294920 | tf_op jit(solution)/shard_map/while/body/eval_jaxpr/ppermute | solution.py:204
  164.0 13.1 %collective-permute-start.1 = (f32[32,768]{1,0:T(8,128)S(1)}, f32[32,768]{1,0:T(8,128)S(1)}, u32[]{:S(2)}, u32[]{:S(2)}) collective-permute-start(f32[32,768]{1,0:T(8,128)S(1)} %north.144), channel_id=1, source_target_pairs={{8,9},{9,10},{10,11},{11,12},{12,13},{13,14},{14,15},{24,25},{25,2... | collective-permute-start | bytes 294920 | tf_op jit(solution)/shard_map/while/body/eval_jaxpr/ppermute | solution.py:204
  177.9 13.5 %collective-permute-start.5 = (f32[32,768]{1,0:T(8,128)S(1)}, f32[32,768]{1,0:T(8,128)S(1)}, u32[]{:S(2)}, u32[]{:S(2)}) collective-permute-start(f32[32,768]{1,0:T(8,128)S(1)} %north.146), channel_id=1, source_target_pairs={{8,9},{9,10},{10,11},{11,12},{12,13},{13,14},{14,15},{24,25},{25,2... | collective-permute-start | bytes 294920 | tf_op jit(solution)/shard_map/while/body/eval_jaxpr/ppermute | solution.py:204
  192.1 13.5 %collective-permute-start.9 = (f32[32,768]{1,0:T(8,128)S(1)}, f32[32,768]{1,0:T(8,128)S(1)}, u32[]{:S(2)}, u32[]{:S(2)}) collective-permute-start(f32[32,768]{1,0:T(8,128)S(1)} %north.148), channel_id=1, source_target_pairs={{8,9},{9,10},{10,11},{11,12},{12,13},{13,14},{14,15},{24,25},{25,2... | collective-permute-start | bytes 294920 | tf_op jit(solution)/shard_map/while/body/eval_jaxpr/ppermute | solution.py:204
  219.0 12.1 %collective-permute-start.17 = (f32[32,768]{1,0:T(8,128)S(1)}, f32[32,768]{1,0:T(8,128)S(1)}, u32[]{:S(2)}, u32[]{:S(2)}) collective-permute-start(f32[32,768]{1,0:T(8,128)S(1)} %north.152), channel_id=1, source_target_pairs={{8,9},{9,10},{10,11},{11,12},{12,13},{13,14},{14,15},{24,25},{25,2... | collective-permute-start | bytes 294920 | tf_op jit(solution)/shard_map/while/body/eval_jaxpr/ppermute | solution.py:204
  231.8 13.0 %collective-permute-start.21 = (f32[32,768]{1,0:T(8,128)S(1)}, f32[32,768]{1,0:T(8,128)S(1)}, u32[]{:S(2)}, u32[]{:S(2)}) collective-permute-start(f32[32,768]{1,0:T(8,128)S(1)} %north.154), channel_id=1, source_target_pairs={{8,9},{9,10},{10,11},{11,12},{12,13},{13,14},{14,15},{24,25},{25,2... | collective-permute-start | bytes 294920 | tf_op jit(solution)/shard_map/while/body/eval_jaxpr/ppermute | solution.py:204
  245.4 13.0 %collective-permute-start.25 = (f32[32,768]{1,0:T(8,128)S(1)}, f32[32,768]{1,0:T(8,128)S(1)}, u32[]{:S(2)}, u32[]{:S(2)}) collective-permute-start(f32[32,768]{1,0:T(8,128)S(1)} %north.156), channel_id=1, source_target_pairs={{8,9},{9,10},{10,11},{11,12},{12,13},{13,14},{14,15},{24,25},{25,2... | collective-permute-start | bytes 294920 | tf_op jit(solution)/shard_map/while/body/eval_jaxpr/ppermute | solution.py:204
  265.8 18.4 %collective-permute-start = (f32[32,768]{1,0:T(8,128)S(1)}, f32[32,768]{1,0:T(8,128)S(1)}, u32[]{:S(2)}, u32[]{:S(2)}) collective-permute-start(f32[32,768]{1,0:T(8,128)S(1)} %east.16.refs_0_), channel_id=1, source_target_pairs={{0,8},{1,9},{2,10},{3,11},{4,12},{5,13},{6,14},{7,15},{16,24},{17,... | collective-permute-start | bytes 294920 | tf_op jit(solution)/shard_map/while/body/eval_jaxpr/ppermute | solution.py:198
  273.6 15.8 %collective-permute-start.2 = (f32[32,768]{1,0:T(8,128)S(1)}, f32[32,768]{1,0:T(8,128)S(1)}, u32[]{:S(2)}, u32[]{:S(2)}) collective-permute-start(f32[32,768]{1,0:T(8,128)S(1)} %north.145), channel_id=1, source_target_pairs={{0,1},{1,2},{2,3},{3,4},{4,5},{5,6},{6,7},{16,17},{17,18},{18,19},... | collective-permute-start | bytes 294920 | tf_op jit(solution)/shard_map/while/body/eval_jaxpr/ppermute | solution.py:204
  287.2 13.2 %collective-permute-start.1 = (f32[32,768]{1,0:T(8,128)S(1)}, f32[32,768]{1,0:T(8,128)S(1)}, u32[]{:S(2)}, u32[]{:S(2)}) collective-permute-start(f32[32,768]{1,0:T(8,128)S(1)} %north.144), channel_id=1, source_target_pairs={{8,9},{9,10},{10,11},{11,12},{12,13},{13,14},{14,15},{24,25},{25,2... | collective-permute-start | bytes 294920 | tf_op jit(solution)/shard_map/while/body/eval_jaxpr/ppermute | solution.py:204
  301.1 13.0 %collective-permute-start.5 = (f32[32,768]{1,0:T(8,128)S(1)}, f32[32,768]{1,0:T(8,128)S(1)}, u32[]{:S(2)}, u32[]{:S(2)}) collective-permute-start(f32[32,768]{1,0:T(8,128)S(1)} %north.146), channel_id=1, source_target_pairs={{8,9},{9,10},{10,11},{11,12},{12,13},{13,14},{14,15},{24,25},{25,2... | collective-permute-start | bytes 294920 | tf_op jit(solution)/shard_map/while/body/eval_jaxpr/ppermute | solution.py:204
  314.8 13.0 %collective-permute-start.9 = (f32[32,768]{1,0:T(8,128)S(1)}, f32[32,768]{1,0:T(8,128)S(1)}, u32[]{:S(2)}, u32[]{:S(2)}) collective-permute-start(f32[32,768]{1,0:T(8,128)S(1)} %north.148), channel_id=1, source_target_pairs={{8,9},{9,10},{10,11},{11,12},{12,13},{13,14},{14,15},{24,25},{25,2... | collective-permute-start | bytes 294920 | tf_op jit(solution)/shard_map/while/body/eval_jaxpr/ppermute | solution.py:204
  353.3 12.9 %collective-permute-start.21 = (f32[32,768]{1,0:T(8,128)S(1)}, f32[32,768]{1,0:T(8,128)S(1)}, u32[]{:S(2)}, u32[]{:S(2)}) collective-permute-start(f32[32,768]{1,0:T(8,128)S(1)} %north.154), channel_id=1, source_target_pairs={{8,9},{9,10},{10,11},{11,12},{12,13},{13,14},{14,15},{24,25},{25,2... | collective-permute-start | bytes 294920 | tf_op jit(solution)/shard_map/while/body/eval_jaxpr/ppermute | solution.py:204
  366.8 12.5 %collective-permute-start.25 = (f32[32,768]{1,0:T(8,128)S(1)}, f32[32,768]{1,0:T(8,128)S(1)}, u32[]{:S(2)}, u32[]{:S(2)}) collective-permute-start(f32[32,768]{1,0:T(8,128)S(1)} %north.156), channel_id=1, source_target_pairs={{8,9},{9,10},{10,11},{11,12},{12,13},{13,14},{14,15},{24,25},{25,2... | collective-permute-start | bytes 294920 | tf_op jit(solution)/shard_map/while/body/eval_jaxpr/ppermute | solution.py:204
  386.7 17.9 %collective-permute-start = (f32[32,768]{1,0:T(8,128)S(1)}, f32[32,768]{1,0:T(8,128)S(1)}, u32[]{:S(2)}, u32[]{:S(2)}) collective-permute-start(f32[32,768]{1,0:T(8,128)S(1)} %east.16.refs_0_), channel_id=1, source_target_pairs={{0,8},{1,9},{2,10},{3,11},{4,12},{5,13},{6,14},{7,15},{16,24},{17,... | collective-permute-start | bytes 294920 | tf_op jit(solution)/shard_map/while/body/eval_jaxpr/ppermute | solution.py:198
  393.9 15.8 %collective-permute-start.2 = (f32[32,768]{1,0:T(8,128)S(1)}, f32[32,768]{1,0:T(8,128)S(1)}, u32[]{:S(2)}, u32[]{:S(2)}) collective-permute-start(f32[32,768]{1,0:T(8,128)S(1)} %north.145), channel_id=1, source_target_pairs={{0,1},{1,2},{2,3},{3,4},{4,5},{5,6},{6,7},{16,17},{17,18},{18,19},... | collective-permute-start | bytes 294920 | tf_op jit(solution)/shard_map/while/body/eval_jaxpr/ppermute | solution.py:204
  407.6 13.0 %collective-permute-start.1 = (f32[32,768]{1,0:T(8,128)S(1)}, f32[32,768]{1,0:T(8,128)S(1)}, u32[]{:S(2)}, u32[]{:S(2)}) collective-permute-start(f32[32,768]{1,0:T(8,128)S(1)} %north.144), channel_id=1, source_target_pairs={{8,9},{9,10},{10,11},{11,12},{12,13},{13,14},{14,15},{24,25},{25,2... | collective-permute-start | bytes 294920 | tf_op jit(solution)/shard_map/while/body/eval_jaxpr/ppermute | solution.py:204
  421.4 12.5 %collective-permute-start.5 = (f32[32,768]{1,0:T(8,128)S(1)}, f32[32,768]{1,0:T(8,128)S(1)}, u32[]{:S(2)}, u32[]{:S(2)}) collective-permute-start(f32[32,768]{1,0:T(8,128)S(1)} %north.146), channel_id=1, source_target_pairs={{8,9},{9,10},{10,11},{11,12},{12,13},{13,14},{14,15},{24,25},{25,2... | collective-permute-start | bytes 294920 | tf_op jit(solution)/shard_map/while/body/eval_jaxpr/ppermute | solution.py:204
  434.6 12.5 %collective-permute-start.9 = (f32[32,768]{1,0:T(8,128)S(1)}, f32[32,768]{1,0:T(8,128)S(1)}, u32[]{:S(2)}, u32[]{:S(2)}) collective-permute-start(f32[32,768]{1,0:T(8,128)S(1)} %north.148), channel_id=1, source_target_pairs={{8,9},{9,10},{10,11},{11,12},{12,13},{13,14},{14,15},{24,25},{25,2... | collective-permute-start | bytes 294920 | tf_op jit(solution)/shard_map/while/body/eval_jaxpr/ppermute | solution.py:204
  460.0 12.2 %collective-permute-start.17 = (f32[32,768]{1,0:T(8,128)S(1)}, f32[32,768]{1,0:T(8,128)S(1)}, u32[]{:S(2)}, u32[]{:S(2)}) collective-permute-start(f32[32,768]{1,0:T(8,128)S(1)} %north.152), channel_id=1, source_target_pairs={{8,9},{9,10},{10,11},{11,12},{12,13},{13,14},{14,15},{24,25},{25,2... | collective-permute-start | bytes 294920 | tf_op jit(solution)/shard_map/while/body/eval_jaxpr/ppermute | solution.py:204
  472.9 12.5 %collective-permute-start.21 = (f32[32,768]{1,0:T(8,128)S(1)}, f32[32,768]{1,0:T(8,128)S(1)}, u32[]{:S(2)}, u32[]{:S(2)}) collective-permute-start(f32[32,768]{1,0:T(8,128)S(1)} %north.154), channel_id=1, source_target_pairs={{8,9},{9,10},{10,11},{11,12},{12,13},{13,14},{14,15},{24,25},{25,2... | collective-permute-start | bytes 294920 | tf_op jit(solution)/shard_map/while/body/eval_jaxpr/ppermute | solution.py:204
  486.1 12.5 %collective-permute-start.25 = (f32[32,768]{1,0:T(8,128)S(1)}, f32[32,768]{1,0:T(8,128)S(1)}, u32[]{:S(2)}, u32[]{:S(2)}) collective-permute-start(f32[32,768]{1,0:T(8,128)S(1)} %north.156), channel_id=1, source_target_pairs={{8,9},{9,10},{10,11},{11,12},{12,13},{13,14},{14,15},{24,25},{25,2... | collective-permute-start | bytes 294920 | tf_op jit(solution)/shard_map/while/body/eval_jaxpr/ppermute | solution.py:204
  (134 other events, 734.7 us)

commit v2 on v1

v2 whole, which is shorter than its diff:
```python
import functools

import jax
import jax.numpy as jnp
from jax import lax
from jax.experimental import pallas as pl
from jax.experimental.pallas import tpu as pltpu
from jax.sharding import PartitionSpec as P

PIECES = 2
UNROLL = 7
Z = 8
LIMIT = 8
VMEM = pl.BlockSpec(memory_space=pltpu.VMEM)
SMEM = pl.BlockSpec(memory_space=pltpu.SMEM)
HBM = pl.BlockSpec(memory_space=pltpu.HBM)
ANY = pl.BlockSpec(memory_space=pl.ANY)
F32 = jnp.float32
BF16 = jnp.bfloat16


def halves(value):
    high = value.astype(BF16)
    low = (value - high.astype(F32)).astype(BF16)
    return high, low


def product(value, high_ref, low_ref):
    rows = value.shape[0]
    high, low = halves(value)
    both = jnp.concatenate([high, low], axis=0)
    main = jnp.dot(both, high_ref[...], preferred_element_type=F32)
    rest = jnp.dot(high, low_ref[...], preferred_element_type=F32)
    return main[:rows] + (main[rows:] + rest)


def pass_through_kernel(*refs):
    del refs


def pass_through(*arrays):
    return pl.pallas_call(
        pass_through_kernel,
        out_shape=tuple(jax.ShapeDtypeStruct(a.shape, a.dtype) for a in arrays),
        in_specs=[ANY] * len(arrays),
        out_specs=(ANY,) * len(arrays),
        input_output_aliases={i: i for i in range(len(arrays))},
        compiler_params=params(4),
        name="pass_through",
    )(*arrays)


def params(mib):
    return pltpu.CompilerParams(vmem_limit_bytes=mib << 20)


def split_kernel(chunk, w_hbm, *refs):
    quarters, (buf, sem) = refs[:8], refs[8:]
    half = w_hbm.shape[0] // 2
    count = 2 * half // chunk

    def fetch(i):
        return pltpu.make_async_copy(
            w_hbm.at[pl.ds(i * chunk, chunk)], buf.at[i % 2], sem.at[i % 2]
        )

    fetch(0).start()
    for i in range(count):
        if i + 1 < count:
            fetch(i + 1).start()
        fetch(i).wait()
        high, low = halves(buf[i % 2])
        side, at = divmod(i * chunk, half)
        for j in range(2):
            cols = slice(j * half, (j + 1) * half)
            quarters[4 * side + 2 * j][at : at + chunk, :] = high[:, cols]
            quarters[4 * side + 2 * j + 1][at : at + chunk, :] = low[:, cols]


def split_operator(w):
    order = w.shape[0]
    half = order // 2
    chunk = half // 3
    shape = jax.ShapeDtypeStruct((half, half), BF16)
    return pl.pallas_call(
        functools.partial(split_kernel, chunk),
        out_shape=(shape,) * 8,
        in_specs=[HBM],
        out_specs=(VMEM,) * 8,
        scratch_shapes=[
            pltpu.VMEM((2, chunk, order), F32),
            pltpu.SemaphoreType.DMA((2,)),
        ],
        compiler_params=params(16),
        name="split_operator",
    )(w)


def when_active(offset, count, age_ref):
    age = age_ref[0] + offset
    piece = lax.div(age, 2)
    return (age >= 0) & (age < 2 * count) & (age == 2 * piece), piece


def south_kernel(offset, count, age_ref, placed_ref, south_ref, eh_ref, el_ref, nh_ref, nl_ref, out_ref):
    active, piece = when_active(offset, count, age_ref)
    half = south_ref.shape[1]

    @pl.when(active)
    def _():
        south = south_ref[...]
        out_ref[:, :half] = placed_ref[piece, :, :half] + product(south, eh_ref, el_ref)
        out_ref[:, half:] = placed_ref[piece, :, half:] + product(south, nh_ref, nl_ref)


def chosen(age_ref, west_refs):
    if len(west_refs) == 1:
        return west_refs[0][...]
    return jnp.where(age_ref[1] > 0, west_refs[1][...], west_refs[0][...])


def east_kernel(offset, count, wests, age_ref, partial_ref, high_ref, low_ref, *refs):
    active, _ = when_active(offset, count, age_ref)
    west_refs, (out_ref,) = refs[:wests], refs[wests:]
    half = out_ref.shape[1]

    @pl.when(active)
    def _():
        west = chosen(age_ref, west_refs)
        out_ref[...] = partial_ref[:, :half] + product(west, high_ref, low_ref)


def north_kernel(offset, count, wests, age_ref, partial_ref, high_ref, low_ref, *refs):
    west_refs, (east_ref, _, out_ref, results_ref) = refs[:wests], refs[wests:]
    active, piece = when_active(offset, count, age_ref)
    half = out_ref.shape[1]

    @pl.when(active)
    def _():
        west = chosen(age_ref, west_refs)
        value = partial_ref[:, half:] + product(west, high_ref, low_ref)
        out_ref[...] = value
        results_ref[piece, :, :half] = east_ref[...]
        results_ref[piece, :, half:] = value


def estimate(width, half, quarters):
    return pl.CostEstimate(
        flops=6 * quarters * width * half * half,
        bytes_accessed=1 << 20,
        transcendentals=0,
    )


def south_part(offset, count, age, placed, south, weights):
    _, width, order = placed.shape
    return pl.pallas_call(
        functools.partial(south_kernel, offset, count),
        out_shape=jax.ShapeDtypeStruct((width, order), F32),
        in_specs=[SMEM] + [VMEM] * 6,
        out_specs=VMEM,
        compiler_params=params(LIMIT),
        cost_estimate=estimate(width, order // 2, 2),
        name="south",
    )(age, placed, south, *weights)


def east_part(offset, count, age, partial, wests, weights):
    width, half = wests[0].shape
    return pl.pallas_call(
        functools.partial(east_kernel, offset, count, len(wests)),
        out_shape=jax.ShapeDtypeStruct((width, half), F32),
        in_specs=[SMEM] + [VMEM] * (3 + len(wests)),
        out_specs=VMEM,
        compiler_params=params(LIMIT),
        cost_estimate=estimate(width, half, 1),
        name="east",
    )(age, partial, *weights, *wests)


def north_part(offset, count, age, partial, wests, weights, east, results):
    width, half = wests[0].shape
    return pl.pallas_call(
        functools.partial(north_kernel, offset, count, len(wests)),
        out_shape=(
            jax.ShapeDtypeStruct((width, half), F32),
            jax.ShapeDtypeStruct(results.shape, F32),
        ),
        in_specs=[SMEM] + [VMEM] * (5 + len(wests)),
        out_specs=(VMEM, VMEM),
        input_output_aliases={5 + len(wests): 1},
        compiler_params=params(LIMIT),
        cost_estimate=estimate(width, half, 1),
        name="north",
    )(age, partial, *weights, *wests, east, results)


def summed(value, shape):
    for axis, size in (("gy", shape[1]), ("gx", shape[0])):
        apart = 1
        while apart < size:
            pairs = [(i, i ^ apart) for i in range(size)]
            value = value + lax.ppermute(value, axis, pairs)
            apart *= 2
    return value


def place_kernel(plan_ref, rows_ref, sources_ref, out_ref):
    batches, columns, placed_count = sources_ref.shape
    order = out_ref.shape[-1]
    at = lax.broadcasted_iota(jnp.int32, (order, placed_count), 0)
    placing = jnp.where(at == rows_ref[...], 1.0, 0.0).astype(BF16)
    for b in range(batches):
        source = sources_ref[plan_ref[b]]
        high, middle = halves(source)
        low = (source - high.astype(F32) - middle.astype(F32)).astype(BF16)
        parts = jnp.concatenate([high, middle, low], axis=0)
        spread = lax.dot_general(
            parts, placing, (((1,), (1,)), ((), ())), preferred_element_type=F32
        )
        out_ref[b] = spread[:columns] + (
            spread[columns : 2 * columns] + spread[2 * columns :]
        )


def place(plan, rows, sources, order):
    batches, columns, _ = sources.shape
    return pl.pallas_call(
        place_kernel,
        out_shape=jax.ShapeDtypeStruct((batches, columns, order), F32),
        in_specs=[SMEM, VMEM, VMEM],
        out_specs=VMEM,
        compiler_params=params(8),
        name="place",
    )(plan, rows, sources)


def east_pairs(shape, parity, far):
    nx, ny = shape
    return [
        (x * ny + y, (x + 1) * ny + y)
        for x in range(parity, nx - 1, 2)
        for y in range(ny)
        if ((x + 1) % Z == 0) == far
    ]


def north_pairs(shape, parity):
    nx, ny = shape
    return [
        (x * ny + y, x * ny + y + 1) for x in range(parity, nx, 2) for y in range(ny - 1)
    ]


def body(shape, operators, sources, source_rows, batch_plan):
    nx, ny = shape
    axes = ("gx", "gy")
    column = lax.axis_index("gx")
    depth = column + 2 * lax.div(column, Z) + 2 * lax.axis_index("gy")
    starts_row = (lax.rem(column, Z) == 0).astype(jnp.int32)
    order = operators.shape[-1]
    half = order // 2
    _, _, batches, columns, placed_count = sources.shape
    width = columns // PIECES
    count = batches * PIECES
    placed = place(batch_plan, source_rows[0], sources[0, 0], order)
    placed = placed.reshape(count, width, order)
    quarters = split_operator(operators[0, 0])

    deepest = nx - 1 + 2 * ((nx - 1) // Z) + 2 * (ny - 1)
    steps = (deepest + 2 * (count - 1)) // 2 + 1
    trips = -(-steps // UNROLL)

    def advance(trip, carry):
        even_west, odd_west, far_old, far_new, south, results, fixed = carry
        south = list(south)
        fixed = pass_through(*fixed)
        placed, quarters = fixed[0], fixed[1:]
        age = trip * (2 * UNROLL) - depth
        age_ref = jnp.stack([age, starts_row]).astype(jnp.int32)
        for offset in range(2 * UNROLL):
            parity = offset % 2
            wests = (odd_west,) if parity else (even_west, far_old)
            partial = south_part(
                offset, count, age_ref, placed, south[parity], quarters[4:]
            )
            to_east = east_part(offset, count, age_ref, partial, wests, quarters[:2])
            arrived = lax.ppermute(to_east, axes, east_pairs(shape, parity, False))
            to_north, results = north_part(
                offset, count, age_ref, partial, wests, quarters[2:4], to_east, results
            )
            south[parity] = lax.ppermute(to_north, axes, north_pairs(shape, parity))
            if parity:
                even_west = arrived
                far_old, far_new = far_new, lax.ppermute(
                    to_east, axes, east_pairs(shape, parity, True)
                )
            else:
                odd_west = arrived
        return (even_west, odd_west, far_old, far_new, tuple(south), results, tuple(fixed))

    zero = jnp.zeros((width, half), F32)
    results = jnp.zeros((count, width, order), F32)
    carry = (zero, zero, zero, zero, (zero, zero), results, (placed, *quarters))
    results = lax.fori_loop(0, trips, advance, carry)[5]
    first = results[:PIECES].reshape(columns, order)
    rest = results[PIECES:]
    partial_gram = lax.dot_general(
        first,
        first,
        (((1,), (1,)), ((), ())),
        precision=lax.Precision.HIGHEST,
        preferred_element_type=F32,
    )
    gram = summed(partial_gram, shape) / (nx * ny * order)
    lower = jnp.linalg.cholesky(gram)
    basis = jax.scipy.linalg.solve_triangular(lower, first, lower=True)
    traces = rest.reshape(batches - 1, columns, order)
    return (traces[None, None], basis[None, None], lower.T)


def solution(mesh):
    return jax.shard_map(
        functools.partial(body, (mesh.shape["gx"], mesh.shape["gy"])),
        mesh=mesh,
        in_specs=(
            P("gx", "gy", None, None),
            P("gx", "gy", None, None, None),
            P("gx", "gy", None),
            P(),
        ),
        out_specs=(P("gx", "gy", None, None, None), P("gx", "gy", None, None), P()),
        check_vma=False,
    )
```

time: 603 us -> 625 us (1.036); the launches traced: 600 us -> 615 us
  Pallas kernels: 23.1 us -> 162 us
  local copies, waits for them, and re-layouts: 144 us -> 13.9 us
  blocking collectives: 79.7 us -> 0 us
  starting transfers between devices: 335 us -> 403 us
  waiting for transfers between devices: 0.48 us -> 16.4 us
    pallas_call x130 -> x147, Pallas kernels: 14.2 us -> 103 us  [the longest x70 48.4 us: north_part(): pl.pallas_call(functools.partial(north_kernel, offset, count, len(wests))...]
    dynamic_update_slice x128 -> x0, local copies, waits for them, and re-layouts: 83.9 us -> none  [the longest x64 42.2 us: advance(): results = lax.dynamic_update_slice(results, to_north[None], (slot, 0, half))]
    psum x1 -> x0, blocking collectives: 79.7 us -> none  [body(): gram = lax.psum(partial_gram, axes) / (nx * ny * order)]
    ppermute x128 -> x183, starting transfers between devices: 335 us -> 403 us  [the longest x70 243 us: advance(): arrived = lax.ppermute(to_east, axes, east_pairs(shape, parity, False))]
    pallas_call x64 -> x70, Pallas kernels: 8.95 us -> 59.2 us  [south_part(): pl.pallas_call(functools.partial(south_kernel, offset, count), out_shape=...]
    while x64 -> x90, local copies, waits for them, and re-layouts: 46.1 us -> 2.26 us
    ppermute x128 -> x183, waiting for transfers between devices: 0.48 us -> 16.4 us  [the longest x8 15.9 us: summed(): value = value + lax.ppermute(value, axis, pairs)]
  transfers between devices with their start and end apart: 128 -> 183, of which waited for: 0 -> 8; matrix products, arithmetic and copies ran while one was open for 14% -> 0% of each run, Pallas kernels for 3% -> 22%
where the time goes in v2:
time: 625 us; the launch traced here: 615 us
  starting transfers between devices  403 us (64%)
  Pallas kernels  162 us (26%)
  waiting for transfers between devices  16.4 us (3%)
  local copies, waits for them, and re-layouts  13.9 us (2%)
  other arithmetic  12.5 us (2%)
    ppermute x70, starting transfers between devices, advance(): arrived = lax.ppermute(to_east, axes, east_pairs(shape, parity, False))  243 us
    ppermute x70, starting transfers between devices, advance(): south[parity] = lax.ppermute(to_north, axes, north_pairs(shape, parity))  111 us
    pallas_call x70, Pallas kernels, south_part(): pl.pallas_call(functools.partial(south_kernel, offset, count), out_shape=...  59.2 us
    pallas_call x70, Pallas kernels, north_part(): pl.pallas_call(functools.partial(north_kernel, offset, count, len(wests))...  48.4 us
    pallas_call x70, Pallas kernels, east_part(): pl.pallas_call(functools.partial(east_kernel, offset, count, len(wests)),...  48.1 us
    ppermute x35, starting transfers between devices, advance(): lax.ppermute(to_east, axes, east_pairs(shape, parity, True))  29.6 us
    ppermute x8, starting transfers between devices, summed(): value = value + lax.ppermute(value, axis, pairs)  18.1 us
    ppermute x8, waiting for transfers between devices, summed(): value = value + lax.ppermute(value, axis, pairs)  15.9 us
  transfers between devices with their start and end apart: 183, of which 8 were waited for; matrix products, arithmetic and copies ran while one was open for 0% of the time, Pallas kernels for 22%

profile of v2, /device:TPU:1, one launch (start us, length us, event | category | flops | bytes accessed | tf_op | source)
XLA Modules:
  0.0 615.1 jit_solution(5040052053990946592)
XLA Ops:
  15.6 548.3 %while.41 = (s32[]{:T(128)}, f32[32,768]{1,0:T(8,128)}, f32[32,768]{1,0:T(8,128)}, f32[32,768]{1,0:T(8,128)}, f32[32,768]{1,0:T(8,128)}, /*index=5*/f32[32,768]{...) while((s32[]{:T(128)}, f32[32,768]{1,0:T(8,128)}, ...), condition=%wide.region_1.0_spmd, body=%wide.region_0.0_spmd.sunk | while | flops 6341787648 | bytes 106563408 | solution.py:305
  35.9 6.6 %collective-permute-start.4 = (f32[32,768]{1,0:T(8,128)S(1)}, f32[32,768]{1,0:T(8,128)S(1)}, u32[]{:S(2)}, u32[]{:S(2)}) collective-permute-start(f32[32,768]{1,0:T(8,128)S(1)} %east.16.refs_2_), channel_id=1, source_target_pairs={{0,8},{1,9},{2,10},{3,11},{4,12},{5,13},{6,14},{7,15},{16,24},{17,... | collective-permute-start | bytes 294920 | tf_op jit(solution)/shard_map/while/body/eval_jaxpr/ppermute | solution.py:288
  53.1 7.1 %collective-permute-start.9 = (f32[32,768]{1,0:T(8,128)S(1)}, f32[32,768]{1,0:T(8,128)S(1)}, u32[]{:S(2)}, u32[]{:S(2)}) collective-permute-start(f32[32,768]{1,0:T(8,128)S(1)} %east.18.refs_2_), channel_id=1, source_target_pairs={{0,8},{1,9},{2,10},{3,11},{4,12},{5,13},{6,14},{7,15},{16,24},{17,... | collective-permute-start | bytes 294920 | tf_op jit(solution)/shard_map/while/body/eval_jaxpr/ppermute | solution.py:288
  114.5 5.5 collective-permute-start.29
  151.2 6.0 collective-permute-start.4
  167.1 6.6 %collective-permute-start.9 = (f32[32,768]{1,0:T(8,128)S(1)}, f32[32,768]{1,0:T(8,128)S(1)}, u32[]{:S(2)}, u32[]{:S(2)}) collective-permute-start(f32[32,768]{1,0:T(8,128)S(1)} %east.18.refs_2_), channel_id=1, source_target_pairs={{0,8},{1,9},{2,10},{3,11},{4,12},{5,13},{6,14},{7,15},{16,24},{17,... | collective-permute-start | bytes 294920 | tf_op jit(solution)/shard_map/while/body/eval_jaxpr/ppermute | solution.py:288
  183.1 5.4 collective-permute-start.14
  196.7 6.7 %collective-permute-start.19 = (f32[32,768]{1,0:T(8,128)S(1)}, f32[32,768]{1,0:T(8,128)S(1)}, u32[]{:S(2)}, u32[]{:S(2)}) collective-permute-start(f32[32,768]{1,0:T(8,128)S(1)} %east.22.refs_2_), channel_id=1, source_target_pairs={{0,8},{1,9},{2,10},{3,11},{4,12},{5,13},{6,14},{7,15},{16,24},{17,... | collective-permute-start | bytes 294920 | tf_op jit(solution)/shard_map/while/body/eval_jaxpr/ppermute | solution.py:288
  211.5 6.7 %collective-permute-start.24 = (f32[32,768]{1,0:T(8,128)S(1)}, f32[32,768]{1,0:T(8,128)S(1)}, u32[]{:S(2)}, u32[]{:S(2)}) collective-permute-start(f32[32,768]{1,0:T(8,128)S(1)} %east.24.refs_2_), channel_id=1, source_target_pairs={{0,8},{1,9},{2,10},{3,11},{4,12},{5,13},{6,14},{7,15},{16,24},{17,... | collective-permute-start | bytes 294920 | tf_op jit(solution)/shard_map/while/body/eval_jaxpr/ppermute | solution.py:288
  225.9 6.7 %collective-permute-start.29 = (f32[32,768]{1,0:T(8,128)S(1)}, f32[32,768]{1,0:T(8,128)S(1)}, u32[]{:S(2)}, u32[]{:S(2)}) collective-permute-start(f32[32,768]{1,0:T(8,128)S(1)} %east.26.refs_2_), channel_id=1, source_target_pairs={{0,8},{1,9},{2,10},{3,11},{4,12},{5,13},{6,14},{7,15},{16,24},{17,... | collective-permute-start | bytes 294920 | tf_op jit(solution)/shard_map/while/body/eval_jaxpr/ppermute | solution.py:288
  246.6 6.1 collective-permute-start
  262.1 6.7 %collective-permute-start.4 = (f32[32,768]{1,0:T(8,128)S(1)}, f32[32,768]{1,0:T(8,128)S(1)}, u32[]{:S(2)}, u32[]{:S(2)}) collective-permute-start(f32[32,768]{1,0:T(8,128)S(1)} %east.16.refs_2_), channel_id=1, source_target_pairs={{0,8},{1,9},{2,10},{3,11},{4,12},{5,13},{6,14},{7,15},{16,24},{17,... | collective-permute-start | bytes 294920 | tf_op jit(solution)/shard_map/while/body/eval_jaxpr/ppermute | solution.py:288
  276.8 7.2 %collective-permute-start.9 = (f32[32,768]{1,0:T(8,128)S(1)}, f32[32,768]{1,0:T(8,128)S(1)}, u32[]{:S(2)}, u32[]{:S(2)}) collective-permute-start(f32[32,768]{1,0:T(8,128)S(1)} %east.18.refs_2_), channel_id=1, source_target_pairs={{0,8},{1,9},{2,10},{3,11},{4,12},{5,13},{6,14},{7,15},{16,24},{17,... | collective-permute-start | bytes 294920 | tf_op jit(solution)/shard_map/while/body/eval_jaxpr/ppermute | solution.py:288
  291.7 6.7 %collective-permute-start.14 = (f32[32,768]{1,0:T(8,128)S(1)}, f32[32,768]{1,0:T(8,128)S(1)}, u32[]{:S(2)}, u32[]{:S(2)}) collective-permute-start(f32[32,768]{1,0:T(8,128)S(1)} %east.20.refs_2_), channel_id=1, source_target_pairs={{0,8},{1,9},{2,10},{3,11},{4,12},{5,13},{6,14},{7,15},{16,24},{17,... | collective-permute-start | bytes 294920 | tf_op jit(solution)/shard_map/while/body/eval_jaxpr/ppermute | solution.py:288
  306.1 6.6 %collective-permute-start.19 = (f32[32,768]{1,0:T(8,128)S(1)}, f32[32,768]{1,0:T(8,128)S(1)}, u32[]{:S(2)}, u32[]{:S(2)}) collective-permute-start(f32[32,768]{1,0:T(8,128)S(1)} %east.22.refs_2_), channel_id=1, source_target_pairs={{0,8},{1,9},{2,10},{3,11},{4,12},{5,13},{6,14},{7,15},{16,24},{17,... | collective-permute-start | bytes 294920 | tf_op jit(solution)/shard_map/while/body/eval_jaxpr/ppermute | solution.py:288
  320.3 6.2 %collective-permute-start.24 = (f32[32,768]{1,0:T(8,128)S(1)}, f32[32,768]{1,0:T(8,128)S(1)}, u32[]{:S(2)}, u32[]{:S(2)}) collective-permute-start(f32[32,768]{1,0:T(8,128)S(1)} %east.24.refs_2_), channel_id=1, source_target_pairs={{0,8},{1,9},{2,10},{3,11},{4,12},{5,13},{6,14},{7,15},{16,24},{17,... | collective-permute-start | bytes 294920 | tf_op jit(solution)/shard_map/while/body/eval_jaxpr/ppermute | solution.py:288
  334.2 6.2 %collective-permute-start.29 = (f32[32,768]{1,0:T(8,128)S(1)}, f32[32,768]{1,0:T(8,128)S(1)}, u32[]{:S(2)}, u32[]{:S(2)}) collective-permute-start(f32[32,768]{1,0:T(8,128)S(1)} %east.26.refs_2_), channel_id=1, source_target_pairs={{0,8},{1,9},{2,10},{3,11},{4,12},{5,13},{6,14},{7,15},{16,24},{17,... | collective-permute-start | bytes 294920 | tf_op jit(solution)/shard_map/while/body/eval_jaxpr/ppermute | solution.py:288
  354.5 5.7 collective-permute-start
  369.6 6.2 %collective-permute-start.4 = (f32[32,768]{1,0:T(8,128)S(1)}, f32[32,768]{1,0:T(8,128)S(1)}, u32[]{:S(2)}, u32[]{:S(2)}) collective-permute-start(f32[32,768]{1,0:T(8,128)S(1)} %east.16.refs_2_), channel_id=1, source_target_pairs={{0,8},{1,9},{2,10},{3,11},{4,12},{5,13},{6,14},{7,15},{16,24},{17,... | collective-permute-start | bytes 294920 | tf_op jit(solution)/shard_map/while/body/eval_jaxpr/ppermute | solution.py:288
  383.8 7.2 %collective-permute-start.9 = (f32[32,768]{1,0:T(8,128)S(1)}, f32[32,768]{1,0:T(8,128)S(1)}, u32[]{:S(2)}, u32[]{:S(2)}) collective-permute-start(f32[32,768]{1,0:T(8,128)S(1)} %east.18.refs_2_), channel_id=1, source_target_pairs={{0,8},{1,9},{2,10},{3,11},{4,12},{5,13},{6,14},{7,15},{16,24},{17,... | collective-permute-start | bytes 294920 | tf_op jit(solution)/shard_map/while/body/eval_jaxpr/ppermute | solution.py:288
  398.7 7.0 %collective-permute-start.14 = (f32[32,768]{1,0:T(8,128)S(1)}, f32[32,768]{1,0:T(8,128)S(1)}, u32[]{:S(2)}, u32[]{:S(2)}) collective-permute-start(f32[32,768]{1,0:T(8,128)S(1)} %east.20.refs_2_), channel_id=1, source_target_pairs={{0,8},{1,9},{2,10},{3,11},{4,12},{5,13},{6,14},{7,15},{16,24},{17,... | collective-permute-start | bytes 294920 | tf_op jit(solution)/shard_map/while/body/eval_jaxpr/ppermute | solution.py:288
  413.4 6.2 %collective-permute-start.19 = (f32[32,768]{1,0:T(8,128)S(1)}, f32[32,768]{1,0:T(8,128)S(1)}, u32[]{:S(2)}, u32[]{:S(2)}) collective-permute-start(f32[32,768]{1,0:T(8,128)S(1)} %east.22.refs_2_), channel_id=1, source_target_pairs={{0,8},{1,9},{2,10},{3,11},{4,12},{5,13},{6,14},{7,15},{16,24},{17,... | collective-permute-start | bytes 294920 | tf_op jit(solution)/shard_map/while/body/eval_jaxpr/ppermute | solution.py:288
  427.3 6.2 %collective-permute-start.24 = (f32[32,768]{1,0:T(8,128)S(1)}, f32[32,768]{1,0:T(8,128)S(1)}, u32[]{:S(2)}, u32[]{:S(2)}) collective-permute-start(f32[32,768]{1,0:T(8,128)S(1)} %east.24.refs_2_), channel_id=1, source_target_pairs={{0,8},{1,9},{2,10},{3,11},{4,12},{5,13},{6,14},{7,15},{16,24},{17,... | collective-permute-start | bytes 294920 | tf_op jit(solution)/shard_map/while/body/eval_jaxpr/ppermute | solution.py:288
  441.2 6.3 %collective-permute-start.29 = (f32[32,768]{1,0:T(8,128)S(1)}, f32[32,768]{1,0:T(8,128)S(1)}, u32[]{:S(2)}, u32[]{:S(2)}) collective-permute-start(f32[32,768]{1,0:T(8,128)S(1)} %east.26.refs_2_), channel_id=1, source_target_pairs={{0,8},{1,9},{2,10},{3,11},{4,12},{5,13},{6,14},{7,15},{16,24},{17,... | collective-permute-start | bytes 294920 | tf_op jit(solution)/shard_map/while/body/eval_jaxpr/ppermute | solution.py:288
  461.5 5.6 collective-permute-start
  476.5 6.4 %collective-permute-start.4 = (f32[32,768]{1,0:T(8,128)S(1)}, f32[32,768]{1,0:T(8,128)S(1)}, u32[]{:S(2)}, u32[]{:S(2)}) collective-permute-start(f32[32,768]{1,0:T(8,128)S(1)} %east.16.refs_2_), channel_id=1, source_target_pairs={{0,8},{1,9},{2,10},{3,11},{4,12},{5,13},{6,14},{7,15},{16,24},{17,... | collective-permute-start | bytes 294920 | tf_op jit(solution)/shard_map/while/body/eval_jaxpr/ppermute | solution.py:288
  490.9 7.3 %collective-permute-start.9 = (f32[32,768]{1,0:T(8,128)S(1)}, f32[32,768]{1,0:T(8,128)S(1)}, u32[]{:S(2)}, u32[]{:S(2)}) collective-permute-start(f32[32,768]{1,0:T(8,128)S(1)} %east.18.refs_2_), channel_id=1, source_target_pairs={{0,8},{1,9},{2,10},{3,11},{4,12},{5,13},{6,14},{7,15},{16,24},{17,... | collective-permute-start | bytes 294920 | tf_op jit(solution)/shard_map/while/body/eval_jaxpr/ppermute | solution.py:288
  505.9 6.4 %collective-permute-start.14 = (f32[32,768]{1,0:T(8,128)S(1)}, f32[32,768]{1,0:T(8,128)S(1)}, u32[]{:S(2)}, u32[]{:S(2)}) collective-permute-start(f32[32,768]{1,0:T(8,128)S(1)} %east.20.refs_2_), channel_id=1, source_target_pairs={{0,8},{1,9},{2,10},{3,11},{4,12},{5,13},{6,14},{7,15},{16,24},{17,... | collective-permute-start | bytes 294920 | tf_op jit(solution)/shard_map/while/body/eval_jaxpr/ppermute | solution.py:288
  520.0 6.2 %collective-permute-start.19 = (f32[32,768]{1,0:T(8,128)S(1)}, f32[32,768]{1,0:T(8,128)S(1)}, u32[]{:S(2)}, u32[]{:S(2)}) collective-permute-start(f32[32,768]{1,0:T(8,128)S(1)} %east.22.refs_2_), channel_id=1, source_target_pairs={{0,8},{1,9},{2,10},{3,11},{4,12},{5,13},{6,14},{7,15},{16,24},{17,... | collective-permute-start | bytes 294920 | tf_op jit(solution)/shard_map/while/body/eval_jaxpr/ppermute | solution.py:288
  533.9 6.2 %collective-permute-start.24 = (f32[32,768]{1,0:T(8,128)S(1)}, f32[32,768]{1,0:T(8,128)S(1)}, u32[]{:S(2)}, u32[]{:S(2)}) collective-permute-start(f32[32,768]{1,0:T(8,128)S(1)} %east.24.refs_2_), channel_id=1, source_target_pairs={{0,8},{1,9},{2,10},{3,11},{4,12},{5,13},{6,14},{7,15},{16,24},{17,... | collective-permute-start | bytes 294920 | tf_op jit(solution)/shard_map/while/body/eval_jaxpr/ppermute | solution.py:288
  547.8 6.2 %collective-permute-start.29 = (f32[32,768]{1,0:T(8,128)S(1)}, f32[32,768]{1,0:T(8,128)S(1)}, u32[]{:S(2)}, u32[]{:S(2)}) collective-permute-start(f32[32,768]{1,0:T(8,128)S(1)} %east.26.refs_2_), channel_id=1, source_target_pairs={{0,8},{1,9},{2,10},{3,11},{4,12},{5,13},{6,14},{7,15},{16,24},{17,... | collective-permute-start | bytes 294920 | tf_op jit(solution)/shard_map/while/body/eval_jaxpr/ppermute | solution.py:288
  601.0 5.8 cholesky.16
  (683 shorter events, 411.2 us)
Async XLA Ops:
  32.3 15.3 %collective-permute-start.1 = (f32[32,768]{1,0:T(8,128)S(1)}, f32[32,768]{1,0:T(8,128)S(1)}, u32[]{:S(2)}, u32[]{:S(2)}) collective-permute-start(f32[32,768]{1,0:T(8,128)S(1)} %get-tuple-element.518), channel_id=1, source_target_pairs={{8,9},{9,10},{10,11},{11,12},{12,13},{13,14},{14,15},{24,25},{25,2... | collective-permute-start | bytes 294920 | tf_op jit(solution)/shard_map/while/body/eval_jaxpr/ppermute | solution.py:292
  35.9 12.3 %collective-permute-start.4 = (f32[32,768]{1,0:T(8,128)S(1)}, f32[32,768]{1,0:T(8,128)S(1)}, u32[]{:S(2)}, u32[]{:S(2)}) collective-permute-start(f32[32,768]{1,0:T(8,128)S(1)} %east.16.refs_2_), channel_id=1, source_target_pairs={{0,8},{1,9},{2,10},{3,11},{4,12},{5,13},{6,14},{7,15},{16,24},{17,... | collective-permute-start | bytes 294920 | tf_op jit(solution)/shard_map/while/body/eval_jaxpr/ppermute | solution.py:288
  50.0 15.1 %collective-permute-start.5 = (f32[32,768]{1,0:T(8,128)S(1)}, f32[32,768]{1,0:T(8,128)S(1)}, u32[]{:S(2)}, u32[]{:S(2)}) collective-permute-start(f32[32,768]{1,0:T(8,128)S(1)} %get-tuple-element.522), channel_id=1, source_target_pairs={{8,9},{9,10},{10,11},{11,12},{12,13},{13,14},{14,15},{24,25},{25,2... | collective-permute-start | bytes 294920 | tf_op jit(solution)/shard_map/while/body/eval_jaxpr/ppermute | solution.py:292
  53.1 12.5 %collective-permute-start.9 = (f32[32,768]{1,0:T(8,128)S(1)}, f32[32,768]{1,0:T(8,128)S(1)}, u32[]{:S(2)}, u32[]{:S(2)}) collective-permute-start(f32[32,768]{1,0:T(8,128)S(1)} %east.18.refs_2_), channel_id=1, source_target_pairs={{0,8},{1,9},{2,10},{3,11},{4,12},{5,13},{6,14},{7,15},{16,24},{17,... | collective-permute-start | bytes 294920 | tf_op jit(solution)/shard_map/while/body/eval_jaxpr/ppermute | solution.py:288
  67.4 12.0 %collective-permute-start.10 = (f32[32,768]{1,0:T(8,128)S(1)}, f32[32,768]{1,0:T(8,128)S(1)}, u32[]{:S(2)}, u32[]{:S(2)}) collective-permute-start(f32[32,768]{1,0:T(8,128)S(1)} %get-tuple-element.526), channel_id=1, source_target_pairs={{8,9},{9,10},{10,11},{11,12},{12,13},{13,14},{14,15},{24,25},{25,2... | collective-permute-start | bytes 294920 | tf_op jit(solution)/shard_map/while/body/eval_jaxpr/ppermute | solution.py:292
  81.8 12.4 %collective-permute-start.15 = (f32[32,768]{1,0:T(8,128)S(1)}, f32[32,768]{1,0:T(8,128)S(1)}, u32[]{:S(2)}, u32[]{:S(2)}) collective-permute-start(f32[32,768]{1,0:T(8,128)S(1)} %get-tuple-element.530), channel_id=1, source_target_pairs={{8,9},{9,10},{10,11},{11,12},{12,13},{13,14},{14,15},{24,25},{25,2... | collective-permute-start | bytes 294920 | tf_op jit(solution)/shard_map/while/body/eval_jaxpr/ppermute | solution.py:292
  96.6 12.4 %collective-permute-start.20 = (f32[32,768]{1,0:T(8,128)S(1)}, f32[32,768]{1,0:T(8,128)S(1)}, u32[]{:S(2)}, u32[]{:S(2)}) collective-permute-start(f32[32,768]{1,0:T(8,128)S(1)} %get-tuple-element.534), channel_id=1, source_target_pairs={{8,9},{9,10},{10,11},{11,12},{12,13},{13,14},{14,15},{24,25},{25,2... | collective-permute-start | bytes 294920 | tf_op jit(solution)/shard_map/while/body/eval_jaxpr/ppermute | solution.py:292
  111.4 13.2 %collective-permute-start.25 = (f32[32,768]{1,0:T(8,128)S(1)}, f32[32,768]{1,0:T(8,128)S(1)}, u32[]{:S(2)}, u32[]{:S(2)}) collective-permute-start(f32[32,768]{1,0:T(8,128)S(1)} %get-tuple-element.538), channel_id=1, source_target_pairs={{8,9},{9,10},{10,11},{11,12},{12,13},{13,14},{14,15},{24,25},{25,2... | collective-permute-start | bytes 294920 | tf_op jit(solution)/shard_map/while/body/eval_jaxpr/ppermute | solution.py:292
  147.7 13.9 %collective-permute-start.1 = (f32[32,768]{1,0:T(8,128)S(1)}, f32[32,768]{1,0:T(8,128)S(1)}, u32[]{:S(2)}, u32[]{:S(2)}) collective-permute-start(f32[32,768]{1,0:T(8,128)S(1)} %get-tuple-element.518), channel_id=1, source_target_pairs={{8,9},{9,10},{10,11},{11,12},{12,13},{13,14},{14,15},{24,25},{25,2... | collective-permute-start | bytes 294920 | tf_op jit(solution)/shard_map/while/body/eval_jaxpr/ppermute | solution.py:292
  163.9 13.7 %collective-permute-start.5 = (f32[32,768]{1,0:T(8,128)S(1)}, f32[32,768]{1,0:T(8,128)S(1)}, u32[]{:S(2)}, u32[]{:S(2)}) collective-permute-start(f32[32,768]{1,0:T(8,128)S(1)} %get-tuple-element.522), channel_id=1, source_target_pairs={{8,9},{9,10},{10,11},{11,12},{12,13},{13,14},{14,15},{24,25},{25,2... | collective-permute-start | bytes 294920 | tf_op jit(solution)/shard_map/while/body/eval_jaxpr/ppermute | solution.py:292
  180.0 12.5 %collective-permute-start.10 = (f32[32,768]{1,0:T(8,128)S(1)}, f32[32,768]{1,0:T(8,128)S(1)}, u32[]{:S(2)}, u32[]{:S(2)}) collective-permute-start(f32[32,768]{1,0:T(8,128)S(1)} %get-tuple-element.526), channel_id=1, source_target_pairs={{8,9},{9,10},{10,11},{11,12},{12,13},{13,14},{14,15},{24,25},{25,2... | collective-permute-start | bytes 294920 | tf_op jit(solution)/shard_map/while/body/eval_jaxpr/ppermute | solution.py:292
  194.8 12.5 %collective-permute-start.15 = (f32[32,768]{1,0:T(8,128)S(1)}, f32[32,768]{1,0:T(8,128)S(1)}, u32[]{:S(2)}, u32[]{:S(2)}) collective-permute-start(f32[32,768]{1,0:T(8,128)S(1)} %get-tuple-element.530), channel_id=1, source_target_pairs={{8,9},{9,10},{10,11},{11,12},{12,13},{13,14},{14,15},{24,25},{25,2... | collective-permute-start | bytes 294920 | tf_op jit(solution)/shard_map/while/body/eval_jaxpr/ppermute | solution.py:292
  209.7 12.0 %collective-permute-start.20 = (f32[32,768]{1,0:T(8,128)S(1)}, f32[32,768]{1,0:T(8,128)S(1)}, u32[]{:S(2)}, u32[]{:S(2)}) collective-permute-start(f32[32,768]{1,0:T(8,128)S(1)} %get-tuple-element.534), channel_id=1, source_target_pairs={{8,9},{9,10},{10,11},{11,12},{12,13},{13,14},{14,15},{24,25},{25,2... | collective-permute-start | bytes 294920 | tf_op jit(solution)/shard_map/while/body/eval_jaxpr/ppermute | solution.py:292
  224.1 12.6 %collective-permute-start.25 = (f32[32,768]{1,0:T(8,128)S(1)}, f32[32,768]{1,0:T(8,128)S(1)}, u32[]{:S(2)}, u32[]{:S(2)}) collective-permute-start(f32[32,768]{1,0:T(8,128)S(1)} %get-tuple-element.538), channel_id=1, source_target_pairs={{8,9},{9,10},{10,11},{11,12},{12,13},{13,14},{14,15},{24,25},{25,2... | collective-permute-start | bytes 294920 | tf_op jit(solution)/shard_map/while/body/eval_jaxpr/ppermute | solution.py:292
  259.9 12.7 %collective-permute-start.1 = (f32[32,768]{1,0:T(8,128)S(1)}, f32[32,768]{1,0:T(8,128)S(1)}, u32[]{:S(2)}, u32[]{:S(2)}) collective-permute-start(f32[32,768]{1,0:T(8,128)S(1)} %get-tuple-element.518), channel_id=1, source_target_pairs={{8,9},{9,10},{10,11},{11,12},{12,13},{13,14},{14,15},{24,25},{25,2... | collective-permute-start | bytes 294920 | tf_op jit(solution)/shard_map/while/body/eval_jaxpr/ppermute | solution.py:292
  275.0 12.5 %collective-permute-start.5 = (f32[32,768]{1,0:T(8,128)S(1)}, f32[32,768]{1,0:T(8,128)S(1)}, u32[]{:S(2)}, u32[]{:S(2)}) collective-permute-start(f32[32,768]{1,0:T(8,128)S(1)} %get-tuple-element.522), channel_id=1, source_target_pairs={{8,9},{9,10},{10,11},{11,12},{12,13},{13,14},{14,15},{24,25},{25,2... | collective-permute-start | bytes 294920 | tf_op jit(solution)/shard_map/while/body/eval_jaxpr/ppermute | solution.py:292
  289.9 12.0 %collective-permute-start.10 = (f32[32,768]{1,0:T(8,128)S(1)}, f32[32,768]{1,0:T(8,128)S(1)}, u32[]{:S(2)}, u32[]{:S(2)}) collective-permute-start(f32[32,768]{1,0:T(8,128)S(1)} %get-tuple-element.526), channel_id=1, source_target_pairs={{8,9},{9,10},{10,11},{11,12},{12,13},{13,14},{14,15},{24,25},{25,2... | collective-permute-start | bytes 294920 | tf_op jit(solution)/shard_map/while/body/eval_jaxpr/ppermute | solution.py:292
  304.2 11.9 %collective-permute-start.15 = (f32[32,768]{1,0:T(8,128)S(1)}, f32[32,768]{1,0:T(8,128)S(1)}, u32[]{:S(2)}, u32[]{:S(2)}) collective-permute-start(f32[32,768]{1,0:T(8,128)S(1)} %get-tuple-element.530), channel_id=1, source_target_pairs={{8,9},{9,10},{10,11},{11,12},{12,13},{13,14},{14,15},{24,25},{25,2... | collective-permute-start | bytes 294920 | tf_op jit(solution)/shard_map/while/body/eval_jaxpr/ppermute | solution.py:292
  318.5 11.5 %collective-permute-start.20 = (f32[32,768]{1,0:T(8,128)S(1)}, f32[32,768]{1,0:T(8,128)S(1)}, u32[]{:S(2)}, u32[]{:S(2)}) collective-permute-start(f32[32,768]{1,0:T(8,128)S(1)} %get-tuple-element.534), channel_id=1, source_target_pairs={{8,9},{9,10},{10,11},{11,12},{12,13},{13,14},{14,15},{24,25},{25,2... | collective-permute-start | bytes 294920 | tf_op jit(solution)/shard_map/while/body/eval_jaxpr/ppermute | solution.py:292
  332.4 12.1 %collective-permute-start.25 = (f32[32,768]{1,0:T(8,128)S(1)}, f32[32,768]{1,0:T(8,128)S(1)}, u32[]{:S(2)}, u32[]{:S(2)}) collective-permute-start(f32[32,768]{1,0:T(8,128)S(1)} %get-tuple-element.538), channel_id=1, source_target_pairs={{8,9},{9,10},{10,11},{11,12},{12,13},{13,14},{14,15},{24,25},{25,2... | collective-permute-start | bytes 294920 | tf_op jit(solution)/shard_map/while/body/eval_jaxpr/ppermute | solution.py:292
  367.4 12.2 %collective-permute-start.1 = (f32[32,768]{1,0:T(8,128)S(1)}, f32[32,768]{1,0:T(8,128)S(1)}, u32[]{:S(2)}, u32[]{:S(2)}) collective-permute-start(f32[32,768]{1,0:T(8,128)S(1)} %get-tuple-element.518), channel_id=1, source_target_pairs={{8,9},{9,10},{10,11},{11,12},{12,13},{13,14},{14,15},{24,25},{25,2... | collective-permute-start | bytes 294920 | tf_op jit(solution)/shard_map/while/body/eval_jaxpr/ppermute | solution.py:292
  382.0 12.5 %collective-permute-start.5 = (f32[32,768]{1,0:T(8,128)S(1)}, f32[32,768]{1,0:T(8,128)S(1)}, u32[]{:S(2)}, u32[]{:S(2)}) collective-permute-start(f32[32,768]{1,0:T(8,128)S(1)} %get-tuple-element.522), channel_id=1, source_target_pairs={{8,9},{9,10},{10,11},{11,12},{12,13},{13,14},{14,15},{24,25},{25,2... | collective-permute-start | bytes 294920 | tf_op jit(solution)/shard_map/while/body/eval_jaxpr/ppermute | solution.py:292
  396.9 12.3 %collective-permute-start.10 = (f32[32,768]{1,0:T(8,128)S(1)}, f32[32,768]{1,0:T(8,128)S(1)}, u32[]{:S(2)}, u32[]{:S(2)}) collective-permute-start(f32[32,768]{1,0:T(8,128)S(1)} %get-tuple-element.526), channel_id=1, source_target_pairs={{8,9},{9,10},{10,11},{11,12},{12,13},{13,14},{14,15},{24,25},{25,2... | collective-permute-start | bytes 294920 | tf_op jit(solution)/shard_map/while/body/eval_jaxpr/ppermute | solution.py:292
  411.6 11.5 %collective-permute-start.15 = (f32[32,768]{1,0:T(8,128)S(1)}, f32[32,768]{1,0:T(8,128)S(1)}, u32[]{:S(2)}, u32[]{:S(2)}) collective-permute-start(f32[32,768]{1,0:T(8,128)S(1)} %get-tuple-element.530), channel_id=1, source_target_pairs={{8,9},{9,10},{10,11},{11,12},{12,13},{13,14},{14,15},{24,25},{25,2... | collective-permute-start | bytes 294920 | tf_op jit(solution)/shard_map/while/body/eval_jaxpr/ppermute | solution.py:292
  425.5 11.5 %collective-permute-start.20 = (f32[32,768]{1,0:T(8,128)S(1)}, f32[32,768]{1,0:T(8,128)S(1)}, u32[]{:S(2)}, u32[]{:S(2)}) collective-permute-start(f32[32,768]{1,0:T(8,128)S(1)} %get-tuple-element.534), channel_id=1, source_target_pairs={{8,9},{9,10},{10,11},{11,12},{12,13},{13,14},{14,15},{24,25},{25,2... | collective-permute-start | bytes 294920 | tf_op jit(solution)/shard_map/while/body/eval_jaxpr/ppermute | solution.py:292
  439.4 12.2 %collective-permute-start.25 = (f32[32,768]{1,0:T(8,128)S(1)}, f32[32,768]{1,0:T(8,128)S(1)}, u32[]{:S(2)}, u32[]{:S(2)}) collective-permute-start(f32[32,768]{1,0:T(8,128)S(1)} %get-tuple-element.538), channel_id=1, source_target_pairs={{8,9},{9,10},{10,11},{11,12},{12,13},{13,14},{14,15},{24,25},{25,2... | collective-permute-start | bytes 294920 | tf_op jit(solution)/shard_map/while/body/eval_jaxpr/ppermute | solution.py:292
  474.3 12.4 %collective-permute-start.1 = (f32[32,768]{1,0:T(8,128)S(1)}, f32[32,768]{1,0:T(8,128)S(1)}, u32[]{:S(2)}, u32[]{:S(2)}) collective-permute-start(f32[32,768]{1,0:T(8,128)S(1)} %get-tuple-element.518), channel_id=1, source_target_pairs={{8,9},{9,10},{10,11},{11,12},{12,13},{13,14},{14,15},{24,25},{25,2... | collective-permute-start | bytes 294920 | tf_op jit(solution)/shard_map/while/body/eval_jaxpr/ppermute | solution.py:292
  489.1 12.6 %collective-permute-start.5 = (f32[32,768]{1,0:T(8,128)S(1)}, f32[32,768]{1,0:T(8,128)S(1)}, u32[]{:S(2)}, u32[]{:S(2)}) collective-permute-start(f32[32,768]{1,0:T(8,128)S(1)} %get-tuple-element.522), channel_id=1, source_target_pairs={{8,9},{9,10},{10,11},{11,12},{12,13},{13,14},{14,15},{24,25},{25,2... | collective-permute-start | bytes 294920 | tf_op jit(solution)/shard_map/while/body/eval_jaxpr/ppermute | solution.py:292
  504.1 11.7 %collective-permute-start.10 = (f32[32,768]{1,0:T(8,128)S(1)}, f32[32,768]{1,0:T(8,128)S(1)}, u32[]{:S(2)}, u32[]{:S(2)}) collective-permute-start(f32[32,768]{1,0:T(8,128)S(1)} %get-tuple-element.526), channel_id=1, source_target_pairs={{8,9},{9,10},{10,11},{11,12},{12,13},{13,14},{14,15},{24,25},{25,2... | collective-permute-start | bytes 294920 | tf_op jit(solution)/shard_map/while/body/eval_jaxpr/ppermute | solution.py:292
  518.2 11.5 %collective-permute-start.15 = (f32[32,768]{1,0:T(8,128)S(1)}, f32[32,768]{1,0:T(8,128)S(1)}, u32[]{:S(2)}, u32[]{:S(2)}) collective-permute-start(f32[32,768]{1,0:T(8,128)S(1)} %get-tuple-element.530), channel_id=1, source_target_pairs={{8,9},{9,10},{10,11},{11,12},{12,13},{13,14},{14,15},{24,25},{25,2... | collective-permute-start | bytes 294920 | tf_op jit(solution)/shard_map/while/body/eval_jaxpr/ppermute | solution.py:292
  532.1 11.5 %collective-permute-start.20 = (f32[32,768]{1,0:T(8,128)S(1)}, f32[32,768]{1,0:T(8,128)S(1)}, u32[]{:S(2)}, u32[]{:S(2)}) collective-permute-start(f32[32,768]{1,0:T(8,128)S(1)} %get-tuple-element.534), channel_id=1, source_target_pairs={{8,9},{9,10},{10,11},{11,12},{12,13},{13,14},{14,15},{24,25},{25,2... | collective-permute-start | bytes 294920 | tf_op jit(solution)/shard_map/while/body/eval_jaxpr/ppermute | solution.py:292
  546.0 12.1 %collective-permute-start.25 = (f32[32,768]{1,0:T(8,128)S(1)}, f32[32,768]{1,0:T(8,128)S(1)}, u32[]{:S(2)}, u32[]{:S(2)}) collective-permute-start(f32[32,768]{1,0:T(8,128)S(1)} %get-tuple-element.538), channel_id=1, source_target_pairs={{8,9},{9,10},{10,11},{11,12},{12,13},{13,14},{14,15},{24,25},{25,2... | collective-permute-start | bytes 294920 | tf_op jit(solution)/shard_map/while/body/eval_jaxpr/ppermute | solution.py:292
  (201 other events, 1220.6 us)

commit v3 on v2

--- a/solution.py
+++ b/solution.py
@@ -8,8 +8,7 @@
 from jax.sharding import PartitionSpec as P
 
 PIECES = 2
-UNROLL = 7
-Z = 8
+UNROLL = 9
 LIMIT = 8
 VMEM = pl.BlockSpec(memory_space=pltpu.VMEM)
 SMEM = pl.BlockSpec(memory_space=pltpu.SMEM)
@@ -32,6 +31,16 @@
     main = jnp.dot(both, high_ref[...], preferred_element_type=F32)
     rest = jnp.dot(high, low_ref[...], preferred_element_type=F32)
     return main[:rows] + (main[rows:] + rest)
+
+
+def unwritten(*shapes):
+    return pl.pallas_call(
+        pass_through_kernel,
+        out_shape=tuple(jax.ShapeDtypeStruct(shape, F32) for shape in shapes),
+        out_specs=(ANY,) * len(shapes),
+        compiler_params=params(4),
+        name="unwritten",
+    )()
 
 
 def pass_through_kernel(*refs):
@@ -113,32 +122,23 @@
         out_ref[:, half:] = placed_ref[piece, :, half:] + product(south, nh_ref, nl_ref)
 
 
-def chosen(age_ref, west_refs):
-    if len(west_refs) == 1:
-        return west_refs[0][...]
-    return jnp.where(age_ref[1] > 0, west_refs[1][...], west_refs[0][...])
-
-
-def east_kernel(offset, count, wests, age_ref, partial_ref, high_ref, low_ref, *refs):
+def east_kernel(offset, count, age_ref, partial_ref, west_ref, high_ref, low_ref, out_ref):
     active, _ = when_active(offset, count, age_ref)
-    west_refs, (out_ref,) = refs[:wests], refs[wests:]
-    half = out_ref.shape[1]
+    half = west_ref.shape[1]
 
     @pl.when(active)
     def _():
-        west = chosen(age_ref, west_refs)
-        out_ref[...] = partial_ref[:, :half] + product(west, high_ref, low_ref)
-
-
-def north_kernel(offset, count, wests, age_ref, partial_ref, high_ref, low_ref, *refs):
-    west_refs, (east_ref, _, out_ref, results_ref) = refs[:wests], refs[wests:]
+        out_ref[...] = partial_ref[:, :half] + product(west_ref[...], high_ref, low_ref)
+
+
+def north_kernel(offset, count, age_ref, partial_ref, west_ref, high_ref, low_ref, east_ref, *refs):
+    out_ref, results_ref = refs[-2:]
     active, piece = when_active(offset, count, age_ref)
-    half = out_ref.shape[1]
+    half = west_ref.shape[1]
 
     @pl.when(active)
     def _():
-        west = chosen(age_ref, west_refs)
-        value = partial_ref[:, half:] + product(west, high_ref, low_ref)
+        value = partial_ref[:, half:] + product(west_ref[...], high_ref, low_ref)
         out_ref[...] = value
         results_ref[piece, :, :half] = east_ref[...]
         results_ref[piece, :, half:] = value
@@ -165,34 +165,34 @@
     )(age, placed, south, *weights)
 
 
-def east_part(offset, count, age, partial, wests, weights):
-    width, half = wests[0].shape
-    return pl.pallas_call(
-        functools.partial(east_kernel, offset, count, len(wests)),
+def east_part(offset, count, age, partial, west, weights):
+    width, half = west.shape
+    return pl.pallas_call(
+        functools.partial(east_kernel, offset, count),
         out_shape=jax.ShapeDtypeStruct((width, half), F32),
-        in_specs=[SMEM] + [VMEM] * (3 + len(wests)),
+        in_specs=[SMEM] + [VMEM] * 4,
         out_specs=VMEM,
         compiler_params=params(LIMIT),
         cost_estimate=estimate(width, half, 1),
         name="east",
-    )(age, partial, *weights, *wests)
-
-
-def north_part(offset, count, age, partial, wests, weights, east, results):
-    width, half = wests[0].shape
-    return pl.pallas_call(
-        functools.partial(north_kernel, offset, count, len(wests)),
+    )(age, partial, west, *weights)
+
+
+def north_part(offset, count, age, partial, west, weights, east, results):
+    width, half = west.shape
+    return pl.pallas_call(
+        functools.partial(north_kernel, offset, count),
         out_shape=(
             jax.ShapeDtypeStruct((width, half), F32),
             jax.ShapeDtypeStruct(results.shape, F32),
         ),
-        in_specs=[SMEM] + [VMEM] * (5 + len(wests)),
+        in_specs=[SMEM] + [VMEM] * 6,
         out_specs=(VMEM, VMEM),
-        input_output_aliases={5 + len(wests): 1},
+        input_output_aliases={6: 1},
         compiler_params=params(LIMIT),
         cost_estimate=estimate(width, half, 1),
         name="north",
-    )(age, partial, *weights, *wests, east, results)
+    )(age, partial, west, *weights, east, results)
 
 
 def summed(value, shape):
@@ -235,29 +235,20 @@
     )(plan, rows, sources)
 
 
-def east_pairs(shape, parity, far):
+def sweep_pairs(shape, parity, dx, dy):
     nx, ny = shape
     return [
-        (x * ny + y, (x + 1) * ny + y)
-        for x in range(parity, nx - 1, 2)
-        for y in range(ny)
-        if ((x + 1) % Z == 0) == far
-    ]
-
-
-def north_pairs(shape, parity):
-    nx, ny = shape
-    return [
-        (x * ny + y, x * ny + y + 1) for x in range(parity, nx, 2) for y in range(ny - 1)
+        (x * ny + y, (x + dx) * ny + y + dy)
+        for x in range(nx - dx)
+        for y in range(ny - dy)
+        if (x + y) % 2 == parity
     ]
 
 
 def body(shape, operators, sources, source_rows, batch_plan):
     nx, ny = shape
     axes = ("gx", "gy")
-    column = lax.axis_index("gx")
-    depth = column + 2 * lax.div(column, Z) + 2 * lax.axis_index("gy")
-    starts_row = (lax.rem(column, Z) == 0).astype(jnp.int32)
+    depth = lax.axis_index("gx") + 3 * lax.axis_index("gy")
     order = operators.shape[-1]
     half = order // 2
     _, _, batches, columns, placed_count = sources.shape
@@ -267,42 +258,31 @@
     placed = placed.reshape(count, width, order)
     quarters = split_operator(operators[0, 0])
 
-    deepest = nx - 1 + 2 * ((nx - 1) // Z) + 2 * (ny - 1)
-    steps = (deepest + 2 * (count - 1)) // 2 + 1
+    steps = (nx - 1 + 3 * (ny - 1) + 2 * (count - 1)) // 2 + 1
     trips = -(-steps // UNROLL)
 
     def advance(trip, carry):
-        even_west, odd_west, far_old, far_new, south, results, fixed = carry
-        south = list(south)
+        west, south, results, fixed = carry
         fixed = pass_through(*fixed)
         placed, quarters = fixed[0], fixed[1:]
-        age = trip * (2 * UNROLL) - depth
-        age_ref = jnp.stack([age, starts_row]).astype(jnp.int32)
+        age = (trip * (2 * UNROLL) - depth)[None].astype(jnp.int32)
+        south = list(south)
         for offset in range(2 * UNROLL):
             parity = offset % 2
-            wests = (odd_west,) if parity else (even_west, far_old)
-            partial = south_part(
-                offset, count, age_ref, placed, south[parity], quarters[4:]
+            partial = south_part(offset, count, age, placed, south[0], quarters[4:])
+            to_east = east_part(offset, count, age, partial, west, quarters[:2])
+            arrived = lax.ppermute(to_east, axes, sweep_pairs(shape, parity, 1, 0))
+            to_north, results = north_part(
+                offset, count, age, partial, west, quarters[2:4], to_east, results
             )
-            to_east = east_part(offset, count, age_ref, partial, wests, quarters[:2])
-            arrived = lax.ppermute(to_east, axes, east_pairs(shape, parity, False))
-            to_north, results = north_part(
-                offset, count, age_ref, partial, wests, quarters[2:4], to_east, results
-            )
-            south[parity] = lax.ppermute(to_north, axes, north_pairs(shape, parity))
-            if parity:
-                even_west = arrived
-                far_old, far_new = far_new, lax.ppermute(
-                    to_east, axes, east_pairs(shape, parity, True)
-                )
-            else:
-                odd_west = arrived
-        return (even_west, odd_west, far_old, far_new, tuple(south), results, tuple(fixed))
+            risen = lax.ppermute(to_north, axes, sweep_pairs(shape, parity, 0, 1))
+            west, south = arrived, south[1:] + [risen]
+        return (west, tuple(south), results, tuple(fixed))
 
     zero = jnp.zeros((width, half), F32)
-    results = jnp.zeros((count, width, order), F32)
-    carry = (zero, zero, zero, zero, (zero, zero), results, (placed, *quarters))
-    results = lax.fori_loop(0, trips, advance, carry)[5]
+    (results,) = unwritten((count, width, order))
+    carry = (zero, (zero, zero, zero), results, (placed, *quarters))
+    results = lax.fori_loop(0, trips, advance, carry)[2]
     first = results[:PIECES].reshape(columns, order)
     rest = results[PIECES:]
     partial_gram = lax.dot_general(

time: 625 us -> 558 us (0.89)
  Pallas kernels: 162 us -> 52.5 us
  starting transfers between devices: 403 us -> 441 us
  waiting for transfers between devices: 16.4 us -> 25 us
    pallas_call x140 -> x145, Pallas kernels: 96.5 us -> 18.9 us  [the longest x72 9.47 us: north_part(): pl.pallas_call(functools.partial(north_kernel, offset, count), out_shape=...]
    pallas_call x70 -> x72, Pallas kernels: 59.2 us -> 27.1 us  [south_part(): pl.pallas_call(functools.partial(south_kernel, offset, count), out_shape=...]
    ppermute x175 -> x144, starting transfers between devices: 385 us -> 415 us  [the longest x72 318 us: advance(): risen = lax.ppermute(to_north, axes, sweep_pairs(shape, parity, 0, 1))]
    ppermute x175 -> x144, waiting for transfers between devices: 0.59 us -> 11.6 us  [the longest x72 11.4 us: advance(): arrived = lax.ppermute(to_east, axes, sweep_pairs(shape, parity, 1, 0))]
    ppermute x8, starting transfers between devices: 18.1 us -> 25.6 us  [summed(): value = value + lax.ppermute(value, axis, pairs)]
  transfers between devices with their start and end apart: 183 -> 152, of which waited for: 8 -> 39; matrix products, arithmetic and copies ran while one was open for 0% -> 0% of each run, Pallas kernels for 22% -> 6%
where the time goes in v3:
time: 558 us; the launch traced here: 548 us
  starting transfers between devices  441 us (79%)
  Pallas kernels  52.5 us (9%)
  waiting for transfers between devices  25 us (4%)
  local copies, waits for them, and re-layouts  12.2 us (2%)
  other arithmetic  12.1 us (2%)
    ppermute x72, starting transfers between devices, advance(): risen = lax.ppermute(to_north, axes, sweep_pairs(shape, parity, 0, 1))  318 us
    ppermute x72, starting transfers between devices, advance(): arrived = lax.ppermute(to_east, axes, sweep_pairs(shape, parity, 1, 0))  96.5 us
    pallas_call x72, Pallas kernels, south_part(): pl.pallas_call(functools.partial(south_kernel, offset, count), out_shape=...  27.1 us
    ppermute x8, starting transfers between devices, summed(): value = value + lax.ppermute(value, axis, pairs)  25.6 us
    ppermute x8, waiting for transfers between devices, summed(): value = value + lax.ppermute(value, axis, pairs)  13.4 us
    ppermute x72, waiting for transfers between devices, advance(): arrived = lax.ppermute(to_east, axes, sweep_pairs(shape, parity, 1, 0))  11.4 us
  transfers between devices with their start and end apart: 152, of which 39 were waited for; matrix products, arithmetic and copies ran while one was open for 0% of the time, Pallas kernels for 6%

profile of v3, /device:TPU:1, one launch (start us, length us, event | category | flops | bytes accessed | tf_op | source)
XLA Modules:
  0.0 548.0 jit_solution(14942787349201568520)
XLA Ops:
  13.5 478.4 %while.39 = (s32[]{:T(128)}, f32[32,768]{1,0:T(8,128)}, f32[32,768]{1,0:T(8,128)}, f32[32,768]{1,0:T(8,128)}, f32[32,768]{1,0:T(8,128)}, /*index=5*/f32[10,32,15...) while((s32[]{:T(128)}, f32[32,768]{1,0:T(8,128)}, ...), condition=%wide.region_1.0_spmd, body=%wide.region_0.0_spmd.sunk | while | flops 8153726976 | bytes 119539552 | solution.py:285
  19.4 7.9 %collective-permute-start.1 = (f32[32,768]{1,0:T(8,128)S(1)}, f32[32,768]{1,0:T(8,128)S(1)}, u32[]{:S(2)}, u32[]{:S(2)}) collective-permute-start(f32[32,768]{1,0:T(8,128)S(1)} %east.19.east_ref), channel_id=1, source_target_pairs={{1,9},{3,11},{5,13},{7,15},{8,16},{10,18},{12,20},{14,22},{17,25},... | collective-permute-start | bytes 294920 | tf_op jit(solution)/shard_map/while/body/eval_jaxpr/ppermute | solution.py:274
  31.1 7.8 %collective-permute-start.3 = (f32[32,768]{1,0:T(8,128)S(1)}, f32[32,768]{1,0:T(8,128)S(1)}, u32[]{:S(2)}, u32[]{:S(2)}) collective-permute-start(f32[32,768]{1,0:T(8,128)S(1)} %get-tuple-element.493), channel_id=1, source_target_pairs={{1,2},{3,4},{5,6},{8,9},{10,11},{12,13},{14,15},{17,18},{19,20},{2... | collective-permute-start | bytes 294920 | tf_op jit(solution)/shard_map/while/body/eval_jaxpr/ppermute | solution.py:278
  44.4 6.8 %collective-permute-start.10 = (f32[32,768]{1,0:T(8,128)S(1)}, f32[32,768]{1,0:T(8,128)S(1)}, u32[]{:S(2)}, u32[]{:S(2)}) collective-permute-start(f32[32,768]{1,0:T(8,128)S(1)} %get-tuple-element.500), channel_id=1, source_target_pairs={{1,2},{3,4},{5,6},{8,9},{10,11},{12,13},{14,15},{17,18},{19,20},{2... | collective-permute-start | bytes 294920 | tf_op jit(solution)/shard_map/while/body/eval_jaxpr/ppermute | solution.py:278
  112.3 7.2 %collective-permute-start.33 = (f32[32,768]{1,0:T(8,128)S(1)}, f32[32,768]{1,0:T(8,128)}, u32[]{:S(2)}, u32[]{:S(2)}) collective-permute-start(f32[32,768]{1,0:T(8,128)S(1)} %get-tuple-element.520), channel_id=1, source_target_pairs={{1,2},{3,4},{5,6},{8,9},{10,11},{12,13},{14,15},{17,18},{19,20},{2... | collective-permute-start | bytes 294920 | tf_op jit(solution)/shard_map/while/body/eval_jaxpr/ppermute | solution.py:278
  147.4 7.5 %collective-permute-start.3 = (f32[32,768]{1,0:T(8,128)S(1)}, f32[32,768]{1,0:T(8,128)S(1)}, u32[]{:S(2)}, u32[]{:S(2)}) collective-permute-start(f32[32,768]{1,0:T(8,128)S(1)} %get-tuple-element.493), channel_id=1, source_target_pairs={{1,2},{3,4},{5,6},{8,9},{10,11},{12,13},{14,15},{17,18},{19,20},{2... | collective-permute-start | bytes 294920 | tf_op jit(solution)/shard_map/while/body/eval_jaxpr/ppermute | solution.py:278
  171.3 7.9 %collective-permute-start.8 = (f32[32,768]{1,0:T(8,128)S(1)}, f32[32,768]{1,0:T(8,128)S(1)}, u32[]{:S(2)}, u32[]{:S(2)}) collective-permute-start(f32[32,768]{1,0:T(8,128)S(1)} %get-tuple-element.498), channel_id=1, source_target_pairs={{1,2},{3,4},{5,6},{8,9},{10,11},{12,13},{14,15},{17,18},{19,20},{2... | collective-permute-start | bytes 294920 | tf_op jit(solution)/shard_map/while/body/eval_jaxpr/ppermute | solution.py:278
  182.8 9.3 %collective-permute-start.15 = (f32[32,768]{1,0:T(8,128)S(1)}, f32[32,768]{1,0:T(8,128)S(1)}, u32[]{:S(2)}, u32[]{:S(2)}) collective-permute-start(f32[32,768]{1,0:T(8,128)S(1)} %get-tuple-element.505), channel_id=1, source_target_pairs={{1,2},{3,4},{5,6},{8,9},{10,11},{12,13},{14,15},{17,18},{19,20},{2... | collective-permute-start | bytes 294920 | tf_op jit(solution)/shard_map/while/body/eval_jaxpr/ppermute | solution.py:278
  195.8 8.0 %collective-permute-start.22 = (f32[32,768]{1,0:T(8,128)S(1)}, f32[32,768]{1,0:T(8,128)S(1)}, u32[]{:S(2)}, u32[]{:S(2)}) collective-permute-start(f32[32,768]{1,0:T(8,128)S(1)} %get-tuple-element.512), channel_id=1, source_target_pairs={{1,2},{3,4},{5,6},{8,9},{10,11},{12,13},{14,15},{17,18},{19,20},{2... | collective-permute-start | bytes 294920 | tf_op jit(solution)/shard_map/while/body/eval_jaxpr/ppermute | solution.py:278
  207.5 9.5 %collective-permute-start.20 = (f32[32,768]{1,0:T(8,128)S(1)}, f32[32,768]{1,0:T(8,128)S(1)}, u32[]{:S(2)}, u32[]{:S(2)}) collective-permute-start(f32[32,768]{1,0:T(8,128)S(1)} %get-tuple-element.510), channel_id=1, source_target_pairs={{1,2},{3,4},{5,6},{8,9},{10,11},{12,13},{14,15},{17,18},{19,20},{2... | collective-permute-start | bytes 294920 | tf_op jit(solution)/shard_map/while/body/eval_jaxpr/ppermute | solution.py:278
  220.7 8.3 %collective-permute-start.27 = (f32[32,768]{1,0:T(8,128)S(1)}, f32[32,768]{1,0:T(8,128)S(1)}, u32[]{:S(2)}, u32[]{:S(2)}) collective-permute-start(f32[32,768]{1,0:T(8,128)S(1)} %get-tuple-element.517), channel_id=1, source_target_pairs={{1,2},{3,4},{5,6},{8,9},{10,11},{12,13},{14,15},{17,18},{19,20},{2... | collective-permute-start | bytes 294920 | tf_op jit(solution)/shard_map/while/body/eval_jaxpr/ppermute | solution.py:278
  232.7 9.6 %collective-permute-start.33 = (f32[32,768]{1,0:T(8,128)S(1)}, f32[32,768]{1,0:T(8,128)}, u32[]{:S(2)}, u32[]{:S(2)}) collective-permute-start(f32[32,768]{1,0:T(8,128)S(1)} %get-tuple-element.520), channel_id=1, source_target_pairs={{1,2},{3,4},{5,6},{8,9},{10,11},{12,13},{14,15},{17,18},{19,20},{2... | collective-permute-start | bytes 294920 | tf_op jit(solution)/shard_map/while/body/eval_jaxpr/ppermute | solution.py:278
  243.6 6.9 %collective-permute-start.35 = (f32[32,768]{1,0:T(8,128)S(1)}, f32[32,768]{1,0:T(8,128)}, u32[]{:S(2)}, u32[]{:S(2)}) collective-permute-start(f32[32,768]{1,0:T(8,128)S(1)} %get-tuple-element.524), channel_id=1, source_target_pairs={{1,2},{3,4},{5,6},{8,9},{10,11},{12,13},{14,15},{17,18},{19,20},{2... | collective-permute-start | bytes 294920 | tf_op jit(solution)/shard_map/while/body/eval_jaxpr/ppermute | solution.py:278
  259.3 7.6 %collective-permute-start.1 = (f32[32,768]{1,0:T(8,128)S(1)}, f32[32,768]{1,0:T(8,128)S(1)}, u32[]{:S(2)}, u32[]{:S(2)}) collective-permute-start(f32[32,768]{1,0:T(8,128)S(1)} %east.19.east_ref), channel_id=1, source_target_pairs={{1,9},{3,11},{5,13},{7,15},{8,16},{10,18},{12,20},{14,22},{17,25},... | collective-permute-start | bytes 294920 | tf_op jit(solution)/shard_map/while/body/eval_jaxpr/ppermute | solution.py:274
  270.7 8.5 %collective-permute-start.3 = (f32[32,768]{1,0:T(8,128)S(1)}, f32[32,768]{1,0:T(8,128)S(1)}, u32[]{:S(2)}, u32[]{:S(2)}) collective-permute-start(f32[32,768]{1,0:T(8,128)S(1)} %get-tuple-element.493), channel_id=1, source_target_pairs={{1,2},{3,4},{5,6},{8,9},{10,11},{12,13},{14,15},{17,18},{19,20},{2... | collective-permute-start | bytes 294920 | tf_op jit(solution)/shard_map/while/body/eval_jaxpr/ppermute | solution.py:278
  282.9 8.9 %collective-permute-start.10 = (f32[32,768]{1,0:T(8,128)S(1)}, f32[32,768]{1,0:T(8,128)S(1)}, u32[]{:S(2)}, u32[]{:S(2)}) collective-permute-start(f32[32,768]{1,0:T(8,128)S(1)} %get-tuple-element.500), channel_id=1, source_target_pairs={{1,2},{3,4},{5,6},{8,9},{10,11},{12,13},{14,15},{17,18},{19,20},{2... | collective-permute-start | bytes 294920 | tf_op jit(solution)/shard_map/while/body/eval_jaxpr/ppermute | solution.py:278
  295.5 11.5 %collective-permute-start.8 = (f32[32,768]{1,0:T(8,128)S(1)}, f32[32,768]{1,0:T(8,128)S(1)}, u32[]{:S(2)}, u32[]{:S(2)}) collective-permute-start(f32[32,768]{1,0:T(8,128)S(1)} %get-tuple-element.498), channel_id=1, source_target_pairs={{1,2},{3,4},{5,6},{8,9},{10,11},{12,13},{14,15},{17,18},{19,20},{2... | collective-permute-start | bytes 294920 | tf_op jit(solution)/shard_map/while/body/eval_jaxpr/ppermute | solution.py:278
  310.7 7.7 %collective-permute-start.15 = (f32[32,768]{1,0:T(8,128)S(1)}, f32[32,768]{1,0:T(8,128)S(1)}, u32[]{:S(2)}, u32[]{:S(2)}) collective-permute-start(f32[32,768]{1,0:T(8,128)S(1)} %get-tuple-element.505), channel_id=1, source_target_pairs={{1,2},{3,4},{5,6},{8,9},{10,11},{12,13},{14,15},{17,18},{19,20},{2... | collective-permute-start | bytes 294920 | tf_op jit(solution)/shard_map/while/body/eval_jaxpr/ppermute | solution.py:278
  322.0 7.3 %collective-permute-start.22 = (f32[32,768]{1,0:T(8,128)S(1)}, f32[32,768]{1,0:T(8,128)S(1)}, u32[]{:S(2)}, u32[]{:S(2)}) collective-permute-start(f32[32,768]{1,0:T(8,128)S(1)} %get-tuple-element.512), channel_id=1, source_target_pairs={{1,2},{3,4},{5,6},{8,9},{10,11},{12,13},{14,15},{17,18},{19,20},{2... | collective-permute-start | bytes 294920 | tf_op jit(solution)/shard_map/while/body/eval_jaxpr/ppermute | solution.py:278
  333.0 7.7 %collective-permute-start.20 = (f32[32,768]{1,0:T(8,128)S(1)}, f32[32,768]{1,0:T(8,128)S(1)}, u32[]{:S(2)}, u32[]{:S(2)}) collective-permute-start(f32[32,768]{1,0:T(8,128)S(1)} %get-tuple-element.510), channel_id=1, source_target_pairs={{1,2},{3,4},{5,6},{8,9},{10,11},{12,13},{14,15},{17,18},{19,20},{2... | collective-permute-start | bytes 294920 | tf_op jit(solution)/shard_map/while/body/eval_jaxpr/ppermute | solution.py:278
  344.4 8.4 %collective-permute-start.27 = (f32[32,768]{1,0:T(8,128)S(1)}, f32[32,768]{1,0:T(8,128)S(1)}, u32[]{:S(2)}, u32[]{:S(2)}) collective-permute-start(f32[32,768]{1,0:T(8,128)S(1)} %get-tuple-element.517), channel_id=1, source_target_pairs={{1,2},{3,4},{5,6},{8,9},{10,11},{12,13},{14,15},{17,18},{19,20},{2... | collective-permute-start | bytes 294920 | tf_op jit(solution)/shard_map/while/body/eval_jaxpr/ppermute | solution.py:278
  356.5 9.1 %collective-permute-start.33 = (f32[32,768]{1,0:T(8,128)S(1)}, f32[32,768]{1,0:T(8,128)}, u32[]{:S(2)}, u32[]{:S(2)}) collective-permute-start(f32[32,768]{1,0:T(8,128)S(1)} %get-tuple-element.520), channel_id=1, source_target_pairs={{1,2},{3,4},{5,6},{8,9},{10,11},{12,13},{14,15},{17,18},{19,20},{2... | collective-permute-start | bytes 294920 | tf_op jit(solution)/shard_map/while/body/eval_jaxpr/ppermute | solution.py:278
  380.1 7.1 %collective-permute-start.1 = (f32[32,768]{1,0:T(8,128)S(1)}, f32[32,768]{1,0:T(8,128)S(1)}, u32[]{:S(2)}, u32[]{:S(2)}) collective-permute-start(f32[32,768]{1,0:T(8,128)S(1)} %east.19.east_ref), channel_id=1, source_target_pairs={{1,9},{3,11},{5,13},{7,15},{8,16},{10,18},{12,20},{14,22},{17,25},... | collective-permute-start | bytes 294920 | tf_op jit(solution)/shard_map/while/body/eval_jaxpr/ppermute | solution.py:274
  391.0 8.2 %collective-permute-start.3 = (f32[32,768]{1,0:T(8,128)S(1)}, f32[32,768]{1,0:T(8,128)S(1)}, u32[]{:S(2)}, u32[]{:S(2)}) collective-permute-start(f32[32,768]{1,0:T(8,128)S(1)} %get-tuple-element.493), channel_id=1, source_target_pairs={{1,2},{3,4},{5,6},{8,9},{10,11},{12,13},{14,15},{17,18},{19,20},{2... | collective-permute-start | bytes 294920 | tf_op jit(solution)/shard_map/while/body/eval_jaxpr/ppermute | solution.py:278
  402.9 9.6 %collective-permute-start.10 = (f32[32,768]{1,0:T(8,128)S(1)}, f32[32,768]{1,0:T(8,128)S(1)}, u32[]{:S(2)}, u32[]{:S(2)}) collective-permute-start(f32[32,768]{1,0:T(8,128)S(1)} %get-tuple-element.500), channel_id=1, source_target_pairs={{1,2},{3,4},{5,6},{8,9},{10,11},{12,13},{14,15},{17,18},{19,20},{2... | collective-permute-start | bytes 294920 | tf_op jit(solution)/shard_map/while/body/eval_jaxpr/ppermute | solution.py:278
  416.1 8.9 %collective-permute-start.8 = (f32[32,768]{1,0:T(8,128)S(1)}, f32[32,768]{1,0:T(8,128)S(1)}, u32[]{:S(2)}, u32[]{:S(2)}) collective-permute-start(f32[32,768]{1,0:T(8,128)S(1)} %get-tuple-element.498), channel_id=1, source_target_pairs={{1,2},{3,4},{5,6},{8,9},{10,11},{12,13},{14,15},{17,18},{19,20},{2... | collective-permute-start | bytes 294920 | tf_op jit(solution)/shard_map/while/body/eval_jaxpr/ppermute | solution.py:278
  428.6 8.6 %collective-permute-start.15 = (f32[32,768]{1,0:T(8,128)S(1)}, f32[32,768]{1,0:T(8,128)S(1)}, u32[]{:S(2)}, u32[]{:S(2)}) collective-permute-start(f32[32,768]{1,0:T(8,128)S(1)} %get-tuple-element.505), channel_id=1, source_target_pairs={{1,2},{3,4},{5,6},{8,9},{10,11},{12,13},{14,15},{17,18},{19,20},{2... | collective-permute-start | bytes 294920 | tf_op jit(solution)/shard_map/while/body/eval_jaxpr/ppermute | solution.py:278
  440.9 7.6 %collective-permute-start.22 = (f32[32,768]{1,0:T(8,128)S(1)}, f32[32,768]{1,0:T(8,128)S(1)}, u32[]{:S(2)}, u32[]{:S(2)}) collective-permute-start(f32[32,768]{1,0:T(8,128)S(1)} %get-tuple-element.512), channel_id=1, source_target_pairs={{1,2},{3,4},{5,6},{8,9},{10,11},{12,13},{14,15},{17,18},{19,20},{2... | collective-permute-start | bytes 294920 | tf_op jit(solution)/shard_map/while/body/eval_jaxpr/ppermute | solution.py:278
  452.1 8.5 %collective-permute-start.20 = (f32[32,768]{1,0:T(8,128)S(1)}, f32[32,768]{1,0:T(8,128)S(1)}, u32[]{:S(2)}, u32[]{:S(2)}) collective-permute-start(f32[32,768]{1,0:T(8,128)S(1)} %get-tuple-element.510), channel_id=1, source_target_pairs={{1,2},{3,4},{5,6},{8,9},{10,11},{12,13},{14,15},{17,18},{19,20},{2... | collective-permute-start | bytes 294920 | tf_op jit(solution)/shard_map/while/body/eval_jaxpr/ppermute | solution.py:278
  464.3 8.4 %collective-permute-start.27 = (f32[32,768]{1,0:T(8,128)S(1)}, f32[32,768]{1,0:T(8,128)S(1)}, u32[]{:S(2)}, u32[]{:S(2)}) collective-permute-start(f32[32,768]{1,0:T(8,128)S(1)} %get-tuple-element.517), channel_id=1, source_target_pairs={{1,2},{3,4},{5,6},{8,9},{10,11},{12,13},{14,15},{17,18},{19,20},{2... | collective-permute-start | bytes 294920 | tf_op jit(solution)/shard_map/while/body/eval_jaxpr/ppermute | solution.py:278
  476.4 9.1 %collective-permute-start.33 = (f32[32,768]{1,0:T(8,128)S(1)}, f32[32,768]{1,0:T(8,128)}, u32[]{:S(2)}, u32[]{:S(2)}) collective-permute-start(f32[32,768]{1,0:T(8,128)S(1)} %get-tuple-element.520), channel_id=1, source_target_pairs={{1,2},{3,4},{5,6},{8,9},{10,11},{12,13},{14,15},{17,18},{19,20},{2... | collective-permute-start | bytes 294920 | tf_op jit(solution)/shard_map/while/body/eval_jaxpr/ppermute | solution.py:278
  521.0 7.0 %collective-permute-start.42 = (f32[64,64]{0,1:T(8,128)S(1)}, f32[64,64]{0,1:T(8,128)S(1)}, u32[]{:S(2)}, u32[]{:S(2)}) collective-permute-start(f32[64,64]{0,1:T(8,128)S(1)} %add.61), channel_id=1, source_target_pairs={{0,64},{8,72},{16,80},{24,88},{32,96},{40,104},{48,112},{56,120},{... | collective-permute-start | bytes 49160 | tf_op jit(solution)/shard_map/ppermute | solution.py:203
  (602 shorter events, 287.9 us)
Async XLA Ops:
  31.1 11.9 %collective-permute-start.3 = (f32[32,768]{1,0:T(8,128)S(1)}, f32[32,768]{1,0:T(8,128)S(1)}, u32[]{:S(2)}, u32[]{:S(2)}) collective-permute-start(f32[32,768]{1,0:T(8,128)S(1)} %get-tuple-element.493), channel_id=1, source_target_pairs={{1,2},{3,4},{5,6},{8,9},{10,11},{12,13},{14,15},{17,18},{19,20},{2... | collective-permute-start | bytes 294920 | tf_op jit(solution)/shard_map/while/body/eval_jaxpr/ppermute | solution.py:278
  112.3 16.8 %collective-permute-start.33 = (f32[32,768]{1,0:T(8,128)S(1)}, f32[32,768]{1,0:T(8,128)}, u32[]{:S(2)}, u32[]{:S(2)}) collective-permute-start(f32[32,768]{1,0:T(8,128)S(1)} %get-tuple-element.520), channel_id=1, source_target_pairs={{1,2},{3,4},{5,6},{8,9},{10,11},{12,13},{14,15},{17,18},{19,20},{2... | collective-permute-start | bytes 294920 | tf_op jit(solution)/shard_map/while/body/eval_jaxpr/ppermute | solution.py:278
  147.4 11.6 %collective-permute-start.3 = (f32[32,768]{1,0:T(8,128)S(1)}, f32[32,768]{1,0:T(8,128)S(1)}, u32[]{:S(2)}, u32[]{:S(2)}) collective-permute-start(f32[32,768]{1,0:T(8,128)S(1)} %get-tuple-element.493), channel_id=1, source_target_pairs={{1,2},{3,4},{5,6},{8,9},{10,11},{12,13},{14,15},{17,18},{19,20},{2... | collective-permute-start | bytes 294920 | tf_op jit(solution)/shard_map/while/body/eval_jaxpr/ppermute | solution.py:278
  180.5 11.6 %collective-permute-start.16 = (f32[32,768]{1,0:T(8,128)S(1)}, f32[32,768]{1,0:T(8,128)S(1)}, u32[]{:S(2)}, u32[]{:S(2)}) collective-permute-start(f32[32,768]{1,0:T(8,128)S(1)} %get-tuple-element.506), channel_id=1, source_target_pairs={{0,1},{2,3},{4,5},{6,7},{9,10},{11,12},{13,14},{16,17},{18,19},{20... | collective-permute-start | bytes 294920 | tf_op jit(solution)/shard_map/while/body/eval_jaxpr/ppermute | solution.py:278
  182.8 12.0 %collective-permute-start.15 = (f32[32,768]{1,0:T(8,128)S(1)}, f32[32,768]{1,0:T(8,128)S(1)}, u32[]{:S(2)}, u32[]{:S(2)}) collective-permute-start(f32[32,768]{1,0:T(8,128)S(1)} %get-tuple-element.505), channel_id=1, source_target_pairs={{1,2},{3,4},{5,6},{8,9},{10,11},{12,13},{14,15},{17,18},{19,20},{2... | collective-permute-start | bytes 294920 | tf_op jit(solution)/shard_map/while/body/eval_jaxpr/ppermute | solution.py:278
  205.3 11.8 %collective-permute-start.21 = (f32[32,768]{1,0:T(8,128)S(1)}, f32[32,768]{1,0:T(8,128)S(1)}, u32[]{:S(2)}, u32[]{:S(2)}) collective-permute-start(f32[32,768]{1,0:T(8,128)S(1)} %get-tuple-element.511), channel_id=1, source_target_pairs={{0,1},{2,3},{4,5},{6,7},{9,10},{11,12},{13,14},{16,17},{18,19},{20... | collective-permute-start | bytes 294920 | tf_op jit(solution)/shard_map/while/body/eval_jaxpr/ppermute | solution.py:278
  207.5 12.2 %collective-permute-start.20 = (f32[32,768]{1,0:T(8,128)S(1)}, f32[32,768]{1,0:T(8,128)S(1)}, u32[]{:S(2)}, u32[]{:S(2)}) collective-permute-start(f32[32,768]{1,0:T(8,128)S(1)} %get-tuple-element.510), channel_id=1, source_target_pairs={{1,2},{3,4},{5,6},{8,9},{10,11},{12,13},{14,15},{17,18},{19,20},{2... | collective-permute-start | bytes 294920 | tf_op jit(solution)/shard_map/while/body/eval_jaxpr/ppermute | solution.py:278
  230.4 11.8 %collective-permute-start.26 = (f32[32,768]{1,0:T(8,128)S(1)}, f32[32,768]{1,0:T(8,128)S(1)}, u32[]{:S(2)}, u32[]{:S(2)}) collective-permute-start(f32[32,768]{1,0:T(8,128)S(1)} %get-tuple-element.516), channel_id=1, source_target_pairs={{0,1},{2,3},{4,5},{6,7},{9,10},{11,12},{13,14},{16,17},{18,19},{20... | collective-permute-start | bytes 294920 | tf_op jit(solution)/shard_map/while/body/eval_jaxpr/ppermute | solution.py:278
  232.0 11.5 %collective-permute-start.31 = (f32[32,768]{1,0:T(8,128)S(1)}, f32[32,768]{1,0:T(8,128)S(1)}, u32[]{:S(2)}, u32[]{:S(2)}) collective-permute-start(f32[32,768]{1,0:T(8,128)S(1)} %east.34.east_ref), channel_id=1, source_target_pairs={{0,8},{2,10},{4,12},{6,14},{9,17},{11,19},{13,21},{15,23},{16,24},... | collective-permute-start | bytes 294920 | tf_op jit(solution)/shard_map/while/body/eval_jaxpr/ppermute | solution.py:274
  232.7 19.7 %collective-permute-start.33 = (f32[32,768]{1,0:T(8,128)S(1)}, f32[32,768]{1,0:T(8,128)}, u32[]{:S(2)}, u32[]{:S(2)}) collective-permute-start(f32[32,768]{1,0:T(8,128)S(1)} %get-tuple-element.520), channel_id=1, source_target_pairs={{1,2},{3,4},{5,6},{8,9},{10,11},{12,13},{14,15},{17,18},{19,20},{2... | collective-permute-start | bytes 294920 | tf_op jit(solution)/shard_map/while/body/eval_jaxpr/ppermute | solution.py:278
  267.8 11.4 %collective-permute-start.4 = (f32[32,768]{1,0:T(8,128)S(1)}, f32[32,768]{1,0:T(8,128)S(1)}, u32[]{:S(2)}, u32[]{:S(2)}) collective-permute-start(f32[32,768]{1,0:T(8,128)S(1)} %get-tuple-element.494), channel_id=1, source_target_pairs={{0,1},{2,3},{4,5},{6,7},{9,10},{11,12},{13,14},{16,17},{18,19},{20... | collective-permute-start | bytes 294920 | tf_op jit(solution)/shard_map/while/body/eval_jaxpr/ppermute | solution.py:278
  270.7 11.2 %collective-permute-start.3 = (f32[32,768]{1,0:T(8,128)S(1)}, f32[32,768]{1,0:T(8,128)S(1)}, u32[]{:S(2)}, u32[]{:S(2)}) collective-permute-start(f32[32,768]{1,0:T(8,128)S(1)} %get-tuple-element.493), channel_id=1, source_target_pairs={{1,2},{3,4},{5,6},{8,9},{10,11},{12,13},{14,15},{17,18},{19,20},{2... | collective-permute-start | bytes 294920 | tf_op jit(solution)/shard_map/while/body/eval_jaxpr/ppermute | solution.py:278
  280.6 11.2 %collective-permute-start.2 = (f32[32,768]{1,0:T(8,128)S(1)}, f32[32,768]{1,0:T(8,128)S(1)}, u32[]{:S(2)}, u32[]{:S(2)}) collective-permute-start(f32[32,768]{1,0:T(8,128)S(1)} %get-tuple-element.492), channel_id=1, source_target_pairs={{0,1},{2,3},{4,5},{6,7},{9,10},{11,12},{13,14},{16,17},{18,19},{20... | collective-permute-start | bytes 294920 | tf_op jit(solution)/shard_map/while/body/eval_jaxpr/ppermute | solution.py:278
  282.9 11.6 %collective-permute-start.10 = (f32[32,768]{1,0:T(8,128)S(1)}, f32[32,768]{1,0:T(8,128)S(1)}, u32[]{:S(2)}, u32[]{:S(2)}) collective-permute-start(f32[32,768]{1,0:T(8,128)S(1)} %get-tuple-element.500), channel_id=1, source_target_pairs={{1,2},{3,4},{5,6},{8,9},{10,11},{12,13},{14,15},{17,18},{19,20},{2... | collective-permute-start | bytes 294920 | tf_op jit(solution)/shard_map/while/body/eval_jaxpr/ppermute | solution.py:278
  293.2 13.8 %collective-permute-start.9 = (f32[32,768]{1,0:T(8,128)S(1)}, f32[32,768]{1,0:T(8,128)S(1)}, u32[]{:S(2)}, u32[]{:S(2)}) collective-permute-start(f32[32,768]{1,0:T(8,128)S(1)} %get-tuple-element.499), channel_id=1, source_target_pairs={{0,1},{2,3},{4,5},{6,7},{9,10},{11,12},{13,14},{16,17},{18,19},{20... | collective-permute-start | bytes 294920 | tf_op jit(solution)/shard_map/while/body/eval_jaxpr/ppermute | solution.py:278
  294.8 12.2 %collective-permute-start.12 = (f32[32,768]{1,0:T(8,128)S(1)}, f32[32,768]{1,0:T(8,128)S(1)}, u32[]{:S(2)}, u32[]{:S(2)}) collective-permute-start(f32[32,768]{1,0:T(8,128)S(1)} %east.24.east_ref), channel_id=1, source_target_pairs={{0,8},{2,10},{4,12},{6,14},{9,17},{11,19},{13,21},{15,23},{16,24},... | collective-permute-start | bytes 294920 | tf_op jit(solution)/shard_map/while/body/eval_jaxpr/ppermute | solution.py:274
  295.5 14.2 %collective-permute-start.8 = (f32[32,768]{1,0:T(8,128)S(1)}, f32[32,768]{1,0:T(8,128)S(1)}, u32[]{:S(2)}, u32[]{:S(2)}) collective-permute-start(f32[32,768]{1,0:T(8,128)S(1)} %get-tuple-element.498), channel_id=1, source_target_pairs={{1,2},{3,4},{5,6},{8,9},{10,11},{12,13},{14,15},{17,18},{19,20},{2... | collective-permute-start | bytes 294920 | tf_op jit(solution)/shard_map/while/body/eval_jaxpr/ppermute | solution.py:278
  344.4 11.1 %collective-permute-start.27 = (f32[32,768]{1,0:T(8,128)S(1)}, f32[32,768]{1,0:T(8,128)S(1)}, u32[]{:S(2)}, u32[]{:S(2)}) collective-permute-start(f32[32,768]{1,0:T(8,128)S(1)} %get-tuple-element.517), channel_id=1, source_target_pairs={{1,2},{3,4},{5,6},{8,9},{10,11},{12,13},{14,15},{17,18},{19,20},{2... | collective-permute-start | bytes 294920 | tf_op jit(solution)/shard_map/while/body/eval_jaxpr/ppermute | solution.py:278
  354.3 11.3 %collective-permute-start.26 = (f32[32,768]{1,0:T(8,128)S(1)}, f32[32,768]{1,0:T(8,128)S(1)}, u32[]{:S(2)}, u32[]{:S(2)}) collective-permute-start(f32[32,768]{1,0:T(8,128)S(1)} %get-tuple-element.516), channel_id=1, source_target_pairs={{0,1},{2,3},{4,5},{6,7},{9,10},{11,12},{13,14},{16,17},{18,19},{20... | collective-permute-start | bytes 294920 | tf_op jit(solution)/shard_map/while/body/eval_jaxpr/ppermute | solution.py:278
  355.8 11.0 %collective-permute-start.31 = (f32[32,768]{1,0:T(8,128)S(1)}, f32[32,768]{1,0:T(8,128)S(1)}, u32[]{:S(2)}, u32[]{:S(2)}) collective-permute-start(f32[32,768]{1,0:T(8,128)S(1)} %east.34.east_ref), channel_id=1, source_target_pairs={{0,8},{2,10},{4,12},{6,14},{9,17},{11,19},{13,21},{15,23},{16,24},... | collective-permute-start | bytes 294920 | tf_op jit(solution)/shard_map/while/body/eval_jaxpr/ppermute | solution.py:274
  356.5 16.7 %collective-permute-start.33 = (f32[32,768]{1,0:T(8,128)S(1)}, f32[32,768]{1,0:T(8,128)}, u32[]{:S(2)}, u32[]{:S(2)}) collective-permute-start(f32[32,768]{1,0:T(8,128)S(1)} %get-tuple-element.520), channel_id=1, source_target_pairs={{1,2},{3,4},{5,6},{8,9},{10,11},{12,13},{14,15},{17,18},{19,20},{2... | collective-permute-start | bytes 294920 | tf_op jit(solution)/shard_map/while/body/eval_jaxpr/ppermute | solution.py:278
  388.1 11.1 %collective-permute-start.4 = (f32[32,768]{1,0:T(8,128)S(1)}, f32[32,768]{1,0:T(8,128)S(1)}, u32[]{:S(2)}, u32[]{:S(2)}) collective-permute-start(f32[32,768]{1,0:T(8,128)S(1)} %get-tuple-element.494), channel_id=1, source_target_pairs={{0,1},{2,3},{4,5},{6,7},{9,10},{11,12},{13,14},{16,17},{18,19},{20... | collective-permute-start | bytes 294920 | tf_op jit(solution)/shard_map/while/body/eval_jaxpr/ppermute | solution.py:278
  400.6 11.8 %collective-permute-start.2 = (f32[32,768]{1,0:T(8,128)S(1)}, f32[32,768]{1,0:T(8,128)S(1)}, u32[]{:S(2)}, u32[]{:S(2)}) collective-permute-start(f32[32,768]{1,0:T(8,128)S(1)} %get-tuple-element.492), channel_id=1, source_target_pairs={{0,1},{2,3},{4,5},{6,7},{9,10},{11,12},{13,14},{16,17},{18,19},{20... | collective-permute-start | bytes 294920 | tf_op jit(solution)/shard_map/while/body/eval_jaxpr/ppermute | solution.py:278
  402.9 12.3 %collective-permute-start.10 = (f32[32,768]{1,0:T(8,128)S(1)}, f32[32,768]{1,0:T(8,128)S(1)}, u32[]{:S(2)}, u32[]{:S(2)}) collective-permute-start(f32[32,768]{1,0:T(8,128)S(1)} %get-tuple-element.500), channel_id=1, source_target_pairs={{1,2},{3,4},{5,6},{8,9},{10,11},{12,13},{14,15},{17,18},{19,20},{2... | collective-permute-start | bytes 294920 | tf_op jit(solution)/shard_map/while/body/eval_jaxpr/ppermute | solution.py:278
  413.8 11.2 %collective-permute-start.9 = (f32[32,768]{1,0:T(8,128)S(1)}, f32[32,768]{1,0:T(8,128)S(1)}, u32[]{:S(2)}, u32[]{:S(2)}) collective-permute-start(f32[32,768]{1,0:T(8,128)S(1)} %get-tuple-element.499), channel_id=1, source_target_pairs={{0,1},{2,3},{4,5},{6,7},{9,10},{11,12},{13,14},{16,17},{18,19},{20... | collective-permute-start | bytes 294920 | tf_op jit(solution)/shard_map/while/body/eval_jaxpr/ppermute | solution.py:278
  416.1 11.6 %collective-permute-start.8 = (f32[32,768]{1,0:T(8,128)S(1)}, f32[32,768]{1,0:T(8,128)S(1)}, u32[]{:S(2)}, u32[]{:S(2)}) collective-permute-start(f32[32,768]{1,0:T(8,128)S(1)} %get-tuple-element.498), channel_id=1, source_target_pairs={{1,2},{3,4},{5,6},{8,9},{10,11},{12,13},{14,15},{17,18},{19,20},{2... | collective-permute-start | bytes 294920 | tf_op jit(solution)/shard_map/while/body/eval_jaxpr/ppermute | solution.py:278
  428.6 11.3 %collective-permute-start.15 = (f32[32,768]{1,0:T(8,128)S(1)}, f32[32,768]{1,0:T(8,128)S(1)}, u32[]{:S(2)}, u32[]{:S(2)}) collective-permute-start(f32[32,768]{1,0:T(8,128)S(1)} %get-tuple-element.505), channel_id=1, source_target_pairs={{1,2},{3,4},{5,6},{8,9},{10,11},{12,13},{14,15},{17,18},{19,20},{2... | collective-permute-start | bytes 294920 | tf_op jit(solution)/shard_map/while/body/eval_jaxpr/ppermute | solution.py:278
  452.1 11.2 %collective-permute-start.20 = (f32[32,768]{1,0:T(8,128)S(1)}, f32[32,768]{1,0:T(8,128)S(1)}, u32[]{:S(2)}, u32[]{:S(2)}) collective-permute-start(f32[32,768]{1,0:T(8,128)S(1)} %get-tuple-element.510), channel_id=1, source_target_pairs={{1,2},{3,4},{5,6},{8,9},{10,11},{12,13},{14,15},{17,18},{19,20},{2... | collective-permute-start | bytes 294920 | tf_op jit(solution)/shard_map/while/body/eval_jaxpr/ppermute | solution.py:278
  464.3 11.1 %collective-permute-start.27 = (f32[32,768]{1,0:T(8,128)S(1)}, f32[32,768]{1,0:T(8,128)S(1)}, u32[]{:S(2)}, u32[]{:S(2)}) collective-permute-start(f32[32,768]{1,0:T(8,128)S(1)} %get-tuple-element.517), channel_id=1, source_target_pairs={{1,2},{3,4},{5,6},{8,9},{10,11},{12,13},{14,15},{17,18},{19,20},{2... | collective-permute-start | bytes 294920 | tf_op jit(solution)/shard_map/while/body/eval_jaxpr/ppermute | solution.py:278
  474.1 11.3 %collective-permute-start.26 = (f32[32,768]{1,0:T(8,128)S(1)}, f32[32,768]{1,0:T(8,128)S(1)}, u32[]{:S(2)}, u32[]{:S(2)}) collective-permute-start(f32[32,768]{1,0:T(8,128)S(1)} %get-tuple-element.516), channel_id=1, source_target_pairs={{0,1},{2,3},{4,5},{6,7},{9,10},{11,12},{13,14},{16,17},{18,19},{20... | collective-permute-start | bytes 294920 | tf_op jit(solution)/shard_map/while/body/eval_jaxpr/ppermute | solution.py:278
  475.7 11.0 %collective-permute-start.31 = (f32[32,768]{1,0:T(8,128)S(1)}, f32[32,768]{1,0:T(8,128)S(1)}, u32[]{:S(2)}, u32[]{:S(2)}) collective-permute-start(f32[32,768]{1,0:T(8,128)S(1)} %east.34.east_ref), channel_id=1, source_target_pairs={{0,8},{2,10},{4,12},{6,14},{9,17},{11,19},{13,21},{15,23},{16,24},... | collective-permute-start | bytes 294920 | tf_op jit(solution)/shard_map/while/body/eval_jaxpr/ppermute | solution.py:274
  476.4 14.5 %collective-permute-start.33 = (f32[32,768]{1,0:T(8,128)S(1)}, f32[32,768]{1,0:T(8,128)}, u32[]{:S(2)}, u32[]{:S(2)}) collective-permute-start(f32[32,768]{1,0:T(8,128)S(1)} %get-tuple-element.520), channel_id=1, source_target_pairs={{1,2},{3,4},{5,6},{8,9},{10,11},{12,13},{14,15},{17,18},{19,20},{2... | collective-permute-start | bytes 294920 | tf_op jit(solution)/shard_map/while/body/eval_jaxpr/ppermute | solution.py:278
  (161 other events, 1064.3 us)

commit v4 on v3

--- a/solution.py
+++ b/solution.py
@@ -8,7 +8,7 @@
 from jax.sharding import PartitionSpec as P
 
 PIECES = 2
-UNROLL = 9
+UNROLL = 8
 LIMIT = 8
 VMEM = pl.BlockSpec(memory_space=pltpu.VMEM)
 SMEM = pl.BlockSpec(memory_space=pltpu.SMEM)
@@ -131,8 +131,8 @@
         out_ref[...] = partial_ref[:, :half] + product(west_ref[...], high_ref, low_ref)
 
 
-def north_kernel(offset, count, age_ref, partial_ref, west_ref, high_ref, low_ref, east_ref, *refs):
-    out_ref, results_ref = refs[-2:]
+def north_kernel(offset, count, age_ref, partial_ref, west_ref, high_ref, low_ref, east_ref, kept_ref, out_ref, results_ref):
+    del kept_ref
     active, piece = when_active(offset, count, age_ref)
     half = west_ref.shape[1]
 
@@ -239,16 +239,15 @@
     nx, ny = shape
     return [
         (x * ny + y, (x + dx) * ny + y + dy)
-        for x in range(nx - dx)
+        for x in range(parity, nx - dx, 2)
         for y in range(ny - dy)
-        if (x + y) % 2 == parity
     ]
 
 
 def body(shape, operators, sources, source_rows, batch_plan):
     nx, ny = shape
     axes = ("gx", "gy")
-    depth = lax.axis_index("gx") + 3 * lax.axis_index("gy")
+    depth = lax.axis_index("gx") + 2 * lax.axis_index("gy")
     order = operators.shape[-1]
     half = order // 2
     _, _, batches, columns, placed_count = sources.shape
@@ -258,33 +257,40 @@
     placed = placed.reshape(count, width, order)
     quarters = split_operator(operators[0, 0])
 
-    steps = (nx - 1 + 3 * (ny - 1) + 2 * (count - 1)) // 2 + 1
-    trips = -(-steps // UNROLL)
+    halves_needed = nx - 1 + 2 * (ny - 1) + 2 * (count - 1) + 1
+    trips = -(-halves_needed // (2 * UNROLL))
 
     def advance(trip, carry):
         west, south, results, fixed = carry
         fixed = pass_through(*fixed)
         placed, quarters = fixed[0], fixed[1:]
-        age = (trip * (2 * UNROLL) - depth)[None].astype(jnp.int32)
-        south = list(south)
+        west, south = list(west), list(south)
+        age = trip * (2 * UNROLL) - depth
+        age_ref = age[None].astype(jnp.int32)
         for offset in range(2 * UNROLL):
             parity = offset % 2
-            partial = south_part(offset, count, age, placed, south[0], quarters[4:])
-            to_east = east_part(offset, count, age, partial, west, quarters[:2])
+            partial = south_part(
+                offset, count, age_ref, placed, south[parity], quarters[4:]
+            )
+            to_east = east_part(
+                offset, count, age_ref, partial, west[parity], quarters[:2]
+            )
             arrived = lax.ppermute(to_east, axes, sweep_pairs(shape, parity, 1, 0))
             to_north, results = north_part(
-                offset, count, age, partial, west, quarters[2:4], to_east, results
+                offset, count, age_ref, partial, west[parity], quarters[2:4], to_east, results
             )
-            risen = lax.ppermute(to_north, axes, sweep_pairs(shape, parity, 0, 1))
-            west, south = arrived, south[1:] + [risen]
-        return (west, tuple(south), results, tuple(fixed))
+            west[1 - parity] = arrived
+            south[parity] = lax.ppermute(
+                to_north, axes, sweep_pairs(shape, parity, 0, 1)
+            )
+        return (tuple(west), tuple(south), results, tuple(fixed))
 
     zero = jnp.zeros((width, half), F32)
-    (results,) = unwritten((count, width, order))
-    carry = (zero, (zero, zero, zero), results, (placed, *quarters))
-    results = lax.fori_loop(0, trips, advance, carry)[2]
-    first = results[:PIECES].reshape(columns, order)
-    rest = results[PIECES:]
+    results, odd_west = unwritten((count, width, order), zero.shape)
+    carry = ((zero, odd_west), (zero, zero), results, (placed, *quarters))
+    ready = -(-(nx - 1 + 2 * (ny - 1) + 2 * (PIECES - 1) + 1) // (2 * UNROLL))
+    carry = lax.fori_loop(0, ready, advance, carry)
+    first = carry[2][:PIECES].reshape(columns, order)
     partial_gram = lax.dot_general(
         first,
         first,
@@ -293,6 +299,10 @@
         preferred_element_type=F32,
     )
     gram = summed(partial_gram, shape) / (nx * ny * order)
+    for trip in range(ready, trips):
+        carry = advance(trip, carry)
+    gram, first, results = lax.optimization_barrier((gram, first, carry[2]))
+    rest = results[PIECES:]
     lower = jnp.linalg.cholesky(gram)
     basis = jax.scipy.linalg.solve_triangular(lower, first, lower=True)
     traces = rest.reshape(batches - 1, columns, order)

time: 558 us -> 479 us (0.86); the launches traced: 548 us -> 476 us
  starting transfers between devices: 441 us -> 389 us
  Pallas kernels: 52.5 us -> 42.2 us
  waiting for transfers between devices: 25 us -> 15.1 us
    ppermute x72 -> x62, starting transfers between devices: 318 us -> 102 us  [advance(): lax.ppermute(to_north, axes, sweep_pairs(shape, parity, 0, 1))]
    ppermute x72 -> x63, starting transfers between devices: 96.5 us -> 267 us  [advance(): arrived = lax.ppermute(to_east, axes, sweep_pairs(shape, parity, 1, 0))]
    ppermute x72 -> x63, waiting for transfers between devices: 11.4 us -> 1.56 us  [advance(): arrived = lax.ppermute(to_east, axes, sweep_pairs(shape, parity, 1, 0))]
    pallas_call x72 -> x64, Pallas kernels: 27.1 us -> 23.2 us  [south_part(): pl.pallas_call(functools.partial(south_kernel, offset, count), out_shape=...]
  transfers between devices with their start and end apart: 152 -> 133, of which waited for: 39 -> 30; matrix products, arithmetic and copies ran while one was open for 0% -> 0% of each run, Pallas kernels for 6% -> 5%
where the time goes in v4:
time: 479 us; the launch traced here: 476 us
  starting transfers between devices  389 us (81%)
  Pallas kernels  42.2 us (9%)
  waiting for transfers between devices  15.1 us (3%)
  other arithmetic  12.1 us (3%)
  local copies, waits for them, and re-layouts  11.5 us (2%)
    ppermute x63, starting transfers between devices, advance(): arrived = lax.ppermute(to_east, axes, sweep_pairs(shape, parity, 1, 0))  267 us
    ppermute x62, starting transfers between devices, advance(): lax.ppermute(to_north, axes, sweep_pairs(shape, parity, 0, 1))  102 us
    pallas_call x64, Pallas kernels, south_part(): pl.pallas_call(functools.partial(south_kernel, offset, count), out_shape=...  23.2 us
    ppermute x8, starting transfers between devices, summed(): value = value + lax.ppermute(value, axis, pairs)  20.2 us
  transfers between devices with their start and end apart: 133, of which 30 were waited for; matrix products, arithmetic and copies ran while one was open for 0% of the time, Pallas kernels for 5%

profile of v4, /device:TPU:1, one launch (start us, length us, event | category | flops | bytes accessed | tf_op | source)
XLA Modules:
  0.0 476.2 jit_solution(12283820711048754127)
XLA Ops:
  12.2 311.7 %while.37 = (s32[]{:T(128)}, f32[32,768]{1,0:T(8,128)S(1)}, f32[32,768]{1,0:T(8,128)}, f32[32,768]{1,0:T(8,128)}, f32[10,32,1536]{2,1,0:T(8,128)}, /*index=5*/f3...) while((s32[]{:T(128)}, f32[32,768]{1,0:T(8,128)S(1)}, ...), condition=%wide.region_1.0_spmd, body=%wide.region_0.0_spmd.sunk | while | flops 7247757312 | bytes 111675048 | solution.py:292
  27.8 6.7 %collective-permute-start.4 = (f32[32,768]{1,0:T(8,128)S(1)}, f32[32,768]{1,0:T(8,128)S(1)}, u32[]{:S(2)}, u32[]{:S(2)}) collective-permute-start(f32[32,768]{1,0:T(8,128)S(1)} %east.50.east_ref), channel_id=1, source_target_pairs={{0,8},{1,9},{2,10},{3,11},{4,12},{5,13},{6,14},{7,15},{16,24},{17,... | collective-permute-start | bytes 294920 | tf_op jit(solution)/shard_map/while/body/eval_jaxpr/ppermute | solution.py:278
  41.0 7.3 %collective-permute-start.8 = (f32[32,768]{1,0:T(8,128)S(1)}, f32[32,768]{1,0:T(8,128)S(1)}, u32[]{:S(2)}, u32[]{:S(2)}) collective-permute-start(f32[32,768]{1,0:T(8,128)S(1)} %east.52.east_ref), channel_id=1, source_target_pairs={{0,8},{1,9},{2,10},{3,11},{4,12},{5,13},{6,14},{7,15},{16,24},{17,... | collective-permute-start | bytes 294920 | tf_op jit(solution)/shard_map/while/body/eval_jaxpr/ppermute | solution.py:278
  54.9 6.2 %collective-permute-start.12 = (f32[32,768]{1,0:T(8,128)S(1)}, f32[32,768]{1,0:T(8,128)S(1)}, u32[]{:S(2)}, u32[]{:S(2)}) collective-permute-start(f32[32,768]{1,0:T(8,128)S(1)} %east.54.east_ref), channel_id=1, source_target_pairs={{0,8},{1,9},{2,10},{3,11},{4,12},{5,13},{6,14},{7,15},{16,24},{17,... | collective-permute-start | bytes 294920 | tf_op jit(solution)/shard_map/while/body/eval_jaxpr/ppermute | solution.py:278
  78.4 5.9 %collective-permute-start.20 = (f32[32,768]{1,0:T(8,128)S(1)}, f32[32,768]{1,0:T(8,128)S(1)}, u32[]{:S(2)}, u32[]{:S(2)}) collective-permute-start(f32[32,768]{1,0:T(8,128)S(1)} %east.58.east_ref), channel_id=1, source_target_pairs={{0,8},{1,9},{2,10},{3,11},{4,12},{5,13},{6,14},{7,15},{16,24},{17,... | collective-permute-start | bytes 294920 | tf_op jit(solution)/shard_map/while/body/eval_jaxpr/ppermute | solution.py:278
  90.0 6.3 %collective-permute-start.24 = (f32[32,768]{1,0:T(8,128)S(1)}, f32[32,768]{1,0:T(8,128)S(1)}, u32[]{:S(2)}, u32[]{:S(2)}) collective-permute-start(f32[32,768]{1,0:T(8,128)S(1)} %east.60.east_ref), channel_id=1, source_target_pairs={{0,8},{1,9},{2,10},{3,11},{4,12},{5,13},{6,14},{7,15},{16,24},{17,... | collective-permute-start | bytes 294920 | tf_op jit(solution)/shard_map/while/body/eval_jaxpr/ppermute | solution.py:278
  102.0 6.3 %collective-permute-start.28 = (f32[32,768]{1,0:T(8,128)S(1)}, f32[32,768]{1,0:T(8,128)S(1)}, u32[]{:S(2)}, u32[]{:S(2)}) collective-permute-start(f32[32,768]{1,0:T(8,128)S(1)} %east.62.east_ref), channel_id=1, source_target_pairs={{0,8},{1,9},{2,10},{3,11},{4,12},{5,13},{6,14},{7,15},{16,24},{17,... | collective-permute-start | bytes 294920 | tf_op jit(solution)/shard_map/while/body/eval_jaxpr/ppermute | solution.py:278
  117.1 6.8 %collective-permute-start = (f32[32,768]{1,0:T(8,128)S(1)}, f32[32,768]{1,0:T(8,128)S(1)}, u32[]{:S(2)}, u32[]{:S(2)}) collective-permute-start(f32[32,768]{1,0:T(8,128)S(1)} %east.48.east_ref), channel_id=1, source_target_pairs={{0,8},{1,9},{2,10},{3,11},{4,12},{5,13},{6,14},{7,15},{16,24},{17,... | collective-permute-start | bytes 294920 | tf_op jit(solution)/shard_map/while/body/eval_jaxpr/ppermute | solution.py:278
  131.8 6.4 %collective-permute-start.4 = (f32[32,768]{1,0:T(8,128)S(1)}, f32[32,768]{1,0:T(8,128)S(1)}, u32[]{:S(2)}, u32[]{:S(2)}) collective-permute-start(f32[32,768]{1,0:T(8,128)S(1)} %east.50.east_ref), channel_id=1, source_target_pairs={{0,8},{1,9},{2,10},{3,11},{4,12},{5,13},{6,14},{7,15},{16,24},{17,... | collective-permute-start | bytes 294920 | tf_op jit(solution)/shard_map/while/body/eval_jaxpr/ppermute | solution.py:278
  144.0 6.5 %collective-permute-start.8 = (f32[32,768]{1,0:T(8,128)S(1)}, f32[32,768]{1,0:T(8,128)S(1)}, u32[]{:S(2)}, u32[]{:S(2)}) collective-permute-start(f32[32,768]{1,0:T(8,128)S(1)} %east.52.east_ref), channel_id=1, source_target_pairs={{0,8},{1,9},{2,10},{3,11},{4,12},{5,13},{6,14},{7,15},{16,24},{17,... | collective-permute-start | bytes 294920 | tf_op jit(solution)/shard_map/while/body/eval_jaxpr/ppermute | solution.py:278
  154.8 8.0 %collective-permute-start.12 = (f32[32,768]{1,0:T(8,128)S(1)}, f32[32,768]{1,0:T(8,128)S(1)}, u32[]{:S(2)}, u32[]{:S(2)}) collective-permute-start(f32[32,768]{1,0:T(8,128)S(1)} %east.54.east_ref), channel_id=1, source_target_pairs={{0,8},{1,9},{2,10},{3,11},{4,12},{5,13},{6,14},{7,15},{16,24},{17,... | collective-permute-start | bytes 294920 | tf_op jit(solution)/shard_map/while/body/eval_jaxpr/ppermute | solution.py:278
  167.2 9.3 %collective-permute-start.16 = (f32[32,768]{1,0:T(8,128)S(1)}, f32[32,768]{1,0:T(8,128)S(1)}, u32[]{:S(2)}, u32[]{:S(2)}) collective-permute-start(f32[32,768]{1,0:T(8,128)S(1)} %east.56.east_ref), channel_id=1, source_target_pairs={{0,8},{1,9},{2,10},{3,11},{4,12},{5,13},{6,14},{7,15},{16,24},{17,... | collective-permute-start | bytes 294920 | tf_op jit(solution)/shard_map/while/body/eval_jaxpr/ppermute | solution.py:278
  180.3 8.6 %collective-permute-start.20 = (f32[32,768]{1,0:T(8,128)S(1)}, f32[32,768]{1,0:T(8,128)S(1)}, u32[]{:S(2)}, u32[]{:S(2)}) collective-permute-start(f32[32,768]{1,0:T(8,128)S(1)} %east.58.east_ref), channel_id=1, source_target_pairs={{0,8},{1,9},{2,10},{3,11},{4,12},{5,13},{6,14},{7,15},{16,24},{17,... | collective-permute-start | bytes 294920 | tf_op jit(solution)/shard_map/while/body/eval_jaxpr/ppermute | solution.py:278
  192.9 8.6 %collective-permute-start.24 = (f32[32,768]{1,0:T(8,128)S(1)}, f32[32,768]{1,0:T(8,128)S(1)}, u32[]{:S(2)}, u32[]{:S(2)}) collective-permute-start(f32[32,768]{1,0:T(8,128)S(1)} %east.60.east_ref), channel_id=1, source_target_pairs={{0,8},{1,9},{2,10},{3,11},{4,12},{5,13},{6,14},{7,15},{16,24},{17,... | collective-permute-start | bytes 294920 | tf_op jit(solution)/shard_map/while/body/eval_jaxpr/ppermute | solution.py:278
  205.5 8.6 %collective-permute-start.28 = (f32[32,768]{1,0:T(8,128)S(1)}, f32[32,768]{1,0:T(8,128)S(1)}, u32[]{:S(2)}, u32[]{:S(2)}) collective-permute-start(f32[32,768]{1,0:T(8,128)S(1)} %east.62.east_ref), channel_id=1, source_target_pairs={{0,8},{1,9},{2,10},{3,11},{4,12},{5,13},{6,14},{7,15},{16,24},{17,... | collective-permute-start | bytes 294920 | tf_op jit(solution)/shard_map/while/body/eval_jaxpr/ppermute | solution.py:278
  221.7 8.6 %collective-permute-start = (f32[32,768]{1,0:T(8,128)S(1)}, f32[32,768]{1,0:T(8,128)S(1)}, u32[]{:S(2)}, u32[]{:S(2)}) collective-permute-start(f32[32,768]{1,0:T(8,128)S(1)} %east.48.east_ref), channel_id=1, source_target_pairs={{0,8},{1,9},{2,10},{3,11},{4,12},{5,13},{6,14},{7,15},{16,24},{17,... | collective-permute-start | bytes 294920 | tf_op jit(solution)/shard_map/while/body/eval_jaxpr/ppermute | solution.py:278
  236.2 8.6 %collective-permute-start.4 = (f32[32,768]{1,0:T(8,128)S(1)}, f32[32,768]{1,0:T(8,128)S(1)}, u32[]{:S(2)}, u32[]{:S(2)}) collective-permute-start(f32[32,768]{1,0:T(8,128)S(1)} %east.50.east_ref), channel_id=1, source_target_pairs={{0,8},{1,9},{2,10},{3,11},{4,12},{5,13},{6,14},{7,15},{16,24},{17,... | collective-permute-start | bytes 294920 | tf_op jit(solution)/shard_map/while/body/eval_jaxpr/ppermute | solution.py:278
  248.8 8.6 %collective-permute-start.8 = (f32[32,768]{1,0:T(8,128)S(1)}, f32[32,768]{1,0:T(8,128)S(1)}, u32[]{:S(2)}, u32[]{:S(2)}) collective-permute-start(f32[32,768]{1,0:T(8,128)S(1)} %east.52.east_ref), channel_id=1, source_target_pairs={{0,8},{1,9},{2,10},{3,11},{4,12},{5,13},{6,14},{7,15},{16,24},{17,... | collective-permute-start | bytes 294920 | tf_op jit(solution)/shard_map/while/body/eval_jaxpr/ppermute | solution.py:278
  261.4 8.6 %collective-permute-start.12 = (f32[32,768]{1,0:T(8,128)S(1)}, f32[32,768]{1,0:T(8,128)S(1)}, u32[]{:S(2)}, u32[]{:S(2)}) collective-permute-start(f32[32,768]{1,0:T(8,128)S(1)} %east.54.east_ref), channel_id=1, source_target_pairs={{0,8},{1,9},{2,10},{3,11},{4,12},{5,13},{6,14},{7,15},{16,24},{17,... | collective-permute-start | bytes 294920 | tf_op jit(solution)/shard_map/while/body/eval_jaxpr/ppermute | solution.py:278
  274.0 8.2 %collective-permute-start.16 = (f32[32,768]{1,0:T(8,128)S(1)}, f32[32,768]{1,0:T(8,128)S(1)}, u32[]{:S(2)}, u32[]{:S(2)}) collective-permute-start(f32[32,768]{1,0:T(8,128)S(1)} %east.56.east_ref), channel_id=1, source_target_pairs={{0,8},{1,9},{2,10},{3,11},{4,12},{5,13},{6,14},{7,15},{16,24},{17,... | collective-permute-start | bytes 294920 | tf_op jit(solution)/shard_map/while/body/eval_jaxpr/ppermute | solution.py:278
  286.3 8.5 %collective-permute-start.20 = (f32[32,768]{1,0:T(8,128)S(1)}, f32[32,768]{1,0:T(8,128)S(1)}, u32[]{:S(2)}, u32[]{:S(2)}) collective-permute-start(f32[32,768]{1,0:T(8,128)S(1)} %east.58.east_ref), channel_id=1, source_target_pairs={{0,8},{1,9},{2,10},{3,11},{4,12},{5,13},{6,14},{7,15},{16,24},{17,... | collective-permute-start | bytes 294920 | tf_op jit(solution)/shard_map/while/body/eval_jaxpr/ppermute | solution.py:278
  298.8 8.1 %collective-permute-start.24 = (f32[32,768]{1,0:T(8,128)S(1)}, f32[32,768]{1,0:T(8,128)S(1)}, u32[]{:S(2)}, u32[]{:S(2)}) collective-permute-start(f32[32,768]{1,0:T(8,128)S(1)} %east.60.east_ref), channel_id=1, source_target_pairs={{0,8},{1,9},{2,10},{3,11},{4,12},{5,13},{6,14},{7,15},{16,24},{17,... | collective-permute-start | bytes 294920 | tf_op jit(solution)/shard_map/while/body/eval_jaxpr/ppermute | solution.py:278
  311.0 8.1 %collective-permute-start.28 = (f32[32,768]{1,0:T(8,128)S(1)}, f32[32,768]{1,0:T(8,128)S(1)}, u32[]{:S(2)}, u32[]{:S(2)}) collective-permute-start(f32[32,768]{1,0:T(8,128)S(1)} %east.62.east_ref), channel_id=1, source_target_pairs={{0,8},{1,9},{2,10},{3,11},{4,12},{5,13},{6,14},{7,15},{16,24},{17,... | collective-permute-start | bytes 294920 | tf_op jit(solution)/shard_map/while/body/eval_jaxpr/ppermute | solution.py:278
  327.0 8.3 %collective-permute-start.40 = (f32[32,768]{1,0:T(8,128)S(1)}, f32[32,768]{1,0:T(8,128)S(1)}, u32[]{:S(2)}, u32[]{:S(2)}) collective-permute-start(f32[32,768]{1,0:T(8,128)S(1)} %east.32.east_ref), channel_id=1, source_target_pairs={{0,8},{1,9},{2,10},{3,11},{4,12},{5,13},{6,14},{7,15},{16,24},{17,... | collective-permute-start | bytes 294920 | tf_op jit(solution)/shard_map/ppermute | solution.py:278
  341.3 8.2 %collective-permute-start.44 = (f32[32,768]{1,0:T(8,128)S(1)}, f32[32,768]{1,0:T(8,128)S(1)}, u32[]{:S(2)}, u32[]{:S(2)}) collective-permute-start(f32[32,768]{1,0:T(8,128)S(1)} %east.34.east_ref), channel_id=1, source_target_pairs={{0,8},{1,9},{2,10},{3,11},{4,12},{5,13},{6,14},{7,15},{16,24},{17,... | collective-permute-start | bytes 294920 | tf_op jit(solution)/shard_map/ppermute | solution.py:278
  353.5 8.1 %collective-permute-start.48 = (f32[32,768]{1,0:T(8,128)S(1)}, f32[32,768]{1,0:T(8,128)S(1)}, u32[]{:S(2)}, u32[]{:S(2)}) collective-permute-start(f32[32,768]{1,0:T(8,128)S(1)} %east.36.east_ref), channel_id=1, source_target_pairs={{0,8},{1,9},{2,10},{3,11},{4,12},{5,13},{6,14},{7,15},{16,24},{17,... | collective-permute-start | bytes 294920 | tf_op jit(solution)/shard_map/ppermute | solution.py:278
  365.6 8.1 %collective-permute-start.52 = (f32[32,768]{1,0:T(8,128)S(1)}, f32[32,768]{1,0:T(8,128)S(1)}, u32[]{:S(2)}, u32[]{:S(2)}) collective-permute-start(f32[32,768]{1,0:T(8,128)S(1)} %east.38.east_ref), channel_id=1, source_target_pairs={{0,8},{1,9},{2,10},{3,11},{4,12},{5,13},{6,14},{7,15},{16,24},{17,... | collective-permute-start | bytes 294920 | tf_op jit(solution)/shard_map/ppermute | solution.py:278
  377.7 8.2 %collective-permute-start.56 = (f32[32,768]{1,0:T(8,128)S(1)}, f32[32,768]{1,0:T(8,128)S(1)}, u32[]{:S(2)}, u32[]{:S(2)}) collective-permute-start(f32[32,768]{1,0:T(8,128)S(1)} %east.40.east_ref), channel_id=1, source_target_pairs={{0,8},{1,9},{2,10},{3,11},{4,12},{5,13},{6,14},{7,15},{16,24},{17,... | collective-permute-start | bytes 294920 | tf_op jit(solution)/shard_map/ppermute | solution.py:278
  389.9 8.0 %collective-permute-start.60 = (f32[32,768]{1,0:T(8,128)S(1)}, f32[32,768]{1,0:T(8,128)S(1)}, u32[]{:S(2)}, u32[]{:S(2)}) collective-permute-start(f32[32,768]{1,0:T(8,128)S(1)} %east.42.east_ref), channel_id=1, source_target_pairs={{0,8},{1,9},{2,10},{3,11},{4,12},{5,13},{6,14},{7,15},{16,24},{17,... | collective-permute-start | bytes 294920 | tf_op jit(solution)/shard_map/ppermute | solution.py:278
  402.0 8.1 %collective-permute-start.64 = (f32[32,768]{1,0:T(8,128)S(1)}, f32[32,768]{1,0:T(8,128)S(1)}, u32[]{:S(2)}, u32[]{:S(2)}) collective-permute-start(f32[32,768]{1,0:T(8,128)S(1)} %east.44.east_ref), channel_id=1, source_target_pairs={{0,8},{1,9},{2,10},{3,11},{4,12},{5,13},{6,14},{7,15},{16,24},{17,... | collective-permute-start | bytes 294920 | tf_op jit(solution)/shard_map/ppermute | solution.py:278
  429.4 5.9 %collective-permute-start.37 = (f32[64,64]{0,1:T(8,128)S(1)}, f32[64,64]{0,1:T(8,128)S(1)}, u32[]{:S(2)}, u32[]{:S(2)}) collective-permute-start(f32[64,64]{0,1:T(8,128)S(1)} %add.60), channel_id=1, source_target_pairs={{0,32},{8,40},{16,48},{24,56},{32,0},{40,8},{48,16},{56,24},{64,96... | collective-permute-start | bytes 49160 | tf_op jit(solution)/shard_map/ppermute | solution.py:203
  444.8 10.2 %collective-permute-start.68 = (f32[32,768]{1,0:T(8,128)S(1)}, f32[32,768]{1,0:T(8,128)S(1)}, u32[]{:S(2)}, u32[]{:S(2)}) collective-permute-start(f32[32,768]{1,0:T(8,128)S(1)} %east.46.east_ref), channel_id=1, source_target_pairs={{0,8},{1,9},{2,10},{3,11},{4,12},{5,13},{6,14},{7,15},{16,24},{17,... | collective-permute-start | bytes 294920 | tf_op jit(solution)/shard_map/ppermute | solution.py:278
  (541 shorter events, 230.1 us)
Async XLA Ops:
  25.7 12.2 %collective-permute-start.1 = (f32[32,768]{1,0:T(8,128)S(1)}, f32[32,768]{1,0:T(8,128)S(1)}, u32[]{:S(2)}, u32[]{:S(2)}) collective-permute-start(f32[32,768]{1,0:T(8,128)S(1)} %get-tuple-element.573), channel_id=1, source_target_pairs={{8,9},{9,10},{10,11},{11,12},{12,13},{13,14},{14,15},{24,25},{25,2... | collective-permute-start | bytes 294920 | tf_op jit(solution)/shard_map/while/body/eval_jaxpr/ppermute | solution.py:283
  38.7 13.2 %collective-permute-start.5 = (f32[32,768]{1,0:T(8,128)S(1)}, f32[32,768]{1,0:T(8,128)S(1)}, u32[]{:S(2)}, u32[]{:S(2)}) collective-permute-start(f32[32,768]{1,0:T(8,128)S(1)} %get-tuple-element.577), channel_id=1, source_target_pairs={{8,9},{9,10},{10,11},{11,12},{12,13},{13,14},{14,15},{24,25},{25,2... | collective-permute-start | bytes 294920 | tf_op jit(solution)/shard_map/while/body/eval_jaxpr/ppermute | solution.py:283
  99.8 11.3 %collective-permute-start.25 = (f32[32,768]{1,0:T(8,128)S(1)}, f32[32,768]{1,0:T(8,128)S(1)}, u32[]{:S(2)}, u32[]{:S(2)}) collective-permute-start(f32[32,768]{1,0:T(8,128)S(1)} %get-tuple-element.597), channel_id=1, source_target_pairs={{8,9},{9,10},{10,11},{11,12},{12,13},{13,14},{14,15},{24,25},{25,2... | collective-permute-start | bytes 294920 | tf_op jit(solution)/shard_map/while/body/eval_jaxpr/ppermute | solution.py:283
  117.1 11.9 %collective-permute-start = (f32[32,768]{1,0:T(8,128)S(1)}, f32[32,768]{1,0:T(8,128)S(1)}, u32[]{:S(2)}, u32[]{:S(2)}) collective-permute-start(f32[32,768]{1,0:T(8,128)S(1)} %east.48.east_ref), channel_id=1, source_target_pairs={{0,8},{1,9},{2,10},{3,11},{4,12},{5,13},{6,14},{7,15},{16,24},{17,... | collective-permute-start | bytes 294920 | tf_op jit(solution)/shard_map/while/body/eval_jaxpr/ppermute | solution.py:278
  129.7 11.3 %collective-permute-start.1 = (f32[32,768]{1,0:T(8,128)S(1)}, f32[32,768]{1,0:T(8,128)S(1)}, u32[]{:S(2)}, u32[]{:S(2)}) collective-permute-start(f32[32,768]{1,0:T(8,128)S(1)} %get-tuple-element.573), channel_id=1, source_target_pairs={{8,9},{9,10},{10,11},{11,12},{12,13},{13,14},{14,15},{24,25},{25,2... | collective-permute-start | bytes 294920 | tf_op jit(solution)/shard_map/while/body/eval_jaxpr/ppermute | solution.py:283
  141.8 11.4 %collective-permute-start.5 = (f32[32,768]{1,0:T(8,128)S(1)}, f32[32,768]{1,0:T(8,128)S(1)}, u32[]{:S(2)}, u32[]{:S(2)}) collective-permute-start(f32[32,768]{1,0:T(8,128)S(1)} %get-tuple-element.577), channel_id=1, source_target_pairs={{8,9},{9,10},{10,11},{11,12},{12,13},{13,14},{14,15},{24,25},{25,2... | collective-permute-start | bytes 294920 | tf_op jit(solution)/shard_map/while/body/eval_jaxpr/ppermute | solution.py:283
  153.9 11.6 %collective-permute-start.9 = (f32[32,768]{1,0:T(8,128)S(1)}, f32[32,768]{1,0:T(8,128)S(1)}, u32[]{:S(2)}, u32[]{:S(2)}) collective-permute-start(f32[32,768]{1,0:T(8,128)S(1)} %get-tuple-element.581), channel_id=1, source_target_pairs={{8,9},{9,10},{10,11},{11,12},{12,13},{13,14},{14,15},{24,25},{25,2... | collective-permute-start | bytes 294920 | tf_op jit(solution)/shard_map/while/body/eval_jaxpr/ppermute | solution.py:283
  166.3 12.4 %collective-permute-start.13 = (f32[32,768]{1,0:T(8,128)S(1)}, f32[32,768]{1,0:T(8,128)S(1)}, u32[]{:S(2)}, u32[]{:S(2)}) collective-permute-start(f32[32,768]{1,0:T(8,128)S(1)} %get-tuple-element.585), channel_id=1, source_target_pairs={{8,9},{9,10},{10,11},{11,12},{12,13},{13,14},{14,15},{24,25},{25,2... | collective-permute-start | bytes 294920 | tf_op jit(solution)/shard_map/while/body/eval_jaxpr/ppermute | solution.py:283
  167.2 11.5 %collective-permute-start.16 = (f32[32,768]{1,0:T(8,128)S(1)}, f32[32,768]{1,0:T(8,128)S(1)}, u32[]{:S(2)}, u32[]{:S(2)}) collective-permute-start(f32[32,768]{1,0:T(8,128)S(1)} %east.56.east_ref), channel_id=1, source_target_pairs={{0,8},{1,9},{2,10},{3,11},{4,12},{5,13},{6,14},{7,15},{16,24},{17,... | collective-permute-start | bytes 294920 | tf_op jit(solution)/shard_map/while/body/eval_jaxpr/ppermute | solution.py:278
  179.5 11.8 %collective-permute-start.17 = (f32[32,768]{1,0:T(8,128)S(1)}, f32[32,768]{1,0:T(8,128)S(1)}, u32[]{:S(2)}, u32[]{:S(2)}) collective-permute-start(f32[32,768]{1,0:T(8,128)S(1)} %get-tuple-element.589), channel_id=1, source_target_pairs={{8,9},{9,10},{10,11},{11,12},{12,13},{13,14},{14,15},{24,25},{25,2... | collective-permute-start | bytes 294920 | tf_op jit(solution)/shard_map/while/body/eval_jaxpr/ppermute | solution.py:283
  192.0 11.8 %collective-permute-start.21 = (f32[32,768]{1,0:T(8,128)S(1)}, f32[32,768]{1,0:T(8,128)S(1)}, u32[]{:S(2)}, u32[]{:S(2)}) collective-permute-start(f32[32,768]{1,0:T(8,128)S(1)} %get-tuple-element.593), channel_id=1, source_target_pairs={{8,9},{9,10},{10,11},{11,12},{12,13},{13,14},{14,15},{24,25},{25,2... | collective-permute-start | bytes 294920 | tf_op jit(solution)/shard_map/while/body/eval_jaxpr/ppermute | solution.py:283
  204.6 11.8 %collective-permute-start.25 = (f32[32,768]{1,0:T(8,128)S(1)}, f32[32,768]{1,0:T(8,128)S(1)}, u32[]{:S(2)}, u32[]{:S(2)}) collective-permute-start(f32[32,768]{1,0:T(8,128)S(1)} %get-tuple-element.597), channel_id=1, source_target_pairs={{8,9},{9,10},{10,11},{11,12},{12,13},{13,14},{14,15},{24,25},{25,2... | collective-permute-start | bytes 294920 | tf_op jit(solution)/shard_map/while/body/eval_jaxpr/ppermute | solution.py:283
  221.7 13.1 %collective-permute-start = (f32[32,768]{1,0:T(8,128)S(1)}, f32[32,768]{1,0:T(8,128)S(1)}, u32[]{:S(2)}, u32[]{:S(2)}) collective-permute-start(f32[32,768]{1,0:T(8,128)S(1)} %east.48.east_ref), channel_id=1, source_target_pairs={{0,8},{1,9},{2,10},{3,11},{4,12},{5,13},{6,14},{7,15},{16,24},{17,... | collective-permute-start | bytes 294920 | tf_op jit(solution)/shard_map/while/body/eval_jaxpr/ppermute | solution.py:278
  235.5 11.7 %collective-permute-start.1 = (f32[32,768]{1,0:T(8,128)S(1)}, f32[32,768]{1,0:T(8,128)S(1)}, u32[]{:S(2)}, u32[]{:S(2)}) collective-permute-start(f32[32,768]{1,0:T(8,128)S(1)} %get-tuple-element.573), channel_id=1, source_target_pairs={{8,9},{9,10},{10,11},{11,12},{12,13},{13,14},{14,15},{24,25},{25,2... | collective-permute-start | bytes 294920 | tf_op jit(solution)/shard_map/while/body/eval_jaxpr/ppermute | solution.py:283
  248.0 11.8 %collective-permute-start.5 = (f32[32,768]{1,0:T(8,128)S(1)}, f32[32,768]{1,0:T(8,128)S(1)}, u32[]{:S(2)}, u32[]{:S(2)}) collective-permute-start(f32[32,768]{1,0:T(8,128)S(1)} %get-tuple-element.577), channel_id=1, source_target_pairs={{8,9},{9,10},{10,11},{11,12},{12,13},{13,14},{14,15},{24,25},{25,2... | collective-permute-start | bytes 294920 | tf_op jit(solution)/shard_map/while/body/eval_jaxpr/ppermute | solution.py:283
  260.6 11.9 %collective-permute-start.9 = (f32[32,768]{1,0:T(8,128)S(1)}, f32[32,768]{1,0:T(8,128)S(1)}, u32[]{:S(2)}, u32[]{:S(2)}) collective-permute-start(f32[32,768]{1,0:T(8,128)S(1)} %get-tuple-element.581), channel_id=1, source_target_pairs={{8,9},{9,10},{10,11},{11,12},{12,13},{13,14},{14,15},{24,25},{25,2... | collective-permute-start | bytes 294920 | tf_op jit(solution)/shard_map/while/body/eval_jaxpr/ppermute | solution.py:283
  273.2 11.5 %collective-permute-start.13 = (f32[32,768]{1,0:T(8,128)S(1)}, f32[32,768]{1,0:T(8,128)S(1)}, u32[]{:S(2)}, u32[]{:S(2)}) collective-permute-start(f32[32,768]{1,0:T(8,128)S(1)} %get-tuple-element.585), channel_id=1, source_target_pairs={{8,9},{9,10},{10,11},{11,12},{12,13},{13,14},{14,15},{24,25},{25,2... | collective-permute-start | bytes 294920 | tf_op jit(solution)/shard_map/while/body/eval_jaxpr/ppermute | solution.py:283
  285.5 11.7 %collective-permute-start.17 = (f32[32,768]{1,0:T(8,128)S(1)}, f32[32,768]{1,0:T(8,128)S(1)}, u32[]{:S(2)}, u32[]{:S(2)}) collective-permute-start(f32[32,768]{1,0:T(8,128)S(1)} %get-tuple-element.589), channel_id=1, source_target_pairs={{8,9},{9,10},{10,11},{11,12},{12,13},{13,14},{14,15},{24,25},{25,2... | collective-permute-start | bytes 294920 | tf_op jit(solution)/shard_map/while/body/eval_jaxpr/ppermute | solution.py:283
  297.9 11.4 %collective-permute-start.21 = (f32[32,768]{1,0:T(8,128)S(1)}, f32[32,768]{1,0:T(8,128)S(1)}, u32[]{:S(2)}, u32[]{:S(2)}) collective-permute-start(f32[32,768]{1,0:T(8,128)S(1)} %get-tuple-element.593), channel_id=1, source_target_pairs={{8,9},{9,10},{10,11},{11,12},{12,13},{13,14},{14,15},{24,25},{25,2... | collective-permute-start | bytes 294920 | tf_op jit(solution)/shard_map/while/body/eval_jaxpr/ppermute | solution.py:283
  310.1 11.3 %collective-permute-start.25 = (f32[32,768]{1,0:T(8,128)S(1)}, f32[32,768]{1,0:T(8,128)S(1)}, u32[]{:S(2)}, u32[]{:S(2)}) collective-permute-start(f32[32,768]{1,0:T(8,128)S(1)} %get-tuple-element.597), channel_id=1, source_target_pairs={{8,9},{9,10},{10,11},{11,12},{12,13},{13,14},{14,15},{24,25},{25,2... | collective-permute-start | bytes 294920 | tf_op jit(solution)/shard_map/while/body/eval_jaxpr/ppermute | solution.py:283
  327.0 12.8 %collective-permute-start.40 = (f32[32,768]{1,0:T(8,128)S(1)}, f32[32,768]{1,0:T(8,128)S(1)}, u32[]{:S(2)}, u32[]{:S(2)}) collective-permute-start(f32[32,768]{1,0:T(8,128)S(1)} %east.32.east_ref), channel_id=1, source_target_pairs={{0,8},{1,9},{2,10},{3,11},{4,12},{5,13},{6,14},{7,15},{16,24},{17,... | collective-permute-start | bytes 294920 | tf_op jit(solution)/shard_map/ppermute | solution.py:278
  340.5 11.3 %collective-permute-start.41 = (f32[32,768]{1,0:T(8,128)S(1)}, f32[32,768]{1,0:T(8,128)S(1)}, u32[]{:S(2)}, u32[]{:S(2)}) collective-permute-start(f32[32,768]{1,0:T(8,128)S(1)} %get-tuple-element.364), channel_id=1, source_target_pairs={{8,9},{9,10},{10,11},{11,12},{12,13},{13,14},{14,15},{24,25},{25,2... | collective-permute-start | bytes 294920 | tf_op jit(solution)/shard_map/ppermute | solution.py:283
  352.6 11.3 %collective-permute-start.45 = (f32[32,768]{1,0:T(8,128)S(1)}, f32[32,768]{1,0:T(8,128)S(1)}, u32[]{:S(2)}, u32[]{:S(2)}) collective-permute-start(f32[32,768]{1,0:T(8,128)S(1)} %get-tuple-element.368), channel_id=1, source_target_pairs={{8,9},{9,10},{10,11},{11,12},{12,13},{13,14},{14,15},{24,25},{25,2... | collective-permute-start | bytes 294920 | tf_op jit(solution)/shard_map/ppermute | solution.py:283
  364.7 11.3 %collective-permute-start.49 = (f32[32,768]{1,0:T(8,128)S(1)}, f32[32,768]{1,0:T(8,128)S(1)}, u32[]{:S(2)}, u32[]{:S(2)}) collective-permute-start(f32[32,768]{1,0:T(8,128)S(1)} %get-tuple-element.372), channel_id=1, source_target_pairs={{8,9},{9,10},{10,11},{11,12},{12,13},{13,14},{14,15},{24,25},{25,2... | collective-permute-start | bytes 294920 | tf_op jit(solution)/shard_map/ppermute | solution.py:283
  376.8 11.4 %collective-permute-start.53 = (f32[32,768]{1,0:T(8,128)S(1)}, f32[32,768]{1,0:T(8,128)S(1)}, u32[]{:S(2)}, u32[]{:S(2)}) collective-permute-start(f32[32,768]{1,0:T(8,128)S(1)} %get-tuple-element.376), channel_id=1, source_target_pairs={{8,9},{9,10},{10,11},{11,12},{12,13},{13,14},{14,15},{24,25},{25,2... | collective-permute-start | bytes 294920 | tf_op jit(solution)/shard_map/ppermute | solution.py:283
  401.1 17.2 %collective-permute-start.61 = (f32[32,768]{1,0:T(8,128)S(1)}, f32[32,768]{1,0:T(8,128)S(1)}, u32[]{:S(2)}, u32[]{:S(2)}) collective-permute-start(f32[32,768]{1,0:T(8,128)S(1)} %get-tuple-element.384), channel_id=1, source_target_pairs={{8,9},{9,10},{10,11},{11,12},{12,13},{13,14},{14,15},{24,25},{25,2... | collective-permute-start | bytes 294920 | tf_op jit(solution)/shard_map/ppermute | solution.py:283
  402.0 16.3 %collective-permute-start.64 = (f32[32,768]{1,0:T(8,128)S(1)}, f32[32,768]{1,0:T(8,128)S(1)}, u32[]{:S(2)}, u32[]{:S(2)}) collective-permute-start(f32[32,768]{1,0:T(8,128)S(1)} %east.44.east_ref), channel_id=1, source_target_pairs={{0,8},{1,9},{2,10},{3,11},{4,12},{5,13},{6,14},{7,15},{16,24},{17,... | collective-permute-start | bytes 294920 | tf_op jit(solution)/shard_map/ppermute | solution.py:278
  415.2 29.5 %collective-permute-start.66 = (f32[32,768]{1,0:T(8,128)S(1)}, f32[32,768]{1,0:T(8,128)S(1)}, u32[]{:S(2)}, u32[]{:S(2)}) collective-permute-start(f32[32,768]{1,0:T(8,128)S(1)} %get-tuple-element.389), channel_id=1, source_target_pairs={{0,1},{1,2},{2,3},{3,4},{4,5},{5,6},{6,7},{16,17},{17,18},{18,19},... | collective-permute-start | bytes 294920 | tf_op jit(solution)/shard_map/ppermute | solution.py:283
  418.3 26.4 %collective-permute-start.67 = (f32[32,768]{1,0:T(8,128)S(1)}, f32[32,768]{1,0:T(8,128)S(1)}, u32[]{:S(2)}, u32[]{:S(2)}) collective-permute-start(f32[32,768]{1,0:T(8,128)S(1)} %east.45.east_ref), channel_id=1, source_target_pairs={{8,16},{9,17},{10,18},{11,19},{12,20},{13,21},{14,22},{15,23},{24,... | collective-permute-start | bytes 294920 | tf_op jit(solution)/shard_map/ppermute | solution.py:278
  441.2 13.8 %collective-permute-start.39 = (f32[64,64]{0,1:T(8,128)S(1)}, f32[64,64]{0,1:T(8,128)S(1)}, u32[]{:S(2)}, u32[]{:S(2)}) collective-permute-start(f32[64,64]{0,1:T(8,128)S(1)} %add.62), channel_id=1, source_target_pairs={{0,128},{8,136},{16,144},{24,152},{32,160},{40,168},{48,176},{56,1... | collective-permute-start | bytes 49160 | tf_op jit(solution)/shard_map/ppermute | solution.py:203
  444.0 11.6 %collective-permute-start.65 = (f32[32,768]{1,0:T(8,128)S(1)}, f32[32,768]{1,0:T(8,128)S(1)}, u32[]{:S(2)}, u32[]{:S(2)}) collective-permute-start(f32[32,768]{1,0:T(8,128)S(1)} %get-tuple-element.388), channel_id=1, source_target_pairs={{8,9},{9,10},{10,11},{11,12},{12,13},{13,14},{14,15},{24,25},{25,2... | collective-permute-start | bytes 294920 | tf_op jit(solution)/shard_map/ppermute | solution.py:283
  444.8 12.3 %collective-permute-start.68 = (f32[32,768]{1,0:T(8,128)S(1)}, f32[32,768]{1,0:T(8,128)S(1)}, u32[]{:S(2)}, u32[]{:S(2)}) collective-permute-start(f32[32,768]{1,0:T(8,128)S(1)} %east.46.east_ref), channel_id=1, source_target_pairs={{0,8},{1,9},{2,10},{3,11},{4,12},{5,13},{6,14},{7,15},{16,24},{17,... | collective-permute-start | bytes 294920 | tf_op jit(solution)/shard_map/ppermute | solution.py:278
  (143 other events, 793.6 us)
